TPU v7x, 32 devices: a whole 2x2x4 slice. The times are simulated.
32 devices in a mesh: img: 8 (over z, y), seq: 4 (over x, core).
Axes of the slice: x: 2, y: 2, z: 4, core: 2. Of those that a mesh axis runs over, the one named last changes fastest.
Arguments:
- tokens: bfloat16 [8192, 1152], P(('img', 'seq')), may hold values from -6 to 6
- conditioning: float32 [32, 1152], P('img'), may hold values from -6 to 6
- slot_ids: int32 [8192], P('img'), may hold values from 0 to 3, as said below
- dino_target: bfloat16 [8192, 768], P(('img', 'seq')), may hold values from -6 to 6
- out_cotangent: bfloat16 [8192, 1152], P(('img', 'seq')), may hold values from -6 to 6
- ada_weight: bfloat16 [1152, 6912], P('img', 'seq'), may hold values from -0.1875 to 0.1875
- qkv_weight: bfloat16 [1152, 3456], P('img', 'seq'), may hold values from -0.1875 to 0.1875
- attn_weight: bfloat16 [1152, 1152], P('img', 'seq'), may hold values from -0.75 to 0.75
- up_weight: bfloat16 [1152, 4608], P('img', 'seq'), may hold values from -0.1875 to 0.1875
- down_weight: bfloat16 [4608, 1152], P('img', 'seq'), may hold values from -0.09375 to 0.09375
- first_proj: bfloat16 [1152, 2048], P('img', 'seq'), may hold values from -0.1875 to 0.1875
- second_proj: bfloat16 [2048, 2048], P('img', 'seq'), may hold values from -0.125 to 0.125
- third_proj: bfloat16 [2048, 768], P('img', 'seq'), may hold values from -0.125 to 0.125
- ada_bias: float32 [6912], replicated, may hold values from -2 to 2
- query_bias: float32 [1152], replicated, may hold values from -2 to 2
- value_bias: float32 [1152], replicated, may hold values from -2 to 2
- attn_bias: float32 [1152], replicated, may hold values from -2 to 2
- up_bias: float32 [4608], replicated, may hold values from -2 to 2
- down_bias: float32 [1152], replicated, may hold values from -2 to 2
- first_bias: float32 [2048], replicated, may hold values from -2 to 2
- second_bias: float32 [2048], replicated, may hold values from -2 to 2
- third_bias: float32 [768], replicated, may hold values from -2 to 2
Outputs:
- block_output: bfloat16 [8192, 1152], P(('img', 'seq'))
- tokens_grad: float32 [8192, 1152], P(('img', 'seq'))
- conditioning_grad: float32 [32, 1152], P('img')
- ada_weight_grad: float32 [1152, 6912], P('img', 'seq')
- qkv_weight_grad: float32 [1152, 3456], P('img', 'seq')
- attn_weight_grad: float32 [1152, 1152], P('img', 'seq')
- up_weight_grad: float32 [1152, 4608], P('img', 'seq')
- down_weight_grad: float32 [4608, 1152], P('img', 'seq')
- first_proj_grad: float32 [1152, 2048], P('img', 'seq')
- second_proj_grad: float32 [2048, 2048], P('img', 'seq')
- third_proj_grad: float32 [2048, 768], P('img', 'seq')
- ada_bias_grad: float32 [6912], replicated
- query_bias_grad: float32 [1152], replicated
- value_bias_grad: float32 [1152], replicated
- attn_bias_grad: float32 [1152], replicated
- up_bias_grad: float32 [4608], replicated
- down_bias_grad: float32 [1152], replicated
- first_bias_grad: float32 [2048], replicated
- second_bias_grad: float32 [2048], replicated
- third_bias_grad: float32 [768], replicated
Inputs may be any that keep to these rules, and one draw needn't show every extreme that they name: `slot_ids`: within each group of 1024 consecutive tokens the values start at 0 and never fall; each value covers 256 or 1024 consecutive tokens beginning at a multiple of 256 from the group's start.
All inputs are finite; a program needn't handle non-finite values.
Results may differ from a plain program's by a relative error of at most 0.019.
Values may be sent and summed in bfloat16 or wider, within the bound.
No kernel may reach another device: no remote copies, remote signals or barrier semaphores. Data moves between devices by JAX's collectives and lax.ppermute only.
A program may use at most 320 MiB of HBM per device.

v0:
```python
from functools import partial
import math

import jax
import jax.numpy as jnp
from jax import lax
from jax.sharding import PartitionSpec as P

H = 16
HD = 72


EPS_NORM = 1e-06
EPS_COS = 1e-06
LAMBDA_ALIGN = 0.5
MASKED_SCORE = -1e30
HIGHEST_PREC = lax.Precision.HIGHEST


def product(left, right):
    return jnp.dot(left, right, preferred_element_type=jnp.float32)


def product_tn(left, right):
    return lax.dot_general(
        left, right, (((0,), (0,)), ((), ())), preferred_element_type=jnp.float32
    )


def product_nt(left, right):
    return lax.dot_general(
        left, right, (((1,), (1,)), ((), ())), preferred_element_type=jnp.float32
    )


def column_sums(values):
    return jnp.sum(values.astype(jnp.float32), axis=0)


def layer_norm(values):
    centered = values - jnp.mean(values, axis=-1, keepdims=True)
    return centered * lax.rsqrt(jnp.mean(centered * centered, axis=-1, keepdims=True) + EPS_NORM)


def cosine_total(aligned, target):
    cosine = (
        jnp.sum(aligned * target, axis=1)
        * lax.rsqrt(jnp.sum(aligned * aligned, axis=1) + EPS_COS)
        * lax.rsqrt(jnp.sum(target * target, axis=1) + EPS_COS)
    )
    return -LAMBDA_ALIGN * jnp.sum(cosine)


def masked_scores(queries_block, key_rows, slot_block, group_slots, score_scale):
    scores = (
        jnp.einsum("qhd,khd->hqk", queries_block, key_rows, preferred_element_type=jnp.float32)
        * score_scale
    )
    same_image = slot_block[:, None] == group_slots[None, :]
    return jnp.where(same_image[None], scores, MASKED_SCORE)


def attend_forward(queries, key_rows, value_rows, group_slots):
    group_rows, head_count, head_width = queries.shape
    block_rows = math.gcd(512, group_rows)
    score_scale = head_width ** (-0.5)

    def one_block(block_index):
        first_row = block_index * block_rows
        queries_block = lax.dynamic_slice_in_dim(queries, first_row, block_rows, 0)
        slot_block = lax.dynamic_slice_in_dim(group_slots, first_row, block_rows, 0)
        scores = masked_scores(queries_block, key_rows, slot_block, group_slots, score_scale)
        row_peak = jnp.max(scores, axis=2, keepdims=True)
        raised = jnp.exp(scores - row_peak)
        row_total = jnp.sum(raised, axis=2, keepdims=True)
        weights = (raised / row_total).astype(jnp.bfloat16)
        outcome = jnp.einsum(
            "hqk,khd->qhd", weights, value_rows, preferred_element_type=jnp.float32
        )
        return (outcome.astype(jnp.bfloat16), (row_peak + jnp.log(row_total))[:, :, 0])

    outcomes, log_totals = lax.map(one_block, jnp.arange(group_rows // block_rows, dtype=jnp.int32))
    attended = outcomes.reshape(group_rows, head_count, head_width)
    log_total = log_totals.transpose(1, 0, 2).reshape(head_count, group_rows)
    return (attended, log_total)


def attend_backward(queries, key_rows, value_rows, group_slots, log_total, grad_heads):
    group_rows, head_count, head_width = queries.shape
    block_rows = math.gcd(512, group_rows)
    score_scale = head_width ** (-0.5)

    def one_block(carry, block_index):
        key_grads, value_grads = carry
        first_row = block_index * block_rows
        queries_block = lax.dynamic_slice_in_dim(queries, first_row, block_rows, 0)
        slot_block = lax.dynamic_slice_in_dim(group_slots, first_row, block_rows, 0)
        grad_block = lax.dynamic_slice_in_dim(grad_heads, first_row, block_rows, 0)
        total_block = lax.dynamic_slice_in_dim(log_total, first_row, block_rows, 1)
        scores = masked_scores(queries_block, key_rows, slot_block, group_slots, score_scale)
        weights = jnp.exp(scores - total_block[:, :, None])
        grad_weights = jnp.einsum(
            "qhd,khd->hqk", grad_block, value_rows, preferred_element_type=jnp.float32
        )
        row_delta = jnp.sum(weights * grad_weights, axis=2, keepdims=True)
        grad_scores = (weights * (grad_weights - row_delta)).astype(jnp.bfloat16)
        grad_queries = (
            jnp.einsum("hqk,khd->qhd", grad_scores, key_rows, preferred_element_type=jnp.float32)
            * score_scale
        )
        key_grads = (
            key_grads
            + jnp.einsum(
                "hqk,qhd->khd", grad_scores, queries_block, preferred_element_type=jnp.float32
            )
            * score_scale
        )
        value_grads = value_grads + jnp.einsum(
            "hqk,qhd->khd",
            weights.astype(jnp.bfloat16),
            grad_block,
            preferred_element_type=jnp.float32,
        )
        return ((key_grads, value_grads), grad_queries.astype(jnp.bfloat16))

    zeros_init = jnp.zeros((group_rows, head_count, head_width), jnp.float32)
    (key_grads, value_grads), grad_queries = lax.scan(
        one_block, (zeros_init, zeros_init), jnp.arange(group_rows // block_rows, dtype=jnp.int32)
    )
    grad_queries = grad_queries.reshape(group_rows, head_count, head_width)
    return (grad_queries, key_grads.astype(jnp.bfloat16), value_grads.astype(jnp.bfloat16))


def local(
    tokens,
    conditioning,
    slot_ids,
    dino_target,
    out_cotangent,
    ada_weight,
    qkv_weight,
    attn_weight,
    up_weight,
    down_weight,
    first_proj,
    second_proj,
    third_proj,
    ada_bias,
    query_bias,
    value_bias,
    attn_bias,
    up_bias,
    down_bias,
    first_bias,
    second_bias,
    third_bias,
):
    tok_rows, model_width = tokens.shape
    seq_count = lax.axis_size("seq")
    seq_place = lax.axis_index("seq")
    slot_count = conditioning.shape[0]
    ada_cols, qkv_cols, attn_cols, up_cols, down_cols, first_cols, second_cols, third_cols = (
        lax.all_gather(ada_weight, "seq", axis=1, tiled=True),
        lax.all_gather(qkv_weight, "seq", axis=1, tiled=True),
        lax.all_gather(attn_weight, "seq", axis=1, tiled=True),
        lax.all_gather(up_weight, "seq", axis=1, tiled=True),
        lax.all_gather(down_weight, "seq", axis=1, tiled=True),
        lax.all_gather(first_proj, "seq", axis=1, tiled=True),
        lax.all_gather(second_proj, "seq", axis=1, tiled=True),
        lax.all_gather(third_proj, "seq", axis=1, tiled=True),
    )
    ada_full, qkv_full, attn_full, up_full, down_full, first_full, second_full, third_full = (
        lax.all_gather(ada_cols, "img", axis=0, tiled=True),
        lax.all_gather(qkv_cols, "img", axis=0, tiled=True),
        lax.all_gather(attn_cols, "img", axis=0, tiled=True),
        lax.all_gather(up_cols, "img", axis=0, tiled=True),
        lax.all_gather(down_cols, "img", axis=0, tiled=True),
        lax.all_gather(first_cols, "img", axis=0, tiled=True),
        lax.all_gather(second_cols, "img", axis=0, tiled=True),
        lax.all_gather(third_cols, "img", axis=0, tiled=True),
    )
    cond_act, cond_back = jax.vjp(jax.nn.silu, conditioning)
    cond_low = cond_act.astype(jnp.bfloat16)
    modulation = product(cond_low, ada_full) + ada_bias
    my_slots = lax.dynamic_slice_in_dim(slot_ids, seq_place * tok_rows, tok_rows, 0)
    one_hot = (my_slots[:, None] == jnp.arange(slot_count, dtype=jnp.int32)[None, :]).astype(
        jnp.float32
    )
    mod_rows = jnp.dot(
        one_hot, modulation, precision=HIGHEST_PREC, preferred_element_type=jnp.float32
    )
    shift_a, scale_a, gate_a, shift_b, scale_b, gate_b = jnp.split(mod_rows, 6, axis=1)
    tokens_f = tokens.astype(jnp.float32)
    normed_a, norm_back_a = jax.vjp(layer_norm, tokens_f)
    hidden_a = (normed_a * (1.0 + scale_a) + shift_a).astype(jnp.bfloat16)
    qkv_rows = product(hidden_a, qkv_full)
    head_shape = (tok_rows, H, HD)
    queries = (qkv_rows[:, :model_width] + query_bias).astype(jnp.bfloat16).reshape(head_shape)
    key_rows = qkv_rows[:, model_width : 2 * model_width].astype(jnp.bfloat16).reshape(head_shape)
    value_rows = (
        (qkv_rows[:, 2 * model_width :] + value_bias).astype(jnp.bfloat16).reshape(head_shape)
    )
    queries_h, keys_h, values_h = (
        lax.all_to_all(queries, "seq", split_axis=1, concat_axis=0, tiled=True),
        lax.all_to_all(key_rows, "seq", split_axis=1, concat_axis=0, tiled=True),
        lax.all_to_all(value_rows, "seq", split_axis=1, concat_axis=0, tiled=True),
    )
    attended_h, log_total = attend_forward(queries_h, keys_h, values_h, slot_ids)
    attended = lax.all_to_all(attended_h, "seq", split_axis=0, concat_axis=1, tiled=True).reshape(
        tok_rows, model_width
    )
    branch_a = product(attended, attn_full) + attn_bias
    after_attn = tokens_f + gate_a * branch_a
    normed_b, norm_back_b = jax.vjp(layer_norm, after_attn)
    hidden_b = (normed_b * (1.0 + scale_b) + shift_b).astype(jnp.bfloat16)
    pre_act = product(hidden_b, up_full) + up_bias
    activation, gelu_back = jax.vjp(partial(jax.nn.gelu, approximate=True), pre_act)
    act_low = activation.astype(jnp.bfloat16)
    branch_b = product(act_low, down_full) + down_bias
    result = after_attn + gate_b * branch_b
    feed_low = result.astype(jnp.bfloat16)
    first_pre = product(feed_low, first_full) + first_bias
    first_act, first_back = jax.vjp(jax.nn.silu, first_pre)
    first_low = first_act.astype(jnp.bfloat16)
    second_pre = product(first_low, second_full) + second_bias
    second_act, second_back = jax.vjp(jax.nn.silu, second_pre)
    second_low = second_act.astype(jnp.bfloat16)
    aligned = product(second_low, third_full) + third_bias
    target_f = dino_target.astype(jnp.float32)
    align_value, align_back = jax.vjp(partial(cosine_total, target=target_f), aligned)
    (
        ada_again,
        qkv_again,
        attn_again,
        up_again,
        down_again,
        first_again,
        second_again,
        third_again,
    ) = (
        lax.all_gather(ada_weight, "seq", axis=1, tiled=True),
        lax.all_gather(qkv_weight, "seq", axis=1, tiled=True),
        lax.all_gather(attn_weight, "seq", axis=1, tiled=True),
        lax.all_gather(up_weight, "seq", axis=1, tiled=True),
        lax.all_gather(down_weight, "seq", axis=1, tiled=True),
        lax.all_gather(first_proj, "seq", axis=1, tiled=True),
        lax.all_gather(second_proj, "seq", axis=1, tiled=True),
        lax.all_gather(third_proj, "seq", axis=1, tiled=True),
    )
    ada_back, qkv_back, attn_back, up_back, down_back, first_wback, second_wback, third_wback = (
        lax.all_gather(ada_again, "img", axis=0, tiled=True),
        lax.all_gather(qkv_again, "img", axis=0, tiled=True),
        lax.all_gather(attn_again, "img", axis=0, tiled=True),
        lax.all_gather(up_again, "img", axis=0, tiled=True),
        lax.all_gather(down_again, "img", axis=0, tiled=True),
        lax.all_gather(first_again, "img", axis=0, tiled=True),
        lax.all_gather(second_again, "img", axis=0, tiled=True),
        lax.all_gather(third_again, "img", axis=0, tiled=True),
    )
    grad_aligned = align_back(jnp.ones((), jnp.float32))[0].astype(jnp.bfloat16)
    third_bias_term = column_sums(grad_aligned)
    third_term = product_tn(second_low, grad_aligned)
    grad_second = second_back(product_nt(grad_aligned, third_wback))[0].astype(jnp.bfloat16)
    second_bias_term = column_sums(grad_second)
    second_term = product_tn(first_low, grad_second)
    grad_first = first_back(product_nt(grad_second, second_wback))[0].astype(jnp.bfloat16)
    first_bias_term = column_sums(grad_first)
    first_term = product_tn(feed_low, grad_first)
    grad_result = out_cotangent.astype(jnp.float32) + product_nt(grad_first, first_wback)
    grad_branch_b = (gate_b * grad_result).astype(jnp.bfloat16)
    down_bias_term = column_sums(grad_branch_b)
    down_term = product_tn(act_low, grad_branch_b)
    grad_pre = gelu_back(product_nt(grad_branch_b, down_back))[0].astype(jnp.bfloat16)
    up_bias_term = column_sums(grad_pre)
    up_term = product_tn(hidden_b, grad_pre)
    grad_hidden_b = product_nt(grad_pre, up_back)
    grad_after = grad_result + norm_back_b(grad_hidden_b * (1.0 + scale_b))[0]
    grad_branch_a = (gate_a * grad_after).astype(jnp.bfloat16)
    attn_bias_term = column_sums(grad_branch_a)
    attn_term = product_tn(attended, grad_branch_a)
    grad_attended = product_nt(grad_branch_a, attn_back).astype(jnp.bfloat16).reshape(head_shape)
    grad_heads = lax.all_to_all(grad_attended, "seq", split_axis=1, concat_axis=0, tiled=True)
    grad_queries_h, grad_keys_h, grad_values_h = attend_backward(
        queries_h, keys_h, values_h, slot_ids, log_total, grad_heads
    )
    grad_queries, grad_keys, grad_values = (
        lax.all_to_all(grad_queries_h, "seq", split_axis=0, concat_axis=1, tiled=True),
        lax.all_to_all(grad_keys_h, "seq", split_axis=0, concat_axis=1, tiled=True),
        lax.all_to_all(grad_values_h, "seq", split_axis=0, concat_axis=1, tiled=True),
    )
    grad_qkv = jnp.concatenate(
        (
            grad_queries.reshape(tok_rows, model_width),
            grad_keys.reshape(tok_rows, model_width),
            grad_values.reshape(tok_rows, model_width),
        ),
        axis=1,
    )
    query_bias_term = column_sums(grad_qkv[:, :model_width])
    value_bias_term = column_sums(grad_qkv[:, 2 * model_width :])
    qkv_term = product_tn(hidden_a, grad_qkv)
    grad_hidden_a = product_nt(grad_qkv, qkv_back)
    tokens_grad = grad_after + norm_back_a(grad_hidden_a * (1.0 + scale_a))[0]
    grad_mod_rows = jnp.concatenate(
        (
            grad_hidden_a,
            grad_hidden_a * normed_a,
            grad_after * branch_a,
            grad_hidden_b,
            grad_hidden_b * normed_b,
            grad_result * branch_b,
        ),
        axis=1,
    )
    partial_mod = lax.dot_general(
        one_hot,
        grad_mod_rows,
        (((0,), (0,)), ((), ())),
        precision=HIGHEST_PREC,
        preferred_element_type=jnp.float32,
    )
    grad_mod = lax.psum(partial_mod.astype(jnp.bfloat16), "seq")
    conditioning_grad = cond_back(product_nt(grad_mod, ada_back))[0]
    ada_bias_term = jnp.where(seq_place == 0, column_sums(grad_mod), 0.0)
    mod_cols_count = grad_mod.shape[1] // seq_count
    my_mod_cols = lax.dynamic_slice_in_dim(grad_mod, seq_place * mod_cols_count, mod_cols_count, 1)
    ada_weight_grad = lax.psum_scatter(
        product_tn(cond_low, my_mod_cols), "img", scatter_dimension=0, tiled=True
    )
    (
        qkv_rows_sum,
        attn_rows_sum,
        up_rows_sum,
        down_rows_sum,
        first_rows_sum,
        second_rows_sum,
        third_rows_sum,
    ) = (
        lax.psum_scatter(qkv_term, "img", scatter_dimension=0, tiled=True),
        lax.psum_scatter(attn_term, "img", scatter_dimension=0, tiled=True),
        lax.psum_scatter(up_term, "img", scatter_dimension=0, tiled=True),
        lax.psum_scatter(down_term, "img", scatter_dimension=0, tiled=True),
        lax.psum_scatter(first_term, "img", scatter_dimension=0, tiled=True),
        lax.psum_scatter(second_term, "img", scatter_dimension=0, tiled=True),
        lax.psum_scatter(third_term, "img", scatter_dimension=0, tiled=True),
    )
    (
        qkv_weight_grad,
        attn_weight_grad,
        up_weight_grad,
        down_weight_grad,
        first_proj_grad,
        second_proj_grad,
        third_proj_grad,
    ) = (
        lax.psum_scatter(
            qkv_rows_sum.astype(jnp.bfloat16), "seq", scatter_dimension=1, tiled=True
        ).astype(jnp.float32),
        lax.psum_scatter(
            attn_rows_sum.astype(jnp.bfloat16), "seq", scatter_dimension=1, tiled=True
        ).astype(jnp.float32),
        lax.psum_scatter(
            up_rows_sum.astype(jnp.bfloat16), "seq", scatter_dimension=1, tiled=True
        ).astype(jnp.float32),
        lax.psum_scatter(
            down_rows_sum.astype(jnp.bfloat16), "seq", scatter_dimension=1, tiled=True
        ).astype(jnp.float32),
        lax.psum_scatter(
            first_rows_sum.astype(jnp.bfloat16), "seq", scatter_dimension=1, tiled=True
        ).astype(jnp.float32),
        lax.psum_scatter(
            second_rows_sum.astype(jnp.bfloat16), "seq", scatter_dimension=1, tiled=True
        ).astype(jnp.float32),
        lax.psum_scatter(
            third_rows_sum.astype(jnp.bfloat16), "seq", scatter_dimension=1, tiled=True
        ).astype(jnp.float32),
    )
    (
        ada_bias_grad,
        query_bias_grad,
        value_bias_grad,
        attn_bias_grad,
        up_bias_grad,
        down_bias_grad,
        first_bias_grad,
        second_bias_grad,
        third_bias_grad,
    ) = lax.psum(
        (
            ada_bias_term,
            query_bias_term,
            value_bias_term,
            attn_bias_term,
            up_bias_term,
            down_bias_term,
            first_bias_term,
            second_bias_term,
            third_bias_term,
        ),
        ("img", "seq"),
    )
    return (
        feed_low,
        tokens_grad,
        conditioning_grad,
        ada_weight_grad,
        qkv_weight_grad,
        attn_weight_grad,
        up_weight_grad,
        down_weight_grad,
        first_proj_grad,
        second_proj_grad,
        third_proj_grad,
        ada_bias_grad,
        query_bias_grad,
        value_bias_grad,
        attn_bias_grad,
        up_bias_grad,
        down_bias_grad,
        first_bias_grad,
        second_bias_grad,
        third_bias_grad,
    )


def solution(mesh):
    return jax.shard_map(
        local,
        mesh=mesh,
        in_specs=(
            P(("img", "seq"), None),
            P("img", None),
            P("img"),
            P(("img", "seq"), None),
            P(("img", "seq"), None),
            P("img", "seq"),
            P("img", "seq"),
            P("img", "seq"),
            P("img", "seq"),
            P("img", "seq"),
            P("img", "seq"),
            P("img", "seq"),
            P("img", "seq"),
            P(),
            P(),
            P(),
            P(),
            P(),
            P(),
            P(),
            P(),
            P(),
        ),
        out_specs=(
            P(("img", "seq"), None),
            P(("img", "seq"), None),
            P("img", None),
            P("img", "seq"),
            P("img", "seq"),
            P("img", "seq"),
            P("img", "seq"),
            P("img", "seq"),
            P("img", "seq"),
            P("img", "seq"),
            P("img", "seq"),
            P(),
            P(),
            P(),
            P(),
            P(),
            P(),
            P(),
            P(),
            P(),
        ),
        check_vma=False,
    )
```

profile of v0, /device:TPU:0, one launch (start us, length us, event | category | flops | bytes accessed | tf_op | source)
XLA Modules:
  0.0 3260.9 jit_solution(17865043251224692005)
XLA Ops:
  10.0 24.7 all-gather.38.cloned.1.call-done
  97.4 218.6 %all-gather.16.cloned.1.call-done = bf16[1152,6912]{1,0:T(8,128)(2,1)} async-done(((bf16[144,6912]{1,0:T(8,128)(2,1)}), bf16[1152,6912]{1,0:T(8,128)(2,1)}) %all-gather.16.cloned.1.call-update) | async-done | bytes 15925264 | tf_op jit(solution)/shard_map/all_gather | solution.py:173
  330.0 106.5 %all-gather.18.cloned.1.call-done = bf16[1152,3456]{1,0:T(8,128)(2,1)} async-done(((bf16[144,3456]{1,0:T(8,128)(2,1)}), bf16[1152,3456]{1,0:T(8,128)(2,1)}) %all-gather.18.cloned.1.call-update) | async-done | bytes 7962640 | tf_op jit(solution)/shard_map/all_gather | solution.py:174
  484.9 18.3 while.27
  508.4 17.8 all_gather.78
  534.2 111.5 %all-gather.24.cloned.1.call-done = bf16[1152,4608]{1,0:T(8,128)(2,1)} async-done(((bf16[144,4608]{1,0:T(8,128)(2,1)}), bf16[1152,4608]{1,0:T(8,128)(2,1)}) %all-gather.24.cloned.1.call-update) | async-done | bytes 10616848 | tf_op jit(solution)/shard_map/all_gather | solution.py:176
  654.7 143.8 %all-gather.28.cloned.1.call-done = bf16[4608,1152]{1,0:T(8,128)(2,1)} async-done(((bf16[576,1152]{1,0:T(8,128)(2,1)}), bf16[4608,1152]{1,0:T(8,128)(2,1)}) %all-gather.28.cloned.1.call-update) | async-done | bytes 10616848 | tf_op jit(solution)/shard_map/all_gather | solution.py:177
  808.7 70.0 %all-gather.30.cloned.1.call-done = bf16[1152,2048]{1,0:T(8,128)(2,1)} async-done(((bf16[144,2048]{1,0:T(8,128)(2,1)}), bf16[1152,2048]{1,0:T(8,128)(2,1)}) %all-gather.30.cloned.1.call-update) | async-done | bytes 4718608 | tf_op jit(solution)/shard_map/all_gather | solution.py:178
  883.9 120.0 %all-gather.34.cloned.1.call-done = bf16[2048,2048]{1,0:T(8,128)(2,1)} async-done(((bf16[256,2048]{1,0:T(8,128)(2,1)}), bf16[2048,2048]{1,0:T(8,128)(2,1)}) %all-gather.34.cloned.1.call-update) | async-done | bytes 8388624 | tf_op jit(solution)/shard_map/all_gather | solution.py:179
  1011.6 55.5 %all-gather.36.cloned.1.call-done = bf16[2048,768]{0,1:T(8,128)(2,1)} async-done(((bf16[256,768]{0,1:T(8,128)(2,1)}), bf16[2048,768]{0,1:T(8,128)(2,1)}) %all-gather.36.cloned.1.call-update) | async-done | bytes 3145744 | tf_op jit(solution)/shard_map/all_gather | solution.py:180
  1142.8 44.7 %while.28 = (s32[]{:T(128)}, f32[1024,4,72]{0,2,1:T(8,128)S(1)}, f32[1024,4,72]{0,2,1:T(8,128)}, bf16[2,512,4,72]{1,3,2,0:T(8,128)(2,1)}, s32[2]{0:T(128)S(1)}, ...) while((s32[]{:T(128)}, f32[1024,4,72]{0,2,1:T(8,128)S(1)}, ...), condition=%wide.region_15.16_spmd.clone, body=%wide.region_13.15_spmd.clone.sunk | while | flops 1543698432 | bytes 144935824 | solution.py:127
  1294.9 39.0 %reduce-scatter.44.cloned.1.call-done = f32[256,768]{1,0:T(8,128)} async-done(((f32[2048,768]{1,0:T(8,128)}), f32[256,768]{1,0:T(8,128)}) %reduce-scatter.44.cloned.1.call-update) | async-done | bytes 786448 | tf_op jit(solution)/shard_map/reduce_scatter | solution.py:345
  1336.0 164.3 %reduce-scatter.36.cloned.1.call-done = f32[144,2048]{1,0:T(8,128)} async-done(((f32[1152,2048]{1,0:T(8,128)}), f32[144,2048]{1,0:T(8,128)}) %reduce-scatter.36.cloned.1.call-update) | async-done | bytes 1179664 | tf_op jit(solution)/shard_map/reduce_scatter | solution.py:343
  1502.6 270.4 %reduce-scatter.28.cloned.1.call-done = f32[144,3456]{1,0:T(8,128)} async-done(((f32[1152,3456]{1,0:T(8,128)}), f32[144,3456]{1,0:T(8,128)}) %reduce-scatter.28.cloned.1.call-update) | async-done | bytes 1990672 | tf_op jit(solution)/shard_map/reduce_scatter | solution.py:339
  1778.2 280.6 %reduce-scatter.40.cloned.1.call-done = f32[256,2048]{1,0:T(8,128)} async-done(((f32[2048,2048]{1,0:T(8,128)}), f32[256,2048]{1,0:T(8,128)}) %reduce-scatter.40.cloned.1.call-update) | async-done | bytes 2097168 | tf_op jit(solution)/shard_map/reduce_scatter | solution.py:344
  2061.7 347.3 %reduce-scatter.34.cloned.1.call-done = f32[576,1152]{1,0:T(8,128)} async-done(((f32[4608,1152]{1,0:T(8,128)}), f32[576,1152]{1,0:T(8,128)}) %reduce-scatter.34.cloned.1.call-update) | async-done | bytes 2654224 | tf_op jit(solution)/shard_map/reduce_scatter | solution.py:342
  2434.2 325.0 %reduce-scatter.32.cloned.1.call-done = f32[144,4608]{1,0:T(8,128)} async-done(((f32[1152,4608]{1,0:T(8,128)}), f32[144,4608]{1,0:T(8,128)}) %reduce-scatter.32.cloned.1.call-update) | async-done | bytes 2654224 | tf_op jit(solution)/shard_map/reduce_scatter | solution.py:341
  2809.2 22.4 reduce-scatter.38.cloned.1.call-done
  2833.3 30.3 reduce-scatter.46.cloned.1.call-done
  2865.7 25.5 reduce-scatter.42.cloned.1.call-done
  2892.9 28.3 reduce-scatter.52.cloned.1.call-done
  2923.6 33.4 %reduce-scatter.50.cloned.1.call-done = bf16[1152,144]{1,0:T(8,128)(2,1)} async-done(((bf16[4608,144]{1,0:T(8,128)(2,1)}), bf16[1152,144]{1,0:T(8,128)(2,1)}) %reduce-scatter.50.cloned.1.call-update) | async-done | bytes 331792
  2959.1 130.4 %all-reduce.3.cloned.1.call-done = (f32[6912]{0:T(1024)}, f32[1152]{0:T(1024)}, f32[1152]{0:T(1024)}, f32[1152]{0:T(1024)}, f32[4608]{0:T(1024)}, /*index=5*/f32...) async-done(((f32[6912]{0:T(1024)}, f32[1152]{0:T(1024)}, f32[1152]{0:T(1024)}, f32[1152]{0:T(1024)}, f32[4608]{0:T(1024)}, /*index=5*/f32[1152]{0:T(1024)}, ...) | async-done | bytes 83984 | tf_op jit(solution)/shard_map/psum | solution.py:388
  3089.5 152.6 %reduce-scatter.26.cloned.1.call-done = f32[144,1728]{1,0:T(8,128)} async-done(((f32[1152,1728]{1,0:T(8,128)}), f32[144,1728]{1,0:T(8,128)}) %reduce-scatter.26.cloned.1.call-update) | async-done | bytes 995344 | tf_op jit(solution)/shard_map/reduce_scatter | solution.py:327
  (400 shorter events, 524.5 us)
Async XLA Ops:
  10.0 306.1 %all-gather.16.cloned.1.call-start = ((), (), s32[]{:S(2)}) async-start(), calls=%async_computation.23 | async-start | bytes 17915904 | tf_op jit(solution)/shard_map/all_gather | solution.py:173
  40.2 396.3 %all-gather.18.cloned.1.call-start = ((), (), s32[]{:S(2)}) async-start(), calls=%async_computation.24 | async-start | bytes 8957952 | tf_op jit(solution)/shard_map/all_gather | solution.py:174
  56.2 471.3 %all-gather.20.cloned.1.call-start = ((), (), s32[]{:S(2)}) async-start(), calls=%async_computation.25 | async-start | bytes 2985984 | tf_op jit(solution)/shard_map/all_gather | solution.py:175
  64.3 581.4 %all-gather.24.cloned.1.call-start = ((), (), s32[]{:S(2)}) async-start(), calls=%async_computation.27 | async-start | bytes 11943936 | tf_op jit(solution)/shard_map/all_gather | solution.py:176
  65.1 733.5 %all-gather.28.cloned.1.call-start = ((), (), s32[]{:S(2)}) async-start(), calls=%async_computation.29 | async-start | bytes 11943936 | tf_op jit(solution)/shard_map/all_gather | solution.py:177
  81.2 797.4 %all-gather.30.cloned.1.call-start = ((), (), s32[]{:S(2)}) async-start(), calls=%async_computation.30 | async-start | bytes 5308416 | tf_op jit(solution)/shard_map/all_gather | solution.py:178
  89.4 914.5 %all-gather.34.cloned.1.call-start = ((), (), s32[]{:S(2)}) async-start(), calls=%async_computation.32 | async-start | bytes 9437184 | tf_op jit(solution)/shard_map/all_gather | solution.py:179
  508.3 558.8 %all-gather.36.cloned.1.call-start = ((), (), s32[]{:S(2)}) async-start(), calls=%async_computation.33 | async-start | bytes 3538944 | tf_op jit(solution)/shard_map/all_gather | solution.py:180
  526.2 766.4 %reduce-scatter.30.cloned.1.call-start = ((), (), s32[]{:S(2)}) async-start(), calls=%async_computation.36 | async-start | bytes 5971968 | tf_op jit(solution)/shard_map/reduce_scatter | solution.py:340
  1109.9 224.0 %reduce-scatter.44.cloned.1.call-start = ((), (), s32[]{:S(2)}) async-start(), calls=%async_computation.43 | async-start | bytes 7077888 | tf_op jit(solution)/shard_map/reduce_scatter | solution.py:345
  1116.5 383.9 %reduce-scatter.36.cloned.1.call-start = ((), (), s32[]{:S(2)}) async-start(), calls=%async_computation.39 | async-start | bytes 10616832 | tf_op jit(solution)/shard_map/reduce_scatter | solution.py:343
  1229.5 543.5 %reduce-scatter.28.cloned.1.call-start = ((), (), s32[]{:S(2)}) async-start(), calls=%async_computation.35 | async-start | bytes 17915904 | tf_op jit(solution)/shard_map/reduce_scatter | solution.py:339
  1254.4 804.4 %reduce-scatter.40.cloned.1.call-start = ((), (), s32[]{:S(2)}) async-start(), calls=%async_computation.41 | async-start | bytes 18874368 | tf_op jit(solution)/shard_map/reduce_scatter | solution.py:344
  1264.7 1144.3 %reduce-scatter.34.cloned.1.call-start = ((), (), s32[]{:S(2)}) async-start(), calls=%async_computation.38 | async-start | bytes 23887872 | tf_op jit(solution)/shard_map/reduce_scatter | solution.py:342
  1279.6 1479.6 %reduce-scatter.32.cloned.1.call-start = ((), (), s32[]{:S(2)}) async-start(), calls=%async_computation.37 | async-start | bytes 23887872 | tf_op jit(solution)/shard_map/reduce_scatter | solution.py:341
  1292.5 1513.2 %reduce-scatter.48.cloned.1.call-start = ((), (), s32[]{:S(2)}) async-start(), calls=%async_computation.46 | async-start | bytes 737280
  1294.8 1512.6 %reduce-scatter.54.cloned.1.call-start = ((), (), s32[]{:S(2)}) async-start(), calls=%async_computation.49 | async-start | bytes 491520
  1336.0 1495.7 %reduce-scatter.38.cloned.1.call-start = ((), (), s32[]{:S(2)}) async-start(), calls=%async_computation.40 | async-start | bytes 737280 | tf_op jit(solution)/shard_map/reduce_scatter | solution.py:368
  1502.5 1361.1 %reduce-scatter.46.cloned.1.call-start = ((), (), s32[]{:S(2)}) async-start(), calls=%async_computation.45 | async-start | bytes 2211840
  1778.2 1112.9 %reduce-scatter.42.cloned.1.call-start = ((), (), s32[]{:S(2)}) async-start(), calls=%async_computation.42 | async-start | bytes 1310720 | tf_op jit(solution)/shard_map/reduce_scatter | solution.py:371
  2061.6 859.6 %reduce-scatter.52.cloned.1.call-start = ((), (), s32[]{:S(2)}) async-start(), calls=%async_computation.48 | async-start | bytes 1843200
  2414.6 542.4 %reduce-scatter.50.cloned.1.call-start = ((), (), s32[]{:S(2)}) async-start(), calls=%async_computation.47 | async-start | bytes 2949120
  2763.5 326.0 %all-reduce.3.cloned.1.call-start = ((), (), s32[]{:S(2)}) async-start(), calls=%async_computation.50 | async-start | bytes 204800 | tf_op jit(solution)/shard_map/psum | solution.py:388
  2790.6 451.4 %reduce-scatter.26.cloned.1.call-start = ((), (), s32[]{:S(2)}) async-start(), calls=%async_computation.34 | async-start | bytes 9289728 | tf_op jit(solution)/shard_map/reduce_scatter | solution.py:327
  (89 other events, 4494.5 us)
Sparse Core Ops, SparseCore 0:
  9.6 25.0 all-gather.37
  36.3 21.5 all-gather.21
  98.8 217.1 all-gather.15
  318.6 117.7 all-gather.17
  439.2 53.1 all-gather.19
  494.6 151.0 all-gather.23
  647.9 150.6 all-gather.27
  800.6 78.0 all-gather.29
  880.8 123.0 all-gather.33
  1005.8 61.2 all-gather.35
  1110.0 102.2 reduce-scatter.29
  1216.2 117.6 reduce-scatter.43
  1337.7 162.5 reduce-scatter.35
  1504.6 268.3 reduce-scatter.27
  1777.1 281.7 reduce-scatter.39
  2062.6 346.3 reduce-scatter.33
  2413.3 345.8 reduce-scatter.31
  2809.6 22.0 reduce-scatter.37
  2834.2 29.3 reduce-scatter.45
  2866.2 24.8 reduce-scatter.41
  2893.7 27.5 reduce-scatter.51
  2923.8 33.0 reduce-scatter.49
  2964.3 125.0 all-reduce.2
  3094.2 147.7 reduce-scatter.25
  (4 shorter events, 78.0 us)
where the time goes:
time: 3270 us; the launch traced here: 3260 us
  waiting for transfers between devices  2790 us (85%)
  matrix products  222 us (7%)
  local copies, waits for them, and re-layouts  82.8 us (3%)
  blocking collectives  58.4 us (2%)
  other arithmetic  54.3 us (2%)
    reduce_scatter x1, waiting for transfers between devices, local(): lax.psum_scatter(down_term, 'img', scatter_dimension=0, tiled=True)  347 us
    reduce_scatter x1, waiting for transfers between devices, local(): lax.psum_scatter(up_term, 'img', scatter_dimension=0, tiled=True)  325 us
    reduce_scatter x1, waiting for transfers between devices, local(): lax.psum_scatter(second_term, 'img', scatter_dimension=0, tiled=True)  281 us
    reduce_scatter x1, waiting for transfers between devices, local(): lax.psum_scatter(qkv_term, 'img', scatter_dimension=0, tiled=True)  270 us
    all_gather x1, waiting for transfers between devices, local(): lax.all_gather(ada_cols, 'img', axis=0, tiled=True)  219 us
    reduce_scatter x1, waiting for transfers between devices, local(): lax.psum_scatter(first_term, 'img', scatter_dimension=0, tiled=True)  164 us
    reduce_scatter x1, waiting for transfers between devices, local(): lax.psum_scatter(product_tn(cond_low, my_mod_cols), 'img', scatter_dimens...  153 us
    all_gather x1, waiting for transfers between devices, local(): lax.all_gather(down_cols, 'img', axis=0, tiled=True)  144 us
  transfers between devices with their start and end apart: 36, of which 30 were waited for; matrix products, arithmetic and copies ran while one was open for 9% of the time, Pallas kernels for 0%

commit v1 on v0

v1 whole, which is shorter than its diff:
```python
import jax
import jax.numpy as jnp
from jax import lax
from jax.experimental import pallas as pl
from jax.experimental.pallas import tpu as pltpu
from jax.sharding import PartitionSpec as P

H = 16
HD = 72
LANES = 128
EPS_NORM = 1e-06
EPS_COS = 1e-06
LAMBDA_ALIGN = 0.5
MASKED_SCORE = -1e30
F32 = jnp.float32
BF16 = jnp.bfloat16
SEQ = 4


def product(left, right, out=F32):
    return lax.dot_general(
        left, right, (((1,), (0,)), ((), ())), preferred_element_type=F32
    ).astype(out)


def product_tn(left, right, out=F32):
    return lax.dot_general(
        left, right, (((0,), (0,)), ((), ())), preferred_element_type=F32
    ).astype(out)


def product_nt(left, right, out=F32):
    return lax.dot_general(
        left, right, (((1,), (1,)), ((), ())), preferred_element_type=F32
    ).astype(out)


def column_sums(values):
    return jnp.sum(values.astype(F32), axis=0)


def norm_parts(values):
    centered = values - jnp.mean(values, axis=-1, keepdims=True)
    inverse = lax.rsqrt(jnp.mean(centered * centered, axis=-1, keepdims=True) + EPS_NORM)
    return centered * inverse, inverse


def norm_back(normed, inverse, grad):
    return inverse * (
        grad
        - jnp.mean(grad, axis=-1, keepdims=True)
        - normed * jnp.mean(grad * normed, axis=-1, keepdims=True)
    )


def silu_parts(values):
    gate = 1.0 / (1.0 + jnp.exp(-values))
    return values * gate, gate * (1.0 + values * (1.0 - gate))


GELU_C = 0.7978845608028654


def gelu_parts(values):
    inner = GELU_C * (values + 0.044715 * values * values * values)
    bent = jnp.tanh(inner)
    slope = GELU_C * (1.0 + 3.0 * 0.044715 * values * values)
    value = 0.5 * values * (1.0 + bent)
    return value, 0.5 * (1.0 + bent) + 0.5 * values * (1.0 - bent * bent) * slope


def swap(values, distance):
    return lax.ppermute(values, "seq", [(i, i ^ distance) for i in range(SEQ)])


def gather_rows(own):
    across = swap(own, 2)
    near = swap(own, 1)
    far = swap(across, 1)
    return jnp.concatenate([own, near], 0), jnp.concatenate([across, far], 0)


def scatter_rows(near, far):
    rows = near.shape[0] // 2
    from_far = swap(far[rows:], 1)
    across = swap((far[:rows].astype(F32) + from_far.astype(F32)).astype(BF16), 2)
    from_near = swap(near[rows:], 1)
    return near[:rows].astype(F32) + from_near.astype(F32) + across.astype(F32)


def img_swap(values):
    count = lax.axis_size("img")
    return lax.ppermute(values, "img", [(i, i ^ 1) for i in range(count)])


def slow_groups():
    half = lax.axis_size("img") // 2
    return [[2 * k + fast for k in range(half)] for fast in range(2)]


def gather_img(shard):
    half = lax.axis_size("img") // 2
    fast = lax.axis_index("img") % 2
    copies = jnp.broadcast_to(shard[None], (half,) + shard.shape)
    mine = lax.all_to_all(
        copies, "img", split_axis=0, concat_axis=0, tiled=True, axis_index_groups=slow_groups()
    )
    other = img_swap(mine)
    return mine, other, fast


def interleave(gathered, first, count):
    mine, other, fast = gathered
    half, rows = mine.shape[:2]
    mine, other = mine[:, :, first : first + count], other[:, :, first : first + count]
    even = jnp.where(fast == 0, mine, other)
    odd = jnp.where(fast == 0, other, mine)
    return jnp.concatenate([even[:, None], odd[:, None]], 1).reshape(2 * half * rows, count)


def reduce_img(blocks):
    count, rows, cols = blocks.shape
    half = count // 2
    fast = lax.axis_index("img") % 2
    pairs = blocks.reshape(half, 2, rows, cols)
    keep = jnp.where(fast == 0, pairs[:, 0], pairs[:, 1])
    send = jnp.where(fast == 0, pairs[:, 1], pairs[:, 0])
    joined = (keep.astype(F32) + img_swap(send).astype(F32)).astype(BF16)
    parts = lax.all_to_all(
        joined, "img", split_axis=0, concat_axis=0, tiled=True, axis_index_groups=slow_groups()
    )
    return jnp.sum(parts.astype(F32), axis=0)


def seq_exchange(parts):
    return lax.all_to_all(parts, "seq", split_axis=0, concat_axis=0, tiled=True)


def img_exchange(parts):
    return lax.all_to_all(parts, "img", split_axis=0, concat_axis=0, tiled=True)


def img_gather(values):
    count = lax.axis_size("img")
    return img_exchange(jnp.broadcast_to(values[None], (count,) + values.shape))


def pick(stacked, index):
    return lax.dynamic_index_in_dim(stacked, index, 0, keepdims=False)


def attend_kernel(slots, q_ref, k_ref, v_ref, out_ref):
    rows = q_ref.shape[0] // SEQ
    scale = HD ** (-0.5)
    keys = k_ref[...]
    values = v_ref[...]
    for block in range(SEQ):
        queries = q_ref[block * rows : (block + 1) * rows, :]
        scores = lax.dot_general(
            queries, keys, (((1,), (1,)), ((), ())), preferred_element_type=F32
        )
        scores = jnp.concatenate(
            [
                jnp.where(
                    slots[block] == slots[other],
                    scores[:, other * rows : (other + 1) * rows] * scale,
                    MASKED_SCORE,
                )
                for other in range(SEQ)
            ],
            axis=1,
        )
        raised = jnp.exp(scores - jnp.max(scores, axis=1, keepdims=True))
        probs = raised / jnp.sum(raised, axis=1, keepdims=True)
        out_ref[block * rows : (block + 1) * rows, :] = jnp.dot(
            probs.astype(BF16), values, preferred_element_type=F32
        ).astype(BF16)


def attend_back_kernel(slots, q_ref, k_ref, v_ref, g_ref, gq_ref, gk_ref, gv_ref, gk_sum, gv_sum):
    rows = q_ref.shape[0] // SEQ
    scale = HD ** (-0.5)
    keys = k_ref[...]
    values = v_ref[...]
    for block in range(SEQ):
        queries = q_ref[block * rows : (block + 1) * rows, :]
        grads = g_ref[block * rows : (block + 1) * rows, :]
        scores = lax.dot_general(
            queries, keys, (((1,), (1,)), ((), ())), preferred_element_type=F32
        )
        scores = jnp.concatenate(
            [
                jnp.where(
                    slots[block] == slots[other],
                    scores[:, other * rows : (other + 1) * rows] * scale,
                    MASKED_SCORE,
                )
                for other in range(SEQ)
            ],
            axis=1,
        )
        raised = jnp.exp(scores - jnp.max(scores, axis=1, keepdims=True))
        probs = raised / jnp.sum(raised, axis=1, keepdims=True)
        grad_probs = lax.dot_general(
            grads, values, (((1,), (1,)), ((), ())), preferred_element_type=F32
        )
        delta = jnp.sum(probs * grad_probs, axis=1, keepdims=True)
        grad_scores = (probs * (grad_probs - delta)).astype(BF16)
        gq_ref[block * rows : (block + 1) * rows, :] = (
            jnp.dot(grad_scores, keys, preferred_element_type=F32) * scale
        ).astype(BF16)
        gk = lax.dot_general(
            grad_scores, queries, (((0,), (0,)), ((), ())), preferred_element_type=F32
        )
        gv = lax.dot_general(
            probs.astype(BF16), grads, (((0,), (0,)), ((), ())), preferred_element_type=F32
        )
        if block == 0:
            gk_sum[...] = gk
            gv_sum[...] = gv
        else:
            gk_sum[...] += gk
            gv_sum[...] += gv
    gk_ref[...] = (gk_sum[...] * scale).astype(BF16)
    gv_ref[...] = gv_sum[...].astype(BF16)


def head_block(rows, first):
    return pl.BlockSpec((rows, LANES), lambda head, slots: (0, first + head))


def attend_forward(qkv, slots):
    rows, heads = qkv.shape[0], qkv.shape[1] // (3 * LANES)
    return pl.pallas_call(
        attend_kernel,
        grid_spec=pltpu.PrefetchScalarGridSpec(
            num_scalar_prefetch=1,
            grid=(heads,),
            in_specs=[head_block(rows, kind * heads) for kind in range(3)],
            out_specs=head_block(rows, 0),
        ),
        out_shape=jax.ShapeDtypeStruct((rows, heads * LANES), BF16),
        name="attend",
    )(slots, qkv, qkv, qkv)


def attend_backward(qkv, grads, slots):
    rows, heads = qkv.shape[0], qkv.shape[1] // (3 * LANES)
    shape = jax.ShapeDtypeStruct((rows, heads * LANES), BF16)
    return pl.pallas_call(
        attend_back_kernel,
        grid_spec=pltpu.PrefetchScalarGridSpec(
            num_scalar_prefetch=1,
            grid=(heads,),
            in_specs=[head_block(rows, kind * heads) for kind in range(3)] + [head_block(rows, 0)],
            out_specs=[head_block(rows, 0)] * 3,
            scratch_shapes=[pltpu.VMEM((rows, LANES), F32)] * 2,
        ),
        out_shape=(shape,) * 3,
        name="attend_back",
    )(slots, qkv, qkv, qkv, grads)


def pad_heads(values):
    lead = values.shape[:-1]
    heads = values.shape[-1] // HD
    parted = values.reshape(lead + (heads, HD))
    padded = jnp.pad(parted, [(0, 0)] * len(lead) + [(0, 0), (0, LANES - HD)])
    return padded.reshape(lead + (heads * LANES,))


def strip_heads(values):
    lead = values.shape[:-1]
    heads = values.shape[-1] // LANES
    return values.reshape(lead + (heads, LANES))[..., :HD].reshape(lead + (heads * HD,))


def local(
    tokens,
    conditioning,
    slot_ids,
    dino_target,
    out_cotangent,
    ada_weight,
    qkv_weight,
    attn_weight,
    up_weight,
    down_weight,
    first_proj,
    second_proj,
    third_proj,
    ada_bias,
    query_bias,
    value_bias,
    attn_bias,
    up_bias,
    down_bias,
    first_bias,
    second_bias,
    third_bias,
):
    own_rows, width = tokens.shape
    place = lax.axis_index("seq")
    img = lax.axis_size("img")
    slot_count = conditioning.shape[0]
    part_width = width // SEQ
    feat = qkv_weight.shape[0]
    mod_cols = ada_weight.shape[1]
    ff = up_bias.shape[0]
    ph = first_bias.shape[0]
    zd = third_bias.shape[0]
    ff_part = ff // SEQ
    ph_part = ph // SEQ
    ff_cell = ff // img // SEQ
    ph_cell = ph // img // SEQ

    dests = jnp.arange(SEQ, dtype=jnp.int32)
    three = qkv_weight.reshape(feat, 3, part_width).transpose(1, 0, 2)
    qkv_send = jnp.stack([pick(three, jnp.minimum((d - 3 * place) % SEQ, 2)) for d in range(SEQ)])
    qkv_got = seq_exchange(qkv_send)
    qkv_shard = jnp.concatenate(
        [pick(qkv_got, (kind * SEQ + place) // 3) for kind in range(3)], axis=1
    )
    qkv_all = gather_img(qkv_shard)

    rows_full = gather_rows(tokens)

    up_send = up_weight.reshape(feat, img // SEQ, SEQ, ff_cell).transpose(2, 0, 1, 3)
    up_send = up_send.reshape(SEQ, feat, part_width)
    down_send = down_weight.reshape(SEQ, ff_cell, part_width)
    first_send = first_proj.reshape(feat, img // SEQ, SEQ, ph_cell).transpose(2, 0, 1, 3)
    first_send = first_send.reshape(SEQ, feat, ph_part // SEQ)
    mlp_got = seq_exchange(jnp.concatenate([up_send, down_send, first_send], axis=2))
    second_got = seq_exchange(second_proj.reshape(SEQ, ph_cell, ph_part))
    mlp_got = mlp_got.transpose(1, 0, 2)
    up_shard = mlp_got[:, :, :part_width].reshape(feat, ff_part)
    down_shard = mlp_got[:, :, part_width : 2 * part_width].reshape(ff_cell, width)
    first_shard = mlp_got[:, :, 2 * part_width :].reshape(feat, ph_part)
    second_shard = second_got.transpose(1, 0, 2).reshape(ph_cell, ph)
    third_shard = third_proj.reshape(ph_cell, zd)

    cond_act, cond_slope = silu_parts(conditioning)
    cond_low = cond_act.astype(BF16)
    cond_cols = img_exchange(cond_low.reshape(slot_count, img, feat).transpose(1, 0, 2))
    cond_cols = cond_cols.reshape(img * slot_count, feat)
    mod_parts = img_exchange(product(cond_cols, ada_weight).reshape(img, slot_count, mod_cols))
    my_bias = lax.dynamic_slice_in_dim(ada_bias, place * mod_cols, mod_cols, 0)
    modulation = lax.all_gather(jnp.sum(mod_parts, axis=0) + my_bias, "seq", axis=1, tiled=True)
    block_slots = jnp.stack([slot_ids[(place ^ p) * own_rows] for p in range(SEQ)])
    block_mod = jnp.stack([pick(modulation, block_slots[p]) for p in range(SEQ)])
    shift_a, scale_a, gate_a, shift_b, scale_b, gate_b = jnp.split(block_mod[0], 6)

    def modulated(rows, first):
        normed, _ = norm_parts(rows.astype(F32).reshape(2, own_rows, width))
        shift = block_mod[first : first + 2, None, :width]
        scale = block_mod[first : first + 2, None, width : 2 * width]
        return (normed * (1.0 + scale) + shift).astype(BF16).reshape(2 * own_rows, width)

    hidden_a = jnp.concatenate([modulated(rows_full[0], 0), modulated(rows_full[1], 2)], 0)
    qkv_w = pad_heads(interleave(qkv_all, 0, 3 * part_width))
    q_bias = lax.dynamic_slice_in_dim(query_bias, place * part_width, part_width, 0)
    v_bias = lax.dynamic_slice_in_dim(value_bias, place * part_width, part_width, 0)
    qkv_bias = pad_heads(jnp.concatenate([q_bias, jnp.zeros_like(q_bias), v_bias]))
    qkv = (product(hidden_a, qkv_w) + qkv_bias).astype(BF16)
    attended_h = attend_forward(qkv, block_slots)
    attended_h = strip_heads(attended_h).reshape(SEQ, own_rows, part_width)
    heads_rel = jnp.stack([attended_h[0]] + [swap(attended_h[p], p) for p in range(1, SEQ)])
    attended = jnp.concatenate([pick(heads_rel, place ^ j) for j in range(SEQ)], axis=1)

    attn_up = gather_img(jnp.concatenate([attn_weight, up_shard], axis=1))
    attn_w = lax.all_gather(interleave(attn_up, 0, part_width), "seq", axis=1, tiled=True)
    up_w = interleave(attn_up, part_width, ff_part)
    down_first = gather_img(jnp.concatenate([down_shard, first_shard], axis=1))
    down_w = interleave(down_first, 0, width)
    first_w = interleave(down_first, width, ph_part)
    second_third = gather_img(jnp.concatenate([second_shard, third_shard], axis=1))
    second_w = interleave(second_third, 0, ph)
    third_w = interleave(second_third, ph, zd).reshape(ph, zd // SEQ)
    third_w = lax.all_gather(third_w, "seq", axis=1, tiled=True)

    tokens_f = tokens.astype(F32)
    branch_a = product(attended, attn_w) + attn_bias
    after_attn = tokens_f + gate_a * branch_a
    normed_b, inverse_b = norm_parts(after_attn)
    hidden_b = gather_rows((normed_b * (1.0 + scale_b) + shift_b).astype(BF16))

    my_up_bias = up_bias.reshape(img, SEQ, ff_cell)
    my_up_bias = lax.dynamic_index_in_dim(my_up_bias, place, 1, keepdims=False).reshape(ff_part)
    acts, slopes, sums = [], [], []
    for side in range(2):
        value, slope = gelu_parts(product(hidden_b[side], up_w) + my_up_bias)
        acts.append(value.astype(BF16))
        slopes.append(slope)
        sums.append(product(acts[side], down_w, BF16))
    branch_b = scatter_rows(*sums) + down_bias
    result = after_attn + gate_b * branch_b
    feed_low = result.astype(BF16)

    feed = gather_rows(feed_low)
    my_first_bias = first_bias.reshape(img, SEQ, ph_cell)
    my_first_bias = lax.dynamic_index_in_dim(my_first_bias, place, 1, keepdims=False)
    my_first_bias = my_first_bias.reshape(ph_part)
    first_acts, first_slopes, sums = [], [], []
    for side in range(2):
        value, slope = silu_parts(product(feed[side], first_w) + my_first_bias)
        first_acts.append(value.astype(BF16))
        first_slopes.append(slope)
        sums.append(product(first_acts[side], second_w, BF16))
    second_act, second_slope = silu_parts(scatter_rows(*sums) + second_bias)
    second_low = second_act.astype(BF16)
    aligned = product(second_low, third_w) + third_bias

    target = dino_target.astype(F32)
    inv_z = lax.rsqrt(jnp.sum(aligned * aligned, axis=1, keepdims=True) + EPS_COS)
    inv_t = lax.rsqrt(jnp.sum(target * target, axis=1, keepdims=True) + EPS_COS)
    cosine = jnp.sum(aligned * target, axis=1, keepdims=True) * inv_z * inv_t
    grad_aligned = -LAMBDA_ALIGN * (target * inv_t - cosine * aligned * inv_z) * inv_z
    grad_aligned = grad_aligned.astype(BF16)

    grad_second = (product_nt(grad_aligned, third_w) * second_slope).astype(BF16)
    third_term = product_tn(second_low, grad_aligned, BF16)
    third_sum = lax.psum_scatter(third_term, "seq", scatter_dimension=1, tiled=True)
    grad_seconds = gather_rows(grad_second)
    grad_firsts, sums = [], []
    for side in range(2):
        grad = product_nt(grad_seconds[side], second_w) * first_slopes[side]
        grad_firsts.append(grad.astype(BF16))
        sums.append(product_nt(grad_firsts[side], first_w, BF16))
    second_term = product_tn(
        jnp.concatenate(first_acts, 0), jnp.concatenate(grad_seconds, 0), BF16
    )
    second_third_sum = reduce_img(
        jnp.concatenate(
            [second_term.reshape(img, ph_cell, ph), third_sum.reshape(img, ph_cell, zd)], axis=2
        )
    )
    grad_first = jnp.concatenate(grad_firsts, 0)
    first_term = product_tn(jnp.concatenate(feed, 0), grad_first, BF16)
    grad_result = out_cotangent.astype(F32) + scatter_rows(*sums)

    grad_branch_b = (gate_b * grad_result).astype(BF16)
    grad_branches = gather_rows(grad_branch_b)
    grad_pres, sums = [], []
    for side in range(2):
        grad = product_nt(grad_branches[side], down_w) * slopes[side]
        grad_pres.append(grad.astype(BF16))
        sums.append(product_nt(grad_pres[side], up_w, BF16))
    down_term = product_tn(jnp.concatenate(acts, 0), jnp.concatenate(grad_branches, 0), BF16)
    down_first_sum = reduce_img(
        jnp.concatenate(
            [down_term.reshape(img, ff_cell, width), first_term.reshape(img, feat, ph_part)],
            axis=2,
        )
    )
    grad_pre = jnp.concatenate(grad_pres, 0)
    up_term = product_tn(jnp.concatenate(hidden_b, 0), grad_pre, BF16)
    grad_hidden_b = scatter_rows(*sums)
    grad_after = grad_result + norm_back(normed_b, inverse_b, grad_hidden_b * (1.0 + scale_b))

    grad_branch_a = (gate_a * grad_after).astype(BF16)
    grad_attended = product_nt(grad_branch_a, attn_w, BF16)
    attn_term = product_tn(attended, grad_branch_a, BF16)
    attn_sum = lax.psum_scatter(attn_term, "seq", scatter_dimension=1, tiled=True)
    attn_up_sum = reduce_img(
        jnp.concatenate(
            [attn_sum.reshape(img, feat, part_width), up_term.reshape(img, feat, ff_part)], axis=2
        )
    )
    grad_parts = grad_attended.reshape(own_rows, SEQ, part_width).transpose(1, 0, 2)
    grad_heads = [pick(grad_parts, place)]
    grad_heads += [swap(pick(grad_parts, place ^ p), p) for p in range(1, SEQ)]
    grad_heads = pad_heads(jnp.concatenate(grad_heads, 0))
    grad_q, grad_k, grad_v = attend_backward(qkv, grad_heads, block_slots)
    grad_qkv = jnp.concatenate([grad_q, grad_k, grad_v], axis=1)
    grad_hidden_a = scatter_rows(
        product_nt(grad_qkv[: 2 * own_rows], qkv_w, BF16),
        product_nt(grad_qkv[2 * own_rows :], qkv_w, BF16),
    )
    qkv_term = strip_heads(product_tn(hidden_a, grad_qkv, BF16))
    qkv_sum = reduce_img(qkv_term.reshape(img, feat, 3 * part_width))
    normed_a, inverse_a = norm_parts(tokens_f)
    tokens_grad = grad_after + norm_back(normed_a, inverse_a, grad_hidden_a * (1.0 + scale_a))

    own_sums = jnp.concatenate(
        [
            column_sums(grad_hidden_a),
            column_sums(grad_hidden_a * normed_a),
            column_sums(grad_after * branch_a),
            column_sums(grad_hidden_b),
            column_sums(grad_hidden_b * normed_b),
            column_sums(grad_result * branch_b),
        ]
    )
    by_place = [
        own_sums.reshape(SEQ, mod_cols),
        column_sums(grad_branch_a).reshape(SEQ, part_width),
        column_sums(grad_branch_b).reshape(SEQ, part_width),
        column_sums(grad_second).reshape(SEQ, ph_part),
        column_sums(grad_aligned).reshape(SEQ, zd // SEQ),
    ]
    seq_got = seq_exchange(jnp.concatenate(by_place, axis=1))
    all_slots = jnp.stack([slot_ids[p * own_rows] for p in range(SEQ)])
    member = (all_slots[None, :] == jnp.arange(slot_count, dtype=jnp.int32)[:, None]).astype(F32)
    grad_mod = jnp.sum(member[:, :, None] * seq_got[None, :, :mod_cols], axis=1)
    grad_mod = grad_mod.astype(BF16).astype(F32)
    row_biases = jnp.sum(seq_got[:, mod_cols:], axis=0)
    qkv_bias_sums = strip_heads(column_sums(grad_qkv))
    bias_sums = jnp.concatenate(
        [
            row_biases,
            qkv_bias_sums[:part_width],
            qkv_bias_sums[2 * part_width :],
            column_sums(grad_pre),
            column_sums(grad_first),
        ]
    )
    mod_size = slot_count * mod_cols
    img_got = img_gather(jnp.concatenate([grad_mod.reshape(mod_size), bias_sums]))
    grad_mods = img_got[:, :mod_size].reshape(img * slot_count, mod_cols).astype(BF16)
    bias_sums = jnp.sum(img_got[:, mod_size:], axis=0)
    ada_weight_grad = product_tn(cond_cols, grad_mods)
    cond_parts = product_nt(grad_mods, ada_weight).reshape(img, slot_count, feat)
    cond_parts = img_exchange(cond_parts).transpose(1, 0, 2).reshape(slot_count * width)
    last = jnp.concatenate([column_sums(grad_mods), bias_sums, cond_parts])
    last = lax.all_gather(last, "seq", axis=0, tiled=False)
    sizes = [mod_cols, part_width, part_width, ph_part, zd // SEQ, part_width, part_width]
    sizes += [ff_part, ph_part, slot_count * width]
    cuts, start = [], 0
    for size in sizes:
        cuts.append(last[:, start : start + size])
        start += size
    ada_bias_grad, attn_bias_grad, down_bias_grad, second_bias_grad, third_bias_grad = (
        cut.reshape(-1) for cut in cuts[:5]
    )
    query_bias_grad, value_bias_grad = cuts[5].reshape(-1), cuts[6].reshape(-1)
    up_bias_grad = cuts[7].reshape(SEQ, img, ff_cell).transpose(1, 0, 2).reshape(ff)
    first_bias_grad = cuts[8].reshape(SEQ, img, ph_cell).transpose(1, 0, 2).reshape(ph)
    conditioning_grad = jnp.sum(cuts[9], axis=0).reshape(slot_count, width) * cond_slope

    third_proj_grad = second_third_sum[:, ph:].reshape(ph // img, zd // SEQ)
    second_back = second_third_sum[:, :ph].astype(BF16).reshape(ph_cell, SEQ, ph_part)
    second_back = seq_exchange(second_back.transpose(1, 0, 2))
    second_proj_grad = second_back.reshape(ph // img, ph_part).astype(F32)

    down_back = down_first_sum[:, :width].reshape(ff_cell, SEQ, part_width).transpose(1, 0, 2)
    first_back = down_first_sum[:, width:].reshape(feat, SEQ, ph_part // SEQ).transpose(1, 0, 2)
    down_first_back = seq_exchange(jnp.concatenate([down_back, first_back], axis=2).astype(BF16))
    down_weight_grad = down_first_back[:, :, :part_width].reshape(ff // img, part_width)
    down_weight_grad = down_weight_grad.astype(F32)

    def cells_in_order(parts, cell):
        rows = parts.shape[1]
        parts = parts.reshape(SEQ, rows, img // SEQ, cell).transpose(1, 2, 0, 3)
        return parts.reshape(rows, img * cell).astype(F32)

    first_proj_grad = cells_in_order(down_first_back[:, :, part_width:], ph_cell)
    attn_weight_grad = attn_up_sum[:, :part_width]
    up_back = attn_up_sum[:, part_width:].astype(BF16).reshape(feat, SEQ, part_width)
    up_weight_grad = cells_in_order(seq_exchange(up_back.transpose(1, 0, 2)), ff_cell)

    kinds = qkv_sum.astype(BF16).reshape(feat, 3, part_width).transpose(1, 0, 2)
    qkv_back = seq_exchange(
        jnp.stack(
            [
                pick(kinds, jnp.minimum((3 * d + (place - 3 * d) % SEQ) // SEQ, 2))
                for d in range(SEQ)
            ]
        )
    )
    qkv_weight_grad = jnp.concatenate(
        [pick(qkv_back, (3 * place + j) % SEQ) for j in range(3)], axis=1
    ).astype(F32)

    return (
        feed_low,
        tokens_grad,
        conditioning_grad,
        ada_weight_grad,
        qkv_weight_grad,
        attn_weight_grad,
        up_weight_grad,
        down_weight_grad,
        first_proj_grad,
        second_proj_grad,
        third_proj_grad,
        ada_bias_grad,
        query_bias_grad,
        value_bias_grad,
        attn_bias_grad,
        up_bias_grad,
        down_bias_grad,
        first_bias_grad,
        second_bias_grad,
        third_bias_grad,
    )


def solution(mesh):
    rows = P(("img", "seq"), None)
    both = P("img", "seq")
    return jax.shard_map(
        local,
        mesh=mesh,
        in_specs=(rows, P("img", None), P("img"), rows, rows) + (both,) * 8 + (P(),) * 9,
        out_specs=(rows, rows, P("img", None)) + (both,) * 8 + (P(),) * 9,
        check_vma=False,
    )
```

time: 3270 us -> 930 us (0.28)
  waiting for transfers between devices: 2790 us -> 390 us
  matrix products: 222 us -> 92.4 us
  starting transfers between devices: 30.9 us -> 116 us
  local copies, waits for them, and re-layouts: 82.8 us -> 152 us
  blocking collectives: 58.4 us -> 10.9 us
  other arithmetic: 54.3 us -> 97 us
  Pallas kernels: 0 us -> 34.3 us
    reduce_scatter x10 -> x2, waiting for transfers between devices: 1630 us -> 0.02 us  [the longest x1 0.02 us: local(): lax.psum_scatter(third_term, 'seq', scatter_dimension=1, tiled=True)]
    all_gather x12 -> x2, waiting for transfers between devices: 871 us -> 0.01 us  [the longest x1 0.01 us: local(): lax.all_gather(interleave(attn_up, 0, part_width), 'seq', axis=1, tiled=T...]
    ppermute x0 -> x44, waiting for transfers between devices: none -> 231 us  [the longest x36 137 us: swap(): return lax.ppermute(values, 'seq', [(i, i ^ distance) for i in range(SEQ)])]
    psum x1 -> x0, waiting for transfers between devices: 130 us -> none  [local(): lax.psum((ada_bias_term, query_bias_term, value_bias_term, attn_bias_term...]
    unnamed x33 -> x4, waiting for transfers between devices: 95.7 us -> 0.07 us
    all_to_all x8 -> x20, waiting for transfers between devices: 70.3 us -> 159 us  [the longest x4 66.5 us: reduce_img(): lax.all_to_all(joined, 'img', split_axis=0, concat_axis=0, tiled=True, ax...]
    dot_general x24 -> x12, matrix products: 106 us -> 33.1 us  [product(): lax.dot_general(left, right, (((1,), (0,)), ((), ())), preferred_element_...]
    all_to_all x8 -> x20, starting transfers between devices: 29 us -> 84.7 us  [the longest x8 29.8 us: seq_exchange(): return lax.all_to_all(parts, 'seq', split_axis=0, concat_axis=0, tiled=True)]
  transfers between devices with their start and end apart: 36 -> 68, of which waited for: 30 -> 36; matrix products, arithmetic and copies ran while one was open for 9% -> 34% of each run, Pallas kernels for 0% -> 4%
where the time goes in v1:
time: 930 us; the launch traced here: 917 us
  waiting for transfers between devices  390 us (42%)
  local copies, waits for them, and re-layouts  152 us (16%)
  starting transfers between devices  116 us (12%)
  other arithmetic  97 us (10%)
  matrix products  92.4 us (10%)
  Pallas kernels  34.3 us (4%)
  between operations  24.4 us (3%)
  blocking collectives  10.9 us (1%)
    ppermute x36, waiting for transfers between devices, swap(): return lax.ppermute(values, 'seq', [(i, i ^ distance) for i in range(SEQ)])  137 us
    ppermute x8, waiting for transfers between devices, img_swap(): return lax.ppermute(values, 'img', [(i, i ^ 1) for i in range(count)])  94.9 us
    all_to_all x4, waiting for transfers between devices, reduce_img(): lax.all_to_all(joined, 'img', split_axis=0, concat_axis=0, tiled=True, ax...  66.5 us
    all_to_all x4, waiting for transfers between devices, gather_img(): lax.all_to_all(copies, 'img', split_axis=0, concat_axis=0, tiled=True, ax...  38.6 us
    all_to_all x8, waiting for transfers between devices, seq_exchange(): return lax.all_to_all(parts, 'seq', split_axis=0, concat_axis=0, tiled=True)  36.5 us
    unnamed x276, local copies, waits for them, and re-layouts  35.3 us
    dot_general x12, matrix products, product(): lax.dot_general(left, right, (((1,), (0,)), ((), ())), preferred_element_...  33.1 us
    dot_general x8, matrix products, product_tn(): lax.dot_general(left, right, (((0,), (0,)), ((), ())), preferred_element_...  31.7 us
  transfers between devices with their start and end apart: 68, of which 36 were waited for; matrix products, arithmetic and copies ran while one was open for 34% of the time, Pallas kernels for 4%

profile of v1, /device:TPU:0, one launch (start us, length us, event | category | flops | bytes accessed | tf_op | source)
XLA Modules:
  0.0 917.2 jit_solution(7065516817600125292)
XLA Ops:
  8.7 7.3 all-to-all-start
  48.0 11.8 %all-to-all-done.4 = bf16[4,144,704]{2,1,0:T(8,128)(2,1)S(1)} async-done(((bf16[4,144,704]{2,1,0:T(8,128)(2,1)}), bf16[4,144,704]{2,1,0:T(8,128)(2,1)S(1)}, u32[]{:S(2)}, u32[]{:S(2)}) %all-to-all-start.4) | async-done | bytes 811040 | tf_op jit(solution)/shard_map/all_to_all | solution.py:136
  79.3 37.1 %all-to-all-done.5 = bf16[4,144,1440]{2,1,0:T(8,128)(2,1)S(1)} async-done(((bf16[4,144,1440]{2,1,0:T(8,128)(2,1)}), bf16[4,144,1440]{2,1,0:T(8,128)(2,1)S(1)}, u32[]{:S(2)}, u32[]{:S(2)}) %all-to-all-start.5) | async-done | bytes 1658912 | tf_op jit(solution)/shard_map/all_to_all | solution.py:105
  164.1 20.5 %collective-permute-done.7 = bf16[4,144,1440]{2,1,0:T(8,128)(2,1)} collective-permute-done((bf16[4,144,1440]{2,1,0:T(8,128)(2,1)S(1)}, bf16[4,144,1440]{2,1,0:T(8,128)(2,1)}, u32[]{:S(2)}, u32[]{:S(2)}) %collective-permute-start.7) | collective-permute-done | bytes 1658912 | tf_op jit(solution)/shard_map/ppermute | solution.py:93
  223.4 8.7 reshape_reshape.7
  240.1 13.4 %attend.1 = bf16[1024,512]{1,0:T(8,128)(2,1)} custom-call(s32[4]{0:T(128)} %pad_add_fusion.slots, bf16[1024,1536]{1,0:T(8,128)(2,1)} %add_convert_fusion.q_ref.k_ref.v_ref, bf16[1024,1536]{1,0:T(8,128)(2,1)} %add_convert_fusion.q_ref.k_ref.v_ref, bf16[1024,1536]{1,0:T(8,128)(2,1)} %add_convert_fusion.q_ref.k_ref.v_ref), custom_call_target="tpu_custom_call" | custom-call | tf_op jit(solution)/shard_map/attend/pallas_call | solution.py:234
  274.4 11.2 %collective-permute-done.11 = bf16[256,1152]{1,0:T(8,128)(2,1)S(1)} collective-permute-done((bf16[256,1152]{1,0:T(8,128)(2,1)S(1)}, bf16[256,1152]{1,0:T(8,128)(2,1)S(1)}, u32[]{:S(2)}, u32[]{:S(2)}) %collective-permute-start.11) | collective-permute-done | bytes 589856 | tf_op jit(solution)/shard_map/ppermute | solution.py:73
  285.6 47.6 %collective-permute-done.9 = bf16[4,144,1664]{2,1,0:T(8,128)(2,1)} collective-permute-done((bf16[4,144,1664]{2,1,0:T(8,128)(2,1)}, bf16[4,144,1664]{2,1,0:T(8,128)(2,1)}, u32[]{:S(2)}, u32[]{:S(2)}) %collective-permute-start.9) | collective-permute-done | bytes 1916960 | tf_op jit(solution)/shard_map/ppermute | solution.py:93
  356.6 9.3 %collective-permute-done.14 = bf16[256,1152]{1,0:T(8,128)(2,1)} collective-permute-done((bf16[256,1152]{1,0:T(8,128)(2,1)}, bf16[256,1152]{1,0:T(8,128)(2,1)}, u32[]{:S(2)}, u32[]{:S(2)}) %collective-permute-start.14) | collective-permute-done | bytes 589856 | tf_op jit(solution)/shard_map/ppermute | solution.py:73
  370.6 25.6 %collective-permute-done.18 = bf16[256,1152]{1,0:T(8,128)(2,1)} collective-permute-done((bf16[256,1152]{1,0:T(8,128)(2,1)S(1)}, bf16[256,1152]{1,0:T(8,128)(2,1)}, u32[]{:S(2)}, u32[]{:S(2)}) %collective-permute-start.18) | collective-permute-done | bytes 589856 | tf_op jit(solution)/shard_map/ppermute | solution.py:73
  412.0 24.2 %collective-permute-done.21 = bf16[256,2048]{1,0:T(8,128)(2,1)} collective-permute-done((bf16[256,2048]{1,0:T(8,128)(2,1)}, bf16[256,2048]{1,0:T(8,128)(2,1)}, u32[]{:S(2)}, u32[]{:S(2)}) %collective-permute-start.21) | collective-permute-done | bytes 1048608 | tf_op jit(solution)/shard_map/ppermute | solution.py:73
  445.6 23.3 %collective-permute-done.24 = bf16[256,2048]{1,0:T(8,128)(2,1)S(1)} collective-permute-done((bf16[256,2048]{1,0:T(8,128)(2,1)S(1)}, bf16[256,2048]{1,0:T(8,128)(2,1)S(1)}, u32[]{:S(2)}, u32[]{:S(2)}) %collective-permute-start.24) | collective-permute-done | bytes 1048608 | tf_op jit(solution)/shard_map/ppermute | solution.py:73
  481.4 12.0 %collective-permute-done.27 = bf16[256,1152]{1,0:T(8,128)(2,1)S(1)} collective-permute-done((bf16[256,1152]{1,0:T(8,128)(2,1)S(1)}, bf16[256,1152]{1,0:T(8,128)(2,1)S(1)}, u32[]{:S(2)}, u32[]{:S(2)}) %collective-permute-start.27) | collective-permute-done | bytes 589856 | tf_op jit(solution)/shard_map/ppermute | solution.py:73
  501.0 8.7 collective-permute-done.30
  540.7 11.0 %collective-permute-done.33 = bf16[256,1152]{1,0:T(8,128)(2,1)S(1)} collective-permute-done((bf16[256,1152]{1,0:T(8,128)(2,1)S(1)}, bf16[256,1152]{1,0:T(8,128)(2,1)S(1)}, u32[]{:S(2)}, u32[]{:S(2)}) %collective-permute-start.33) | collective-permute-done | bytes 589856 | tf_op jit(solution)/shard_map/ppermute | solution.py:73
  568.3 20.9 %attend_back.1 = (bf16[1024,512]{1,0:T(8,128)(2,1)}, bf16[1024,512]{1,0:T(8,128)(2,1)}, bf16[1024,512]{1,0:T(8,128)(2,1)}) custom-call(s32[4]{0:T(128)} %pad_add_fusion.slots, bf16[1024,1536]{1,0:T(8,128)(2,1)} %add_convert_fusion.q_ref.k_ref.v_ref, bf16[1024,1536]{1,0:T(8,128)(2,1)} %add_convert_fusion.q_ref.k_ref.v_ref, ...), custom_call_target="tpu_custom_call" | custom-call | tf_op jit(solution)/shard_map/attend_back/pallas_call | solution.py:250
  620.7 8.8 fusion.169
  629.6 8.0 copy.438
  637.5 8.3 copy.437
  688.9 20.5 %all-to-all-done.12 = bf16[4,144,864]{2,1,0:T(8,128)(2,1)} async-done(((bf16[4,144,864]{2,1,0:T(8,128)(2,1)}), bf16[4,144,864]{2,1,0:T(8,128)(2,1)}, u32[]{:S(2)}, u32[]{:S(2)}) %all-to-all-start.12) | async-done | bytes 995360 | tf_op jit(solution)/shard_map/all_to_all | solution.py:129
  740.0 17.8 %all-to-all-done.16 = bf16[4,144,1664]{2,1,0:T(8,128)(2,1)} async-done(((bf16[4,144,1664]{2,1,0:T(8,128)(2,1)}), bf16[4,144,1664]{2,1,0:T(8,128)(2,1)}, u32[]{:S(2)}, u32[]{:S(2)}) %all-to-all-start.16) | async-done | bytes 1916960 | tf_op jit(solution)/shard_map/all_to_all | solution.py:129
  805.8 18.6 %collective-permute-done.41 = bf16[4,144,1440]{2,1,0:T(8,128)(2,1)} collective-permute-done((bf16[4,144,1440]{2,1,0:T(8,128)(2,1)}, bf16[4,144,1440]{2,1,0:T(8,128)(2,1)}, u32[]{:S(2)}, u32[]{:S(2)}) %collective-permute-start.41) | collective-permute-done | bytes 1658912 | tf_op jit(solution)/shard_map/ppermute | solution.py:93
  828.8 11.1 %all-to-all-done.18 = bf16[4,64,2816]{2,1,0:T(8,128)(2,1)} async-done(((bf16[4,64,2816]{2,1,0:T(8,128)(2,1)}), bf16[4,64,2816]{2,1,0:T(8,128)(2,1)}, u32[]{:S(2)}, u32[]{:S(2)}) %all-to-all-start.18) | async-done | bytes 1441824 | tf_op jit(solution)/shard_map/all_to_all | solution.py:129
  867.1 17.0 %all-to-all-done.14 = bf16[4,144,1440]{2,1,0:T(8,128)(2,1)S(1)} async-done(((bf16[4,144,1440]{2,1,0:T(8,128)(2,1)}), bf16[4,144,1440]{2,1,0:T(8,128)(2,1)S(1)}, u32[]{:S(2)}, u32[]{:S(2)}) %all-to-all-start.14) | async-done | bytes 1658912 | tf_op jit(solution)/shard_map/all_to_all | solution.py:129
  (661 shorter events, 490.2 us)
Async XLA Ops:
  72.9 43.4 %all-to-all-start.5 = ((bf16[4,144,1440]{2,1,0:T(8,128)(2,1)}), bf16[4,144,1440]{2,1,0:T(8,128)(2,1)S(1)}, u32[]{:S(2)}, u32[]{:S(2)}) async-start(bf16[4,144,1440]{2,1,0:T(8,128)(2,1)} %broadcast_in_dim.44), calls=%async_computation.5 | async-start | bytes 3538944 | tf_op jit(solution)/shard_map/all_to_all | solution.py:105
  76.7 86.0 %collective-permute-start.1 = (bf16[256,1152]{1,0:T(8,128)(2,1)S(1)}, bf16[256,1152]{1,0:T(8,128)(2,1)S(1)}, u32[]{:S(2)}, u32[]{:S(2)}) collective-permute-start(bf16[256,1152]{1,0:T(8,128)(2,1)S(1)} %copy-done.1), channel_id=1, source_target_pairs={{0,2},{1,3},{2,0},{3,1},{4,6},{5,7},{6,4},{7,5},{8,10},{9,11},{10,... | collective-permute-start | bytes 1769480 | tf_op jit(solution)/shard_map/ppermute | solution.py:73
  77.4 85.5 %collective-permute-start = (bf16[256,1152]{1,0:T(8,128)(2,1)S(1)}, bf16[256,1152]{1,0:T(8,128)(2,1)}, u32[]{:S(2)}, u32[]{:S(2)}) collective-permute-start(bf16[256,1152]{1,0:T(8,128)(2,1)S(1)} %copy-done.1), channel_id=1, source_target_pairs={{0,1},{1,0},{2,3},{3,2},{4,5},{5,4},{6,7},{7,6},{8,9},{9,8},{10,11... | collective-permute-start | bytes 1769480 | tf_op jit(solution)/shard_map/ppermute | solution.py:73
  118.6 35.6 %all-to-all-start.3 = ((bf16[4,144,864]{2,1,0:T(8,128)(2,1)}), bf16[4,144,864]{2,1,0:T(8,128)(2,1)}, u32[]{:S(2)}, u32[]{:S(2)}) async-start(bf16[4,144,864]{2,1,0:T(8,128)(2,1)} %broadcast_in_dim.40), calls=%async_computation.3 | async-start | bytes 2064384 | tf_op jit(solution)/shard_map/all_to_all | solution.py:105
  144.9 39.7 %collective-permute-start.7 = (bf16[4,144,1440]{2,1,0:T(8,128)(2,1)S(1)}, bf16[4,144,1440]{2,1,0:T(8,128)(2,1)}, u32[]{:S(2)}, u32[]{:S(2)}) collective-permute-start(bf16[4,144,1440]{2,1,0:T(8,128)(2,1)S(1)} %all-to-all-done.5), channel_id=1, source_target_pairs={{0,4},{4,0},{8,12},{12,8},{16,20},{20,16},{24,28},{28,24},{1,5},{5... | collective-permute-start | bytes 4976648 | tf_op jit(solution)/shard_map/ppermute | solution.py:93
  156.4 39.8 %all-to-all-start.8 = ((bf16[4,64,2816]{2,1,0:T(8,128)(2,1)}), bf16[4,64,2816]{2,1,0:T(8,128)(2,1)}, u32[]{:S(2)}, u32[]{:S(2)}) async-start(bf16[4,64,2816]{2,1,0:T(8,128)(2,1)} %broadcast_in_dim.54), calls=%async_computation.8 | async-start | bytes 2883584 | tf_op jit(solution)/shard_map/all_to_all | solution.py:105
  161.4 103.6 %all-gather.6.cloned.1.call-start = ((), (), s32[]{:S(2)}) async-start(), calls=%async_computation.22 | async-start | bytes 3317760 | tf_op jit(solution)/shard_map/all_gather | solution.py:371
  162.7 39.6 %collective-permute-start.2 = (bf16[256,1152]{1,0:T(8,128)(2,1)S(1)}, bf16[256,1152]{1,0:T(8,128)(2,1)}, u32[]{:S(2)}, u32[]{:S(2)}) collective-permute-start(bf16[256,1152]{1,0:T(8,128)(2,1)S(1)} %collective-permute-done.1), channel_id=1, source_target_pairs={{0,1},{1,0},{2,3},{3,2},{4,5},{5,4},{6,7},{7,6},{8,9},{9,8},{10,11... | collective-permute-start | bytes 1769480 | tf_op jit(solution)/shard_map/ppermute | solution.py:73
  197.6 66.5 %all-to-all-start.6 = ((bf16[4,144,1664]{2,1,0:T(8,128)(2,1)}), bf16[4,144,1664]{2,1,0:T(8,128)(2,1)}, u32[]{:S(2)}, u32[]{:S(2)}) async-start(bf16[4,144,1664]{2,1,0:T(8,128)(2,1)} %broadcast_in_dim.49), calls=%async_computation.6 | async-start | bytes 3833856 | tf_op jit(solution)/shard_map/all_to_all | solution.py:105
  202.0 209.7 %all-gather.8.cloned.1.call-start = ((), (), s32[]{:S(2)}) async-start(), calls=%async_computation.23 | async-start | bytes 3932160 | tf_op jit(solution)/shard_map/all_gather | solution.py:379
  258.3 92.5 %collective-permute-start.16 = (bf16[4,64,2816]{2,1,0:T(8,128)(2,1)}, bf16[4,64,2816]{2,1,0:T(8,128)(2,1)}, u32[]{:S(2)}, u32[]{:S(2)}) collective-permute-start(bf16[4,64,2816]{2,1,0:T(8,128)(2,1)} %all-to-all-done.8), channel_id=1, source_target_pairs={{0,4},{4,0},{8,12},{12,8},{16,20},{20,16},{24,28},{28,24},{1,5},{5... | collective-permute-start | bytes 4325384 | tf_op jit(solution)/shard_map/ppermute | solution.py:93
  264.1 69.1 %collective-permute-start.9 = (bf16[4,144,1664]{2,1,0:T(8,128)(2,1)}, bf16[4,144,1664]{2,1,0:T(8,128)(2,1)}, u32[]{:S(2)}, u32[]{:S(2)}) collective-permute-start(bf16[4,144,1664]{2,1,0:T(8,128)(2,1)} %all-to-all-done.6), channel_id=1, source_target_pairs={{0,4},{4,0},{8,12},{12,8},{16,20},{20,16},{24,28},{28,24},{1,5},{5... | collective-permute-start | bytes 5750792 | tf_op jit(solution)/shard_map/ppermute | solution.py:93
  285.6 50.2 %collective-permute-start.12 = (bf16[256,1152]{1,0:T(8,128)(2,1)S(1)}, bf16[256,1152]{1,0:T(8,128)(2,1)S(1)}, u32[]{:S(2)}, u32[]{:S(2)}) collective-permute-start(bf16[256,1152]{1,0:T(8,128)(2,1)S(1)} %collective-permute-done.11), channel_id=1, source_target_pairs={{0,1},{1,0},{2,3},{3,2},{4,5},{5,4},{6,7},{7,6},{8,9},{9,8},{10,11... | collective-permute-start | bytes 1769480 | tf_op jit(solution)/shard_map/ppermute | solution.py:73
  356.4 362.4 %reduce-scatter.5.cloned.1.call-start = ((), (), s32[]{:S(2)}) async-start(), calls=%async_computation.25 | async-start | bytes 3932160 | tf_op jit(solution)/shard_map/reduce_scatter | solution.py:422
  367.5 28.6 %collective-permute-start.18 = (bf16[256,1152]{1,0:T(8,128)(2,1)S(1)}, bf16[256,1152]{1,0:T(8,128)(2,1)}, u32[]{:S(2)}, u32[]{:S(2)}) collective-permute-start(bf16[256,1152]{1,0:T(8,128)(2,1)S(1)} %add_convert_fusion.5), channel_id=1, source_target_pairs={{0,2},{1,3},{2,0},{3,1},{4,6},{5,7},{6,4},{7,5},{8,10},{9,11},{10,... | collective-permute-start | bytes 1769480 | tf_op jit(solution)/shard_map/ppermute | solution.py:73
  501.0 271.5 %reduce-scatter.3.cloned.1.call-start = ((), (), s32[]{:S(2)}) async-start(), calls=%async_computation.24 | async-start | bytes 3317760 | tf_op jit(solution)/shard_map/reduce_scatter | solution.py:463
  538.6 147.2 %collective-permute-start.42 = (bf16[4,144,1664]{2,1,0:T(8,128)(2,1)}, bf16[4,144,1664]{2,1,0:T(8,128)(2,1)}, u32[]{:S(2)}, u32[]{:S(2)}) collective-permute-start(bf16[4,144,1664]{2,1,0:T(8,128)(2,1)} %fusion.78), channel_id=1, source_target_pairs={{0,4},{4,0},{8,12},{12,8},{16,20},{20,16},{24,28},{28,24},{1,5},{5... | collective-permute-start | bytes 5750792 | tf_op jit(solution)/shard_map/ppermute | solution.py:93
  599.5 51.8 %collective-permute-start.37 = (bf16[256,1152]{1,0:T(8,128)(2,1)}, bf16[256,1152]{1,0:T(8,128)(2,1)S(1)}, u32[]{:S(2)}, u32[]{:S(2)}) collective-permute-start(bf16[256,1152]{1,0:T(8,128)(2,1)} %slice.409), channel_id=1, source_target_pairs={{0,1},{1,0},{2,3},{3,2},{4,5},{5,4},{6,7},{7,6},{8,9},{9,8},{10,11... | collective-permute-start | bytes 1769480 | tf_op jit(solution)/shard_map/ppermute | solution.py:73
  620.6 30.7 %collective-permute-start.39 = (bf16[256,1152]{1,0:T(8,128)(2,1)}, bf16[256,1152]{1,0:T(8,128)(2,1)}, u32[]{:S(2)}, u32[]{:S(2)}) collective-permute-start(bf16[256,1152]{1,0:T(8,128)(2,1)} %add_convert_fusion.2), channel_id=1, source_target_pairs={{0,2},{1,3},{2,0},{3,1},{4,6},{5,7},{6,4},{7,5},{8,10},{9,11},{10,... | collective-permute-start | bytes 1769480 | tf_op jit(solution)/shard_map/ppermute | solution.py:73
  709.5 48.4 %all-to-all-start.16 = ((bf16[4,144,1664]{2,1,0:T(8,128)(2,1)}), bf16[4,144,1664]{2,1,0:T(8,128)(2,1)}, u32[]{:S(2)}, u32[]{:S(2)}) async-start(bf16[4,144,1664]{2,1,0:T(8,128)(2,1)} %fusion.8), calls=%async_computation.17 | async-start | bytes 3833856 | tf_op jit(solution)/shard_map/all_to_all | solution.py:129
  725.3 65.9 %collective-permute-start.43 = (bf16[4,64,2816]{2,1,0:T(8,128)(2,1)}, bf16[4,64,2816]{2,1,0:T(8,128)(2,1)}, u32[]{:S(2)}, u32[]{:S(2)}) collective-permute-start(bf16[4,64,2816]{2,1,0:T(8,128)(2,1)} %fusion.86), channel_id=1, source_target_pairs={{0,4},{4,0},{8,12},{12,8},{16,20},{20,16},{24,28},{28,24},{1,5},{5... | collective-permute-start | bytes 4325384 | tf_op jit(solution)/shard_map/ppermute | solution.py:93
  782.9 41.6 %collective-permute-start.41 = (bf16[4,144,1440]{2,1,0:T(8,128)(2,1)}, bf16[4,144,1440]{2,1,0:T(8,128)(2,1)}, u32[]{:S(2)}, u32[]{:S(2)}) collective-permute-start(bf16[4,144,1440]{2,1,0:T(8,128)(2,1)} %fusion.81), channel_id=1, source_target_pairs={{0,4},{4,0},{8,12},{12,8},{16,20},{20,16},{24,28},{28,24},{1,5},{5... | collective-permute-start | bytes 4976648 | tf_op jit(solution)/shard_map/ppermute | solution.py:93
  800.7 39.2 %all-to-all-start.18 = ((bf16[4,64,2816]{2,1,0:T(8,128)(2,1)}), bf16[4,64,2816]{2,1,0:T(8,128)(2,1)}, u32[]{:S(2)}, u32[]{:S(2)}) async-start(bf16[4,64,2816]{2,1,0:T(8,128)(2,1)} %fusion.15), calls=%async_computation.20 | async-start | bytes 2883584 | tf_op jit(solution)/shard_map/all_to_all | solution.py:129
  839.9 44.2 %all-to-all-start.14 = ((bf16[4,144,1440]{2,1,0:T(8,128)(2,1)}), bf16[4,144,1440]{2,1,0:T(8,128)(2,1)S(1)}, u32[]{:S(2)}, u32[]{:S(2)}) async-start(bf16[4,144,1440]{2,1,0:T(8,128)(2,1)} %fusion.9), calls=%async_computation.15 | async-start | bytes 3538944 | tf_op jit(solution)/shard_map/all_to_all | solution.py:129
  (170 other events, 1827.9 us)
Sparse Core Ops, SparseCore 0:
  187.3 25.9 all-gather.5
  356.5 41.8 all-gather.7
  501.1 45.0 reduce-scatter.4
  562.1 34.8 reduce-scatter.2

commit v2 on v1

v2 whole, which is shorter than its diff:
```python
import jax
import jax.numpy as jnp
from jax import lax
from jax.experimental import pallas as pl
from jax.experimental.layout import Layout, with_layout_constraint
from jax.experimental.pallas import tpu as pltpu
from jax.sharding import PartitionSpec as P

H = 16
HD = 72
EPS_NORM = 1e-06
EPS_COS = 1e-06
LAMBDA_ALIGN = 0.5
MASKED_SCORE = -1e30
F32 = jnp.float32
BF16 = jnp.bfloat16
SEQ = 4


def product(left, right, out=F32):
    return lax.dot_general(
        left, right, (((1,), (0,)), ((), ())), preferred_element_type=F32
    ).astype(out)


def product_tn(left, right, out=F32):
    return lax.dot_general(
        left, right, (((0,), (0,)), ((), ())), preferred_element_type=F32
    ).astype(out)


def product_nt(left, right, out=F32):
    return lax.dot_general(
        left, right, (((1,), (1,)), ((), ())), preferred_element_type=F32
    ).astype(out)


def column_sums(values):
    return jnp.sum(values.astype(F32), axis=0)


def norm_parts(values):
    centered = values - jnp.mean(values, axis=-1, keepdims=True)
    inverse = lax.rsqrt(jnp.mean(centered * centered, axis=-1, keepdims=True) + EPS_NORM)
    return centered * inverse, inverse


def norm_back(normed, inverse, grad):
    return inverse * (
        grad
        - jnp.mean(grad, axis=-1, keepdims=True)
        - normed * jnp.mean(grad * normed, axis=-1, keepdims=True)
    )


def silu_parts(values):
    gate = 1.0 / (1.0 + jnp.exp(-values))
    return values * gate, gate * (1.0 + values * (1.0 - gate))


GELU_C = 0.7978845608028654


def gelu_parts(values):
    inner = GELU_C * (values + 0.044715 * values * values * values)
    bent = jnp.tanh(inner)
    slope = GELU_C * (1.0 + 3.0 * 0.044715 * values * values)
    value = 0.5 * values * (1.0 + bent)
    return value, 0.5 * (1.0 + bent) + 0.5 * values * (1.0 - bent * bent) * slope


def swap(values, distance):
    return lax.ppermute(values, "seq", [(i, i ^ distance) for i in range(SEQ)])


def gather_rows(own):
    across = swap(own, 2)
    near = swap(own, 1)
    far = swap(across, 1)
    return jnp.concatenate([own, near], 0), jnp.concatenate([across, far], 0)


def scatter_blocks(blocks):
    from_far = swap(blocks[3], 1)
    across = swap((blocks[2].astype(F32) + from_far.astype(F32)).astype(BF16), 2)
    from_near = swap(blocks[1], 1)
    return blocks[0].astype(F32) + from_near.astype(F32) + across.astype(F32)


def scatter_rows(near, far):
    rows = near.shape[0] // 2
    from_far = swap(far[rows:], 1)
    across = swap((far[:rows].astype(F32) + from_far.astype(F32)).astype(BF16), 2)
    from_near = swap(near[rows:], 1)
    return near[:rows].astype(F32) + from_near.astype(F32) + across.astype(F32)


def tie(value, *after):
    return lax.optimization_barrier((value,) + after)[0]


def img_swap(values):
    count = lax.axis_size("img")
    return lax.ppermute(values, "img", [(i, i ^ 1) for i in range(count)])


def slow_swap(values, distance):
    count = lax.axis_size("img")
    return lax.ppermute(values, "img", [(i, i ^ (2 * distance)) for i in range(count)])


def slow_groups():
    half = lax.axis_size("img") // 2
    return [[2 * k + fast for k in range(half)] for fast in range(2)]


def arrange(body, shapes, *arrays, place=None):
    outs = tuple(jax.ShapeDtypeStruct(shape, kind) for shape, kind in shapes)
    count = len(arrays)

    def kernel(where, *refs):
        body(where, refs[:count], refs[count:])

    whole = lambda array: pl.BlockSpec(array.shape, lambda step, where: (0,) * len(array.shape))
    where = jnp.zeros((1,), jnp.int32) if place is None else jnp.reshape(place, (-1,))
    return pl.pallas_call(
        kernel,
        grid_spec=pltpu.PrefetchScalarGridSpec(
            num_scalar_prefetch=1,
            grid=(1,),
            in_specs=[whole(array) for array in arrays],
            out_specs=tuple(whole(out) for out in outs),
        ),
        out_shape=outs,
        name="arrange",
    )(where.astype(jnp.int32), *arrays)


def join_columns(blocks, place=None):
    lead, cols = blocks[0].shape[:-1], blocks[0].shape[-1]

    def body(where, ins, outs):
        for turn in range(1 if place is None else SEQ):

            def put():
                for p, block in enumerate(ins):
                    at = (turn ^ p) * cols
                    outs[0][..., at : at + cols] = block[...]

            if place is None:
                put()
            else:
                pl.when(where[0] == turn)(put)

    return arrange(body, [(lead + (SEQ * cols,), blocks[0].dtype)], *blocks, place=place)[0]


def split_columns(values, place):
    rows, cols = values.shape[0], values.shape[1] // SEQ

    def body(where, ins, outs):
        for turn in range(SEQ):

            def put():
                for p in range(SEQ):
                    at = (turn ^ p) * cols
                    outs[p][...] = ins[0][:, at : at + cols]

            pl.when(where[0] == turn)(put)

    return arrange(body, [((rows, cols), values.dtype)] * SEQ, values, place=place)


def spread_img(shard):
    count = lax.axis_size("img")
    here = lax.axis_index("img")
    if count > 8:
        full = lax.all_gather(shard, "img", axis=0, tiled=False)
        return [full[k] for k in range(count)], jnp.arange(count, dtype=jnp.int32)
    blocks = []
    for k in range(count // 2):
        block = slow_swap(shard, k) if k else shard
        blocks += [block, img_swap(block)]
    return blocks, here ^ jnp.arange(count, dtype=jnp.int32)


def open_spread(body, shapes, blocks, where):
    def each(place, ins, outs):
        for k, block in enumerate(ins):
            body(block, *(out.at[place[k]] for out in outs))

    stacked = [((len(blocks),) + shape, BF16) for shape in shapes]
    return arrange(each, stacked, *blocks, place=where)


def open_blocks(body, shapes, stacked):
    count = stacked.shape[0]
    spec = lambda shape: pl.BlockSpec((1,) + shape, lambda i: (i,) + (0,) * len(shape))
    return pl.pallas_call(
        lambda ref, *outs: body(ref.at[0], *(out.at[0] for out in outs)),
        grid=(count,),
        in_specs=[spec(stacked.shape[1:])],
        out_specs=tuple(spec(shape) for shape in shapes),
        out_shape=tuple(jax.ShapeDtypeStruct((count,) + shape, BF16) for shape in shapes),
        name="open_blocks",
    )(stacked)


def reduce_pair(term, *after):
    count = lax.axis_size("img")
    rows = term.shape[0] // count
    fast = lax.axis_index("img") % 2
    pairs = term.reshape(count // 2, 2, rows, term.shape[1])
    send = lax.dynamic_index_in_dim(pairs, 1 - fast, 1, keepdims=False)
    keep = lax.dynamic_index_in_dim(pairs, fast, 1, keepdims=False)
    got = tie(img_swap(send), *after) if after else img_swap(send)
    return (keep.astype(F32) + got.astype(F32)).astype(BF16)


def slow_exchange(parts):
    return lax.all_to_all(
        parts, "img", split_axis=0, concat_axis=0, tiled=True, axis_index_groups=slow_groups()
    )


def block_sum(parts):
    return jnp.sum(parts.astype(F32), axis=0)


def slow_scatter(parts, *after):
    half = parts.shape[0]
    here = lax.axis_index("img") // 2
    if half > 4:
        return block_sum(slow_exchange(parts))
    got = [tie(slow_swap(pick(parts, here ^ k), k), *after) for k in range(1, half)]
    return sum((part.astype(F32) for part in got), pick(parts, here).astype(F32))


def seq_exchange(parts):
    return lax.all_to_all(parts, "seq", split_axis=0, concat_axis=0, tiled=True)


def img_exchange(parts):
    return lax.all_to_all(parts, "img", split_axis=0, concat_axis=0, tiled=True)


def img_gather(values):
    count = lax.axis_size("img")
    return img_exchange(jnp.broadcast_to(values[None], (count,) + values.shape))


def pick(stacked, index):
    return lax.dynamic_index_in_dim(stacked, index, 0, keepdims=False)


def block_probs(slots, block, queries, keys):
    rows = queries.shape[0]
    scores = lax.dot_general(queries, keys, (((1,), (1,)), ((), ())), preferred_element_type=F32)
    pieces = []
    for other in range(SEQ):
        piece = scores[:, other * rows : (other + 1) * rows] * HD ** (-0.5)
        pieces.append(jnp.where(slots[block] == slots[other], piece, MASKED_SCORE))
    scores = jnp.concatenate(pieces, axis=1)
    raised = jnp.exp(scores - jnp.max(scores, axis=1, keepdims=True))
    return raised * (1.0 / jnp.sum(raised, axis=1, keepdims=True))


def attend_kernel(slots, qkv_ref, out_ref):
    block = pl.program_id(0)
    rows, width = out_ref.shape
    first = pl.multiple_of(block * rows, rows)
    for start in range(0, width, HD):
        queries = qkv_ref[pl.ds(first, rows), start : start + HD]
        keys = qkv_ref[:, width + start : width + start + HD]
        values = qkv_ref[:, 2 * width + start : 2 * width + start + HD]
        probs = block_probs(slots, block, queries, keys)
        out_ref[:, start : start + HD] = jnp.dot(
            probs.astype(BF16), values, preferred_element_type=F32
        ).astype(BF16)


def attend_back_kernel(slots, qkv_ref, g_ref, out_ref, gk_sum, gv_sum):
    block = pl.program_id(0)
    rows, width = g_ref.shape
    scale = HD ** (-0.5)
    first = pl.multiple_of(block * rows, rows)

    @pl.when(block == 0)
    def _():
        gk_sum[...] = jnp.zeros_like(gk_sum)
        gv_sum[...] = jnp.zeros_like(gv_sum)

    for head in range(width // HD):
        start = head * HD
        queries = qkv_ref[pl.ds(first, rows), start : start + HD]
        keys = qkv_ref[:, width + start : width + start + HD]
        values = qkv_ref[:, 2 * width + start : 2 * width + start + HD]
        grads = g_ref[:, start : start + HD]
        probs = block_probs(slots, block, queries, keys)
        grad_probs = lax.dot_general(
            grads, values, (((1,), (1,)), ((), ())), preferred_element_type=F32
        )
        delta = jnp.sum(probs * grad_probs, axis=1, keepdims=True)
        grad_scores = (probs * (grad_probs - delta)).astype(BF16)
        out_ref[pl.ds(first, rows), start : start + HD] = (
            jnp.dot(grad_scores, keys, preferred_element_type=F32) * scale
        ).astype(BF16)
        gk_sum[head] += lax.dot_general(
            grad_scores, queries, (((0,), (0,)), ((), ())), preferred_element_type=F32
        )
        gv_sum[head] += lax.dot_general(
            probs.astype(BF16), grads, (((0,), (0,)), ((), ())), preferred_element_type=F32
        )

    @pl.when(block == SEQ - 1)
    def _():
        for head in range(width // HD):
            start = head * HD
            out_ref[:, width + start : width + start + HD] = (gk_sum[head] * scale).astype(BF16)
            out_ref[:, 2 * width + start : 2 * width + start + HD] = gv_sum[head].astype(BF16)


def attend_forward(qkv, slots):
    rows, width = qkv.shape[0], qkv.shape[1] // 3
    return pl.pallas_call(
        attend_kernel,
        grid_spec=pltpu.PrefetchScalarGridSpec(
            num_scalar_prefetch=1,
            grid=(SEQ,),
            in_specs=[pl.BlockSpec((rows, 3 * width), lambda block, slots: (0, 0))],
            out_specs=pl.BlockSpec((rows // SEQ, width), lambda block, slots: (block, 0)),
        ),
        out_shape=jax.ShapeDtypeStruct((rows, width), BF16),
        cost_estimate=pl.CostEstimate(
            flops=8 * rows * rows * width, bytes_accessed=8 * rows * width, transcendentals=rows * rows
        ),
        name="attend",
    )(slots, qkv)


def attend_backward(qkv, grads, slots):
    rows, width = grads.shape
    return pl.pallas_call(
        attend_back_kernel,
        grid_spec=pltpu.PrefetchScalarGridSpec(
            num_scalar_prefetch=1,
            grid=(SEQ,),
            in_specs=[
                pl.BlockSpec((rows, 3 * width), lambda block, slots: (0, 0)),
                pl.BlockSpec((rows // SEQ, width), lambda block, slots: (block, 0)),
            ],
            out_specs=pl.BlockSpec((rows, 3 * width), lambda block, slots: (0, 0)),
            scratch_shapes=[pltpu.VMEM((width // HD, rows, HD), F32)] * 2,
        ),
        out_shape=jax.ShapeDtypeStruct((rows, 3 * width), BF16),
        cost_estimate=pl.CostEstimate(
            flops=16 * rows * rows * width,
            bytes_accessed=16 * rows * width,
            transcendentals=rows * rows,
        ),
        name="attend_back",
    )(slots, qkv, grads)


def local(
    tokens,
    conditioning,
    slot_ids,
    dino_target,
    out_cotangent,
    ada_weight,
    qkv_weight,
    attn_weight,
    up_weight,
    down_weight,
    first_proj,
    second_proj,
    third_proj,
    ada_bias,
    query_bias,
    value_bias,
    attn_bias,
    up_bias,
    down_bias,
    first_bias,
    second_bias,
    third_bias,
):
    own_rows, width = tokens.shape
    place = lax.axis_index("seq")
    img = lax.axis_size("img")
    slot_count = conditioning.shape[0]
    part_width = width // SEQ
    feat = qkv_weight.shape[0]
    mod_cols = ada_weight.shape[1]
    ff = up_bias.shape[0]
    ph = first_bias.shape[0]
    zd = third_bias.shape[0]
    ff_part = ff // SEQ
    ph_part = ph // SEQ
    ff_cell = ff // img // SEQ
    ph_cell = ph // img // SEQ

    cond_act, cond_slope = silu_parts(conditioning)
    cond_low = cond_act.astype(BF16)
    cond_send = cond_low.reshape(slot_count, img, feat).transpose(1, 0, 2)
    cond_cols = img_exchange(cond_send).reshape(img * slot_count, feat)

    zd_part, third_rows = zd // SEQ, ph // img // 2

    zd_part, third_rows = zd // SEQ, ph // img // 2
    qkv_w = lax.all_gather(qkv_weight, "img", axis=0, tiled=True)
    swaps, swap_where = spread_img(attn_weight)

    rows_full = gather_rows(tokens)
    cells = img // SEQ
    first_width = ph_part // SEQ

    half = ph_part // 2
    first_at, second_at = 2 * part_width, 2 * part_width + first_width
    hidden_cols = second_at + half
    proj_cols = ph_part + SEQ * half

    def cut_hidden(where, ins, outs):
        up, down, first, second = ins
        for d in range(SEQ):
            for j in range(cells):
                at = (j * SEQ + d) * ff_cell
                outs[0][d, :, j * ff_cell : (j + 1) * ff_cell] = up[:, at : at + ff_cell]
                at, to = (j * SEQ + d) * ph_cell, first_at + j * ph_cell
                outs[0][d, :, to : to + ph_cell] = first[:, at : at + ph_cell]
            outs[0][d, :, part_width:first_at] = down[d]
            for side in range(2):
                rows = slice(side * ph_cell, (side + 1) * ph_cell)
                outs[0][d, rows, second_at:] = second[d, :, side * half : (side + 1) * half]

    mlp_send = arrange(
        cut_hidden,
        [((SEQ, feat, hidden_cols), BF16)],
        up_weight,
        down_weight.reshape(SEQ, ff_cell, part_width),
        first_proj,
        second_proj.reshape(SEQ, ph_cell, ph_part),
    )[0]

    def join_hidden(where, ins, outs):
        for d in range(SEQ):
            part = ins[0].at[d]
            at = d * part_width
            outs[0][:, at : at + part_width] = part[:, :part_width]
            at += ff_part
            outs[0][:, at : at + part_width] = part[:, part_width:first_at]
            at = d * first_width
            outs[1][:, at : at + first_width] = part[:, first_at:second_at]
            at = ph_part + d * half
            outs[1][:, at : at + half] = part[:, second_at:]
        for side in range(2):
            at = proj_cols + side * zd_part
            rows = slice(side * third_rows, (side + 1) * third_rows)
            outs[1][:third_rows, at : at + zd_part] = ins[1][rows]

    mod_send = product(cond_cols, ada_weight).reshape(img, slot_count, mod_cols)
    mod_parts = img_exchange(mod_send)
    my_bias = lax.dynamic_slice_in_dim(ada_bias, place * mod_cols, mod_cols, 0)
    mod_own = tie(jnp.sum(mod_parts, axis=0) + my_bias, *rows_full)
    modulation = lax.all_gather(mod_own, "seq", axis=1, tiled=True)
    mlp_got = seq_exchange(tie(mlp_send, modulation))
    mlp_shard, proj_shard = arrange(
        join_hidden,
        [((feat, 2 * ff_part), BF16), ((feat, proj_cols + 2 * zd_part), BF16)],
        mlp_got,
        third_proj,
    )
    mlp_all = lax.all_gather(mlp_shard, "img", axis=0, tiled=True)
    up_w, down_w = mlp_all[:, :ff_part], mlp_all[:, ff_part:]
    proj_all = lax.all_gather(proj_shard, "img", axis=0, tiled=True)
    proj_all = proj_all.reshape((img,) + proj_shard.shape)

    order = jnp.arange(SEQ, dtype=jnp.int32)
    all_slots = slot_ids.reshape(SEQ, own_rows)[:, 0]
    ours = (place ^ order)[:, None] == order[None, :]
    block_slots = jnp.sum(jnp.where(ours, all_slots[None, :], 0), axis=1)
    block_mod = sum(
        jnp.where((block_slots == slot)[:, None], modulation[slot][None, :], 0.0)
        for slot in range(slot_count)
    )
    shift_a, scale_a, gate_a, shift_b, scale_b, gate_b = jnp.split(block_mod[0], 6)

    def modulated(rows, first):
        normed, _ = norm_parts(rows.astype(F32).reshape(2, own_rows, width))
        shift = block_mod[first : first + 2, None, :width]
        scale = block_mod[first : first + 2, None, width : 2 * width]
        return (normed * (1.0 + scale) + shift).astype(BF16).reshape(2 * own_rows, width)

    hidden_a = jnp.concatenate([modulated(rows_full[0], 0), modulated(rows_full[1], 2)], 0)

    def open_attn(block, attn_ref):
        attn_ref[...] = block[...]

    def all_seq(part):
        across = swap(part, 2)
        return [part, swap(part, 1), across, swap(across, 1)]

    attn_part = open_spread(open_attn, [attn_weight.shape], swaps, swap_where)[0]
    attn_blocks = all_seq(attn_part)
    attn_w = join_columns(attn_blocks, place).reshape(width, width)
    zeros = jnp.zeros_like(query_bias)
    qkv_bias = jnp.concatenate([query_bias, zeros, value_bias])
    qkv_bias = lax.dynamic_slice_in_dim(qkv_bias, place * 3 * part_width, 3 * part_width, 0)
    qkv_own = (product(hidden_a, qkv_w) + qkv_bias).astype(BF16)

    distance = place ^ order
    chunk = (SEQ, own_rows, part_width)
    wide = (own_rows, SEQ * part_width)

    def cut_three(where, ins, outs):
        for turn in range(SEQ):

            def put():
                for p in range(SEQ):
                    rows = slice(p * own_rows, (p + 1) * own_rows)
                    at = (turn ^ p) * part_width
                    for j in range(3):
                        piece = ins[0][rows, j * part_width : (j + 1) * part_width]
                        outs[j][:, at : at + part_width] = piece

            pl.when(where[0] == turn)(put)

    turns = [[(i, (3 * i + j) % SEQ) for i in range(SEQ)] for j in range(3)]
    three = arrange(cut_three, [(wide, BF16)] * 3, qkv_own, place=place)
    three = [tie(lax.ppermute(three[j], "seq", turns[j]), *swaps) for j in range(3)]

    def join_three(where, ins, outs):
        for turn in range(3):

            def put():
                for kind in range(3):
                    at = kind * part_width
                    for b in range(SEQ):
                        piece = ins[(kind + turn) % 3][:, b * part_width : (b + 1) * part_width]
                        outs[0][b, :, at : at + part_width] = piece

            pl.when(where[0] == turn)(put)

    joined = (SEQ, own_rows, 3 * part_width)
    qkv = arrange(join_three, [(joined, BF16)], *three, place=place % 3)[0]
    qkv = qkv.reshape(SEQ * own_rows, 3 * part_width)
    attended_h = attend_forward(qkv, all_slots)

    def by_distance_rows(where, ins, outs):
        for p in range(SEQ):
            outs[p][...] = ins[0][where[p]]

    attended_h = arrange(
        by_distance_rows,
        [((own_rows, part_width), BF16)] * SEQ,
        attended_h.reshape(chunk),
        place=distance,
    )
    heads_rel = [attended_h[0]] + [swap(attended_h[p], p) for p in range(1, SEQ)]
    attended = join_columns([tie(block, attn_w) for block in heads_rel], place)
    tokens_f = tokens.astype(F32)
    branch_a = product(attended, attn_w) + attn_bias
    after_attn = tokens_f + gate_a * branch_a
    normed_b, inverse_b = norm_parts(after_attn)
    hidden_b = gather_rows((normed_b * (1.0 + scale_b) + shift_b).astype(BF16))

    my_up_bias = up_bias.reshape(img, SEQ, ff_cell)
    my_up_bias = lax.dynamic_index_in_dim(my_up_bias, place, 1, keepdims=False).reshape(ff_part)

    def open_projector(ref, first_ref, second_ref, third_ref):
        first_ref[...] = ref[:, :ph_part]
        for side in range(2):
            rows = slice(side * ph_cell, (side + 1) * ph_cell)
            for d in range(SEQ):
                at, to = ph_part + d * half, (2 * d + side) * half
                second_ref[:, to : to + half] = ref[rows, at : at + half]
            at = proj_cols + side * zd_part
            rows = slice(side * third_rows, (side + 1) * third_rows)
            third_ref[rows, :] = ref[:third_rows, at : at + zd_part]

    first_w, second_w, third_part = open_blocks(
        open_projector, [(feat, ph_part), (ph_cell, ph), (2 * third_rows, zd_part)], proj_all
    )
    first_w, second_w = first_w.reshape(width, ph_part), second_w.reshape(ph_part, ph)
    third_w = jnp.concatenate(all_seq(third_part.reshape(ph, zd_part).T), 0)
    acts, slopes, sums = [], [], []
    for side in range(2):
        value, slope = gelu_parts(product(hidden_b[side], up_w) + my_up_bias)
        acts.append(value.astype(BF16))
        slopes.append(slope)
        sums.append(product(acts[side], down_w, BF16))
    branch_b = scatter_rows(*sums) + down_bias
    result = after_attn + gate_b * branch_b
    feed_low = result.astype(BF16)

    feed = gather_rows(feed_low)
    my_first_bias = first_bias.reshape(img, SEQ, ph_cell)
    my_first_bias = lax.dynamic_index_in_dim(my_first_bias, place, 1, keepdims=False)
    my_first_bias = my_first_bias.reshape(ph_part)
    first_acts, first_slopes, sums = [], [], []
    for side in range(2):
        value, slope = silu_parts(product(feed[side], first_w) + my_first_bias)
        first_acts.append(value.astype(BF16))
        first_slopes.append(slope)
        sums.append(product(first_acts[side], second_w, BF16))
    second_act, second_slope = silu_parts(scatter_rows(*sums) + second_bias)
    second_low = second_act.astype(BF16)
    def by_distance(values):
        blocks = values.reshape(values.shape[:-1] + (SEQ, zd_part))
        blocks = [
            lax.dynamic_index_in_dim(blocks, place ^ p, blocks.ndim - 2, keepdims=False)
            for p in range(SEQ)
        ]
        return jnp.concatenate(blocks, axis=-1)

    aligned = product_nt(second_low, third_w) + by_distance(third_bias)
    target = join_columns(split_columns(dino_target, place)).astype(F32)
    inv_z = lax.rsqrt(jnp.sum(aligned * aligned, axis=1, keepdims=True) + EPS_COS)
    inv_t = lax.rsqrt(jnp.sum(target * target, axis=1, keepdims=True) + EPS_COS)
    cosine = jnp.sum(aligned * target, axis=1, keepdims=True) * inv_z * inv_t
    grad_aligned = -LAMBDA_ALIGN * (target * inv_t - cosine * aligned * inv_z) * inv_z
    grad_aligned = grad_aligned.astype(BF16)

    grad_second = (product(grad_aligned, third_w) * second_slope).astype(BF16)
    third_blocks = [
        product_tn(grad_aligned[:, p * zd_part : (p + 1) * zd_part], second_low, BF16)
        for p in range(SEQ)
    ]
    grad_seconds = gather_rows(grad_second)
    grad_firsts, sums = [], []
    for side in range(2):
        rows = grad_seconds[side] if side == 0 else tie(grad_seconds[1], sums[0], *third_blocks)
        grad = product_nt(rows, second_w) * first_slopes[side]
        grad_firsts.append(grad.astype(BF16))
        sums.append(product_nt(grad_firsts[side], first_w, BF16))
    first_acts = tie(jnp.concatenate(first_acts, 0), sums[1])
    second_term = product_tn(first_acts, jnp.concatenate(grad_seconds, 0), BF16)
    second_sum = lax.psum_scatter(second_term, "img", scatter_dimension=0, tiled=True)
    grad_first = jnp.concatenate(grad_firsts, 0)
    first_term = product_tn(tie(jnp.concatenate(feed, 0), sums[1]), grad_first, BF16)
    first_got = img_exchange(first_term.reshape(img, feat, ph_part))
    grad_result = tie(scatter_rows(*sums), second_term, first_term)
    grad_result = out_cotangent.astype(F32) + grad_result

    grad_branch_b = (gate_b * grad_result).astype(BF16)
    grad_branches = gather_rows(grad_branch_b)
    third_sum = scatter_blocks([tie(block, grad_branches[1]) for block in third_blocks])
    third_sum = third_sum.astype(BF16)
    grad_pres, sums = [], []
    for side in range(2):
        rows = grad_branches[side] if side == 0 else tie(grad_branches[1], sums[0], first_got)
        grad = product_nt(rows, down_w) * slopes[side]
        grad_pres.append(grad.astype(BF16))
        sums.append(product_nt(grad_pres[side], up_w, BF16))
    acts = tie(jnp.concatenate(acts, 0), sums[1])
    down_term = product_tn(acts, jnp.concatenate(grad_branches, 0), BF16)
    down_sum = lax.psum_scatter(down_term, "img", scatter_dimension=0, tiled=True)
    grad_pre = jnp.concatenate(grad_pres, 0)
    up_term = product_tn(tie(jnp.concatenate(hidden_b, 0), sums[1]), grad_pre, BF16)
    up_pair = reduce_pair(up_term)
    grad_hidden_b = tie(scatter_rows(*sums), down_term, up_term, third_sum)
    grad_after = grad_result + norm_back(normed_b, inverse_b, grad_hidden_b * (1.0 + scale_b))

    grad_branch_a = (gate_a * grad_after).astype(BF16)
    grad_attended = product_nt(tie(grad_branch_a, up_pair), attn_w, BF16)
    grad_parts = split_columns(grad_attended, place)
    grad_heads = [grad_parts[0]] + [swap(grad_parts[p], p) for p in range(1, SEQ)]
    branch_cols = split_columns(grad_branch_a, place)
    attended = tie(attended, *grad_parts)
    attn_sum = scatter_blocks([product_tn(attended, cols, BF16) for cols in branch_cols])
    up_got = slow_exchange(tie(up_pair, first_got))

    def rows_in_order(where, ins, outs):
        for p in range(SEQ):
            outs[0][where[p]] = ins[p][...]

    grad_heads = arrange(rows_in_order, [(chunk, BF16)], *grad_heads, place=distance)[0]
    grad_heads = grad_heads.reshape(SEQ * own_rows, part_width)
    grad_joined = attend_backward(qkv, grad_heads, all_slots)
    third_send = third_sum.reshape(zd_part, img, ph // img).transpose(1, 0, 2)
    third_got = img_exchange(tie(third_send, up_got))
    grad_joined = tie(grad_joined, up_got).reshape(joined)

    def cut_back(where, ins, outs):
        for turn in range(3):

            def put():
                for kind in range(3):
                    at = kind * part_width
                    for b in range(SEQ):
                        piece = ins[0][b, :, at : at + part_width]
                        outs[(kind + turn) % 3][:, b * part_width : (b + 1) * part_width] = piece

            pl.when(where[0] == turn)(put)

    backs = arrange(cut_back, [(wide, BF16)] * 3, grad_joined, place=place % 3)
    backs = [lax.ppermute(backs[j], "seq", [(b, a) for a, b in turns[j]]) for j in range(3)]
    backs = [tie(back, third_got) for back in backs]

    def join_back(where, ins, outs):
        for turn in range(SEQ):

            def put():
                for p in range(SEQ):
                    rows = slice(p * own_rows, (p + 1) * own_rows)
                    at = (turn ^ p) * part_width
                    for j in range(3):
                        piece = ins[j][:, at : at + part_width]
                        outs[0][rows, j * part_width : (j + 1) * part_width] = piece

            pl.when(where[0] == turn)(put)

    grad_qkv = arrange(join_back, [(qkv_own.shape, BF16)], *backs, place=place)[0]
    far = product_nt(grad_qkv[2 * own_rows :], qkv_w, BF16)
    near = product_nt(tie(grad_qkv, far)[: 2 * own_rows], qkv_w, BF16)
    grad_hidden_a = scatter_rows(near, far)
    qkv_term = product_tn(tie(hidden_a, near), grad_qkv, BF16)
    attn_send = attn_sum.astype(BF16).reshape(img, feat, part_width)
    attn_got = img_exchange(tie(attn_send, third_got))
    grad_hidden_a = tie(grad_hidden_a, attn_got)
    normed_a, inverse_a = norm_parts(tokens_f)
    tokens_grad = grad_after + norm_back(normed_a, inverse_a, grad_hidden_a * (1.0 + scale_a))

    own_sums = jnp.concatenate(
        [
            column_sums(grad_hidden_a),
            column_sums(grad_hidden_a * normed_a),
            column_sums(grad_after * branch_a),
            column_sums(grad_hidden_b),
            column_sums(grad_hidden_b * normed_b),
            column_sums(grad_result * branch_b),
        ]
    )
    aligned_sums = column_sums(grad_aligned).reshape(SEQ, zd_part)
    by_place = [
        own_sums.reshape(SEQ, mod_cols),
        column_sums(grad_branch_a).reshape(SEQ, part_width),
        column_sums(grad_branch_b).reshape(SEQ, part_width),
        column_sums(grad_second).reshape(SEQ, ph_part),
        jnp.stack([pick(aligned_sums, place ^ j) for j in range(SEQ)]),
    ]
    def split_sums(where, ins, outs):
        for d in range(SEQ):
            at = d * part_width
            total = ins[0][0, :, at : at + part_width].astype(F32)
            for k in range(1, img // 2):
                total = total + ins[0][k, :, at : at + part_width].astype(F32)
            outs[0][d, :, :part_width] = total.astype(BF16)
            outs[0][d, :, part_width:first_at] = ins[1][:, at : at + part_width]
            at = d * first_width
            total = ins[2][0, :, at : at + first_width].astype(F32)
            for k in range(1, img):
                total = total + ins[2][k, :, at : at + first_width].astype(F32)
            outs[0][d, :, first_at:second_at] = total.astype(BF16)
            for side in range(2):
                rows = slice(side * ph_cell, (side + 1) * ph_cell)
                at = (2 * d + side) * half
                outs[0][d, rows, second_at:] = ins[3][:, at : at + half]

    hidden_send = arrange(
        split_sums, [((SEQ, feat, hidden_cols), BF16)], up_got, down_sum, first_got, second_sum
    )[0]
    hidden_got = seq_exchange(tie(hidden_send, attn_got))

    by_place = jnp.concatenate(by_place, axis=1)
    seq_got = seq_exchange(tie(by_place, hidden_got))
    qkv_pair = reduce_pair(qkv_term, seq_got)
    member = (all_slots[None, :] == jnp.arange(slot_count, dtype=jnp.int32)[:, None]).astype(F32)
    grad_mod = jnp.sum(member[:, :, None] * seq_got[None, :, :mod_cols], axis=1)
    grad_mod = grad_mod.astype(BF16).astype(F32)
    row_biases = jnp.sum(seq_got[:, mod_cols:], axis=0)
    bias_sums = jnp.concatenate(
        [
            row_biases,
            column_sums(grad_qkv),
            column_sums(grad_pre),
            column_sums(grad_first),
        ]
    )
    mod_size = slot_count * mod_cols
    img_got = img_gather(jnp.concatenate([grad_mod.reshape(mod_size), bias_sums]))
    grad_mods = img_got[:, :mod_size].reshape(img * slot_count, mod_cols).astype(BF16)
    bias_sums = jnp.sum(img_got[:, mod_size:], axis=0)
    ada_weight_grad = product_tn(cond_cols, grad_mods)
    cond_parts = product_nt(grad_mods, ada_weight).reshape(img, slot_count, feat)
    qkv_weight_grad = slow_scatter(qkv_pair, img_got)
    cond_parts = img_exchange(cond_parts).transpose(1, 0, 2).reshape(slot_count * width)
    last = jnp.concatenate([column_sums(grad_mods), bias_sums, cond_parts])
    last = jnp.pad(last, (0, -last.shape[0] % 1024))
    last = lax.all_gather(last, "seq", axis=0, tiled=False)
    sizes = [mod_cols, part_width, part_width, ph_part, zd // SEQ, 3 * part_width]
    sizes += [ff_part, ph_part, slot_count * width]
    cuts, start = [], 0
    for size in sizes:
        cuts.append(last[:, start : start + size])
        start += size
    ada_bias_grad, attn_bias_grad, down_bias_grad, second_bias_grad, third_bias_grad = (
        cut.reshape(-1) for cut in cuts[:5]
    )
    qkv_bias_grad = cuts[5].reshape(-1)
    query_bias_grad, value_bias_grad = qkv_bias_grad[:width], qkv_bias_grad[2 * width :]
    up_bias_grad = cuts[6].reshape(SEQ, img, ff_cell).transpose(1, 0, 2).reshape(ff)
    first_bias_grad = cuts[7].reshape(SEQ, img, ph_cell).transpose(1, 0, 2).reshape(ph)
    conditioning_grad = jnp.sum(cuts[8], axis=0).reshape(slot_count, width) * cond_slope

    def join_cells(where, ins, outs):
        up, down, first, second = outs
        for d in range(SEQ):
            part = ins[0].at[d]
            for j in range(cells):
                at = (j * SEQ + d) * ff_cell
                up[:, at : at + ff_cell] = part[:, j * ff_cell : (j + 1) * ff_cell].astype(F32)
                at, to = (j * SEQ + d) * ph_cell, first_at + j * ph_cell
                first[:, at : at + ph_cell] = part[:, to : to + ph_cell].astype(F32)
            down[d] = part[:, part_width:first_at].astype(F32)
            for side in range(2):
                rows = slice(side * ph_cell, (side + 1) * ph_cell)
                second[d, :, side * half : (side + 1) * half] = part[rows, second_at:].astype(F32)

    up_weight_grad, down_weight_grad, first_proj_grad, second_proj_grad = arrange(
        join_cells,
        [
            ((feat, ff_part), F32),
            ((SEQ, ff_cell, part_width), F32),
            ((feat, ph_part), F32),
            ((SEQ, ph_cell, ph_part), F32),
        ],
        hidden_got,
    )
    down_weight_grad = down_weight_grad.reshape(ff // img, part_width)
    second_proj_grad = second_proj_grad.reshape(ph // img, ph_part)
    third_proj_grad = block_sum(third_got).T
    attn_weight_grad = block_sum(attn_got)
    return (
        feed_low,
        tokens_grad,
        conditioning_grad,
        ada_weight_grad,
        qkv_weight_grad,
        attn_weight_grad,
        up_weight_grad,
        down_weight_grad,
        first_proj_grad,
        second_proj_grad,
        third_proj_grad,
        ada_bias_grad,
        query_bias_grad,
        value_bias_grad,
        attn_bias_grad,
        up_bias_grad,
        down_bias_grad,
        first_bias_grad,
        second_bias_grad,
        third_bias_grad,
    )


def solution(mesh):
    rows = P(("img", "seq"), None)
    both = P("img", "seq")
    return jax.shard_map(
        local,
        mesh=mesh,
        in_specs=(rows, P("img", None), P("img"), rows, rows) + (both,) * 8 + (P(),) * 9,
        out_specs=(rows, rows, P("img", None)) + (both,) * 8 + (P(),) * 9,
        check_vma=False,
    )
```

time: 930 us -> 727 us (0.78)
  waiting for transfers between devices: 390 us -> 241 us
  local copies, waits for them, and re-layouts: 152 us -> 53.1 us
  Pallas kernels: 34.3 us -> 97.3 us
  other arithmetic: 97 us -> 68.7 us
  matrix products: 92.4 us -> 113 us
    ppermute x8 -> x6, waiting for transfers between devices: 94.9 us -> 17.5 us  [img_swap(): return lax.ppermute(values, 'img', [(i, i ^ 1) for i in range(count)])]
    all_to_all x8 -> x1, waiting for transfers between devices: 105 us -> 31.3 us  [slow_exchange(): lax.all_to_all(parts, 'img', split_axis=0, concat_axis=0, tiled=True, axi...]
    pallas_call x0 -> x18, Pallas kernels: none -> 56.7 us  [the longest x17 49.9 us: arrange(): pl.pallas_call(kernel, grid_spec=pltpu.PrefetchScalarGridSpec(num_scalar_...]
    ppermute x0 -> x12, waiting for transfers between devices: none -> 31 us  [the longest x6 21.6 us: slow_swap(): lax.ppermute(values, 'img', [(i, i ^ 2 * distance) for i in range(count)])]
    all_to_all x8 -> x1, starting transfers between devices: 34.7 us -> 4.53 us  [slow_exchange(): lax.all_to_all(parts, 'img', split_axis=0, concat_axis=0, tiled=True, axi...]
    ppermute x0 -> x12, starting transfers between devices: none -> 23.9 us  [the longest x3 9.45 us: local(): lax.ppermute(backs[j], 'seq', [(b, a) for a, b in turns[j]])]
    another operation x7 -> x0, local copies, waits for them, and re-layouts: 21.3 us -> none  [the longest x1 8.74 us: pad_heads(): parted = values.reshape(lead + (heads, HD))]
    ppermute x36 -> x48, waiting for transfers between devices: 137 us -> 115 us  [swap(): return lax.ppermute(values, 'seq', [(i, i ^ distance) for i in range(SEQ)])]
  transfers between devices with their start and end apart: 68 -> 82, of which waited for: 36 -> 28; matrix products, arithmetic and copies ran while one was open for 34% -> 29% of each run, Pallas kernels for 4% -> 14%
where the time goes in v2:
time: 727 us; the launch traced here: 715 us
  waiting for transfers between devices  241 us (33%)
  starting transfers between devices  114 us (16%)
  matrix products  113 us (16%)
  Pallas kernels  97.3 us (13%)
  other arithmetic  68.7 us (9%)
  local copies, waits for them, and re-layouts  53.1 us (7%)
  between operations  16.1 us (2%)
  blocking collectives  10.9 us (1%)
    ppermute x48, waiting for transfers between devices, swap(): return lax.ppermute(values, 'seq', [(i, i ^ distance) for i in range(SEQ)])  115 us
    pallas_call x17, Pallas kernels, arrange(): pl.pallas_call(kernel, grid_spec=pltpu.PrefetchScalarGridSpec(num_scalar_...  49.9 us
    dot_general x13, matrix products, product_nt(): lax.dot_general(left, right, (((1,), (1,)), ((), ())), preferred_element_...  38.9 us
    dot_general x12, matrix products, product(): lax.dot_general(left, right, (((1,), (0,)), ((), ())), preferred_element_...  37.2 us
    dot_general x14, matrix products, product_tn(): lax.dot_general(left, right, (((0,), (0,)), ((), ())), preferred_element_...  36.7 us
    all_to_all x7, starting transfers between devices, img_exchange(): return lax.all_to_all(parts, 'img', split_axis=0, concat_axis=0, tiled=True)  36.1 us
    all_to_all x1, waiting for transfers between devices, slow_exchange(): lax.all_to_all(parts, 'img', split_axis=0, concat_axis=0, tiled=True, axi...  31.3 us
    ppermute x48, starting transfers between devices, swap(): return lax.ppermute(values, 'seq', [(i, i ^ distance) for i in range(SEQ)])  29.3 us
  transfers between devices with their start and end apart: 82, of which 28 were waited for; matrix products, arithmetic and copies ran while one was open for 29% of the time, Pallas kernels for 14%

profile of v2, /device:TPU:0, one launch (start us, length us, event | category | flops | bytes accessed | tf_op | source)
XLA Modules:
  0.0 714.7 jit_solution(18076842335729843637)
XLA Ops:
  9.4 7.3 %all-to-all-start = ((bf16[8,4,144]{2,1,0:T(4,128)(2,1)}), bf16[8,4,144]{2,1,0:T(4,128)(2,1)S(1)}, u32[]{:S(2)}, u32[]{:S(2)}) async-start(bf16[8,4,144]{2,1,0:T(4,128)(2,1)} %copy.125), calls=%async_computation | async-start | bytes 32768 | tf_op jit(solution)/shard_map/all_to_all | solution.py:244
  33.2 5.9 all-to-all-done.1
  55.4 14.2 %all-to-all-done.2.refs_0_ = bf16[4,144,960]{2,1,0:T(8,128)(2,1)} async-done(((bf16[4,144,960]{2,1,0:T(8,128)(2,1)}), bf16[4,144,960]{2,1,0:T(8,128)(2,1)}, u32[]{:S(2)}, u32[]{:S(2)}) %all-to-all-start.2) | async-done | bytes 1105952 | tf_op jit(solution)/shard_map/all_to_all | solution.py:240
  80.8 11.2 %collective-permute-done.7.refs_4_ = bf16[144,288]{1,0:T(8,128)(2,1)} collective-permute-done((bf16[144,288]{1,0:T(8,128)(2,1)}, bf16[144,288]{1,0:T(8,128)(2,1)}, u32[]{:S(2)}, u32[]{:S(2)}) %collective-permute-start.7) | collective-permute-done | bytes 82976 | tf_op jit(solution)/shard_map/ppermute | solution.py:109
  107.2 6.5 add_convert_fusion.refs_0_
  134.2 15.8 %attend.1 = bf16[1024,288]{1,0:T(8,128)(2,1)} custom-call(s32[4]{0:T(128)} %copy-done.101, bf16[1024,864]{1,0:T(8,128)(2,1)} %bitcast.143), custom_call_target="tpu_custom_call" | custom-call | flops 2415919104 | bytes 2359296 | tf_op jit(solution)/shard_map/attend/pallas_call | solution.py:325
  174.8 13.7 %collective-permute-done.21 = bf16[256,1152]{1,0:T(8,128)(2,1)S(1)} collective-permute-done((bf16[256,1152]{1,0:T(8,128)(2,1)S(1)}, bf16[256,1152]{1,0:T(8,128)(2,1)S(1)}, u32[]{:S(2)}, u32[]{:S(2)}) %collective-permute-start.21) | collective-permute-done | bytes 589856 | tf_op jit(solution)/shard_map/ppermute | solution.py:73
  207.0 13.6 %collective-permute-done.24 = bf16[256,1152]{1,0:T(8,128)(2,1)S(1)} collective-permute-done((bf16[256,1152]{1,0:T(8,128)(2,1)S(1)}, bf16[256,1152]{1,0:T(8,128)(2,1)S(1)}, u32[]{:S(2)}, u32[]{:S(2)}) %collective-permute-start.24) | collective-permute-done | bytes 589856 | tf_op jit(solution)/shard_map/ppermute | solution.py:73
  222.8 12.9 %collective-permute-done.27 = bf16[256,1152]{1,0:T(8,128)(2,1)S(1)} collective-permute-done((bf16[256,1152]{1,0:T(8,128)(2,1)S(1)}, bf16[256,1152]{1,0:T(8,128)(2,1)S(1)}, u32[]{:S(2)}, u32[]{:S(2)}) %collective-permute-start.27) | collective-permute-done | bytes 589856 | tf_op jit(solution)/shard_map/ppermute | solution.py:73
  237.0 6.8 open_blocks.1
  268.2 30.2 %collective-permute-done.32 = bf16[192,2048]{1,0:T(8,128)(2,1)} collective-permute-done((bf16[192,2048]{1,0:T(8,128)(2,1)}, bf16[192,2048]{1,0:T(8,128)(2,1)}, u32[]{:S(2)}, u32[]{:S(2)}) %collective-permute-start.32) | collective-permute-done | bytes 786464 | tf_op jit(solution)/shard_map/ppermute | solution.py:73
  318.2 17.1 %collective-permute-done.36 = bf16[256,2048]{1,0:T(8,128)(2,1)S(1)} collective-permute-done((bf16[256,2048]{1,0:T(8,128)(2,1)S(1)}, bf16[256,2048]{1,0:T(8,128)(2,1)S(1)}, u32[]{:S(2)}, u32[]{:S(2)}) %collective-permute-start.36) | collective-permute-done | bytes 1048608 | tf_op jit(solution)/shard_map/ppermute | solution.py:73
  350.8 6.4 all-to-all-start.3
  361.0 6.2 fusion.10
  367.2 7.8 %collective-permute-done.39 = bf16[256,1152]{1,0:T(8,128)(2,1)} collective-permute-done((bf16[256,1152]{1,0:T(8,128)(2,1)}, bf16[256,1152]{1,0:T(8,128)(2,1)}, u32[]{:S(2)}, u32[]{:S(2)}) %collective-permute-start.39) | collective-permute-done | bytes 589856 | tf_op jit(solution)/shard_map/ppermute | solution.py:73
  386.4 7.1 collective-permute-done.42
  427.0 6.4 convolution_convert_fusion.1
  444.4 13.8 %collective-permute-done.49 = bf16[4,144,1152]{2,1,0:T(8,128)(2,1)} collective-permute-done((bf16[4,144,1152]{2,1,0:T(8,128)(2,1)}, bf16[4,144,1152]{2,1,0:T(8,128)(2,1)}, u32[]{:S(2)}, u32[]{:S(2)}) %collective-permute-start.49) | collective-permute-done | bytes 1327136 | tf_op jit(solution)/shard_map/ppermute | solution.py:104
  485.2 31.3 %all-to-all-done.4.refs_0_ = bf16[4,144,1152]{2,1,0:T(8,128)(2,1)} async-done(((bf16[4,144,1152]{2,1,0:T(8,128)(2,1)}), bf16[4,144,1152]{2,1,0:T(8,128)(2,1)}, u32[]{:S(2)}, u32[]{:S(2)}) %all-to-all-start.4) | async-done | bytes 1327136 | tf_op jit(solution)/shard_map/all_to_all | solution.py:221
  526.1 24.7 %attend_back.1 = bf16[1024,864]{1,0:T(8,128)(2,1)} custom-call(s32[4]{0:T(128)} %copy-done.101, bf16[1024,864]{1,0:T(8,128)(2,1)} %bitcast.144, bf16[1024,288]{1,0:T(8,128)(2,1)} %bitcast.156), custom_call_target="tpu_custom_call" | custom-call | flops 4831838208 | bytes 4718592 | tf_op jit(solution)/shard_map/attend_back/pallas_call | solution.py:343
  554.3 6.1 collective-permute-start.53
  596.3 6.0 all-to-all-start.6
  634.1 11.4 %all-to-all-done.7.refs_0_ = bf16[4,144,960]{2,1,0:T(8,128)(2,1)} async-done(((bf16[4,144,960]{2,1,0:T(8,128)(2,1)}), bf16[4,144,960]{2,1,0:T(8,128)(2,1)}, u32[]{:S(2)}, u32[]{:S(2)}) %all-to-all-start.7) | async-done | bytes 1105952 | tf_op jit(solution)/shard_map/all_to_all | solution.py:240
  682.7 9.3 %collective-permute-done.64 = bf16[144,864]{1,0:T(8,128)(2,1)S(1)} collective-permute-done((bf16[144,864]{1,0:T(8,128)(2,1)S(1)}, bf16[144,864]{1,0:T(8,128)(2,1)S(1)}, u32[]{:S(2)}, u32[]{:S(2)}) %collective-permute-start.64) | collective-permute-done | bytes 248864 | tf_op jit(solution)/shard_map/ppermute | solution.py:109
  (599 shorter events, 406.8 us)
Async XLA Ops:
  7.2 99.9 %all-gather.6.cloned.1.call-start = ((), (), s32[]{:S(2)}) async-start(), calls=%async_computation.13 | async-start | bytes 2322432 | tf_op jit(solution)/shard_map/all_gather | solution.py:412
  53.7 136.9 %all-gather.8.cloned.1.call-start = ((), (), s32[]{:S(2)}) async-start(), calls=%async_computation.14 | async-start | bytes 5971968 | tf_op jit(solution)/shard_map/all_gather | solution.py:474
  72.4 164.6 %all-gather.10.cloned.1.call-start = ((), (), s32[]{:S(2)}) async-start(), calls=%async_computation.15 | async-start | bytes 4976640 | tf_op jit(solution)/shard_map/all_gather | solution.py:476
  122.7 33.5 %collective-permute-start.13 = (bf16[8,144,288]{2,1,0:T(8,128)(2,1)S(1)}, bf16[8,144,288]{2,1,0:T(8,128)(2,1)S(1)}, u32[]{:S(2)}, u32[]{:S(2)}) collective-permute-start(bf16[8,144,288]{2,1,0:T(8,128)(2,1)S(1)} %copy-done.10), channel_id=1, source_target_pairs={{0,1},{1,0},{2,3},{3,2},{4,5},{5,4},{6,7},{7,6},{8,9},{9,8},{10,11... | collective-permute-start | bytes 1990664 | tf_op jit(solution)/shard_map/ppermute | solution.py:73
  125.5 30.7 %collective-permute-start.15 = (bf16[8,144,288]{2,1,0:T(8,128)(2,1)}, bf16[8,144,288]{2,1,0:T(8,128)(2,1)}, u32[]{:S(2)}, u32[]{:S(2)}) collective-permute-start(bf16[8,144,288]{2,1,0:T(8,128)(2,1)} %collective-permute-done.14.refs_2_), channel_id=1, source_target_pairs={{0,1},{1,0},{2,3},{3,2},{4,5},{5,4},{6,7},{7,6},{8,9},{9,8},{10,11... | collective-permute-start | bytes 1990664 | tf_op jit(solution)/shard_map/ppermute | solution.py:73
  254.2 44.7 %collective-permute-start.26 = (bf16[256,2048]{1,0:T(8,128)(2,1)}, bf16[256,2048]{1,0:T(8,128)(2,1)}, u32[]{:S(2)}, u32[]{:S(2)}) collective-permute-start(bf16[256,2048]{1,0:T(8,128)(2,1)} %slice.235), channel_id=1, source_target_pairs={{0,1},{1,0},{2,3},{3,2},{4,5},{5,4},{6,7},{7,6},{8,9},{9,8},{10,11... | collective-permute-start | bytes 3145736 | tf_op jit(solution)/shard_map/ppermute | solution.py:73
  256.1 42.9 %collective-permute-start.30 = (bf16[256,2048]{1,0:T(8,128)(2,1)}, bf16[256,2048]{1,0:T(8,128)(2,1)}, u32[]{:S(2)}, u32[]{:S(2)}) collective-permute-start(bf16[256,2048]{1,0:T(8,128)(2,1)} %add_convert_fusion.1), channel_id=1, source_target_pairs={{0,2},{1,3},{2,0},{3,1},{4,6},{5,7},{6,4},{7,5},{8,10},{9,11},{10,... | collective-permute-start | bytes 3145736 | tf_op jit(solution)/shard_map/ppermute | solution.py:73
  259.8 38.6 %collective-permute-start.32 = (bf16[192,2048]{1,0:T(8,128)(2,1)}, bf16[192,2048]{1,0:T(8,128)(2,1)}, u32[]{:S(2)}, u32[]{:S(2)}) collective-permute-start(bf16[192,2048]{1,0:T(8,128)(2,1)} %bitcast.152), channel_id=1, source_target_pairs={{0,2},{1,3},{2,0},{3,1},{4,6},{5,7},{6,4},{7,5},{8,10},{9,11},{10,... | collective-permute-start | bytes 2359304 | tf_op jit(solution)/shard_map/ppermute | solution.py:73
  268.2 33.3 %collective-permute-start.31 = (bf16[192,2048]{1,0:T(8,128)(2,1)S(1)}, bf16[192,2048]{1,0:T(8,128)(2,1)S(1)}, u32[]{:S(2)}, u32[]{:S(2)}) collective-permute-start(bf16[192,2048]{1,0:T(8,128)(2,1)S(1)} %bitcast.153), channel_id=1, source_target_pairs={{0,1},{1,0},{2,3},{3,2},{4,5},{5,4},{6,7},{7,6},{8,9},{9,8},{10,11... | collective-permute-start | bytes 2359304 | tf_op jit(solution)/shard_map/ppermute | solution.py:73
  350.8 57.5 %all-to-all-start.3 = ((bf16[8,144,512]{2,1,0:T(8,128)(2,1)}), bf16[8,144,512]{2,1,0:T(8,128)(2,1)}, u32[]{:S(2)}, u32[]{:S(2)}) async-start(bf16[8,144,512]{2,1,0:T(8,128)(2,1)} %bitcast.147), calls=%async_computation.3 | async-start | bytes 2359296 | tf_op jit(solution)/shard_map/all_to_all | solution.py:244
  357.2 260.1 %reduce-scatter.5.cloned.1.call-start = ((), (), s32[]{:S(2)}) async-start(), calls=%async_computation.17 | async-start | bytes 2359296 | tf_op jit(solution)/shard_map/reduce_scatter | solution.py:639
  383.3 234.0 %reduce-scatter.3.cloned.1.call-start = ((), (), s32[]{:S(2)}) async-start(), calls=%async_computation.16 | async-start | bytes 2985984 | tf_op jit(solution)/shard_map/reduce_scatter | solution.py:658
  404.1 32.3 %collective-permute-start.41 = (bf16[256,1152]{1,0:T(8,128)(2,1)}, bf16[256,1152]{1,0:T(8,128)(2,1)}, u32[]{:S(2)}, u32[]{:S(2)}) collective-permute-start(bf16[256,1152]{1,0:T(8,128)(2,1)} %slice.247), channel_id=1, source_target_pairs={{0,1},{1,0},{2,3},{3,2},{4,5},{5,4},{6,7},{7,6},{8,9},{9,8},{10,11... | collective-permute-start | bytes 1769480 | tf_op jit(solution)/shard_map/ppermute | solution.py:73
  421.7 43.8 %collective-permute-start.46 = (bf16[192,2048]{1,0:T(8,128)(2,1)}, bf16[192,2048]{1,0:T(8,128)(2,1)}, u32[]{:S(2)}, u32[]{:S(2)}) collective-permute-start(bf16[192,2048]{1,0:T(8,128)(2,1)} %convolution_convert_fusion.21), channel_id=1, source_target_pairs={{0,1},{1,0},{2,3},{3,2},{4,5},{5,4},{6,7},{7,6},{8,9},{9,8},{10,11... | collective-permute-start | bytes 2359304 | tf_op jit(solution)/shard_map/ppermute | solution.py:73
  422.9 35.3 %collective-permute-start.49 = (bf16[4,144,1152]{2,1,0:T(8,128)(2,1)}, bf16[4,144,1152]{2,1,0:T(8,128)(2,1)}, u32[]{:S(2)}, u32[]{:S(2)}) collective-permute-start(bf16[4,144,1152]{2,1,0:T(8,128)(2,1)} %dynamic-slice_bitcast_fusion), channel_id=1, source_target_pairs={{0,4},{4,0},{8,12},{12,8},{16,20},{20,16},{24,28},{28,24},{1,5},{5... | collective-permute-start | bytes 3981320 | tf_op jit(solution)/shard_map/ppermute | solution.py:104
  460.9 55.6 %all-to-all-start.4 = ((bf16[4,144,1152]{2,1,0:T(8,128)(2,1)}), bf16[4,144,1152]{2,1,0:T(8,128)(2,1)}, u32[]{:S(2)}, u32[]{:S(2)}) async-start(bf16[4,144,1152]{2,1,0:T(8,128)(2,1)} %fusion.17), calls=%async_computation.4 | async-start | bytes 2654208 | tf_op jit(solution)/shard_map/all_to_all | solution.py:221
  480.9 41.7 %collective-permute-start.50 = (bf16[256,288]{1,0:T(8,128)(2,1)}, bf16[256,288]{1,0:T(8,128)(2,1)S(1)}, u32[]{:S(2)}, u32[]{:S(2)}) collective-permute-start(bf16[256,288]{1,0:T(8,128)(2,1)} %get-tuple-element.129), channel_id=1, source_target_pairs={{0,1},{1,0},{2,3},{3,2},{4,5},{5,4},{6,7},{7,6},{8,9},{9,8},{10,11... | collective-permute-start | bytes 442376 | tf_op jit(solution)/shard_map/ppermute | solution.py:73
  480.9 41.7 %collective-permute-start.51 = (bf16[256,288]{1,0:T(8,128)(2,1)}, bf16[256,288]{1,0:T(8,128)(2,1)S(1)}, u32[]{:S(2)}, u32[]{:S(2)}) collective-permute-start(bf16[256,288]{1,0:T(8,128)(2,1)} %get-tuple-element.130), channel_id=1, source_target_pairs={{0,2},{1,3},{2,0},{3,1},{4,6},{5,7},{6,4},{7,5},{8,10},{9,11},{10,... | collective-permute-start | bytes 442376 | tf_op jit(solution)/shard_map/ppermute | solution.py:73
  482.5 40.1 %collective-permute-start.52 = (bf16[256,288]{1,0:T(8,128)(2,1)}, bf16[256,288]{1,0:T(8,128)(2,1)}, u32[]{:S(2)}, u32[]{:S(2)}) collective-permute-start(bf16[256,288]{1,0:T(8,128)(2,1)} %get-tuple-element.131), channel_id=1, source_target_pairs={{0,3},{1,2},{2,1},{3,0},{4,7},{5,6},{6,5},{7,4},{8,11},{9,10},{10,... | collective-permute-start | bytes 442376 | tf_op jit(solution)/shard_map/ppermute | solution.py:73
  485.0 78.8 %collective-permute-start.60 = (bf16[1152,288]{0,1:T(8,128)(2,1)}, bf16[1152,288]{0,1:T(8,128)(2,1)S(1)}, u32[]{:S(2)}, u32[]{:S(2)}) collective-permute-start(bf16[1152,288]{0,1:T(8,128)(2,1)} %convolution_convert_fusion.14), channel_id=1, source_target_pairs={{0,1},{1,0},{2,3},{3,2},{4,5},{5,4},{6,7},{7,6},{8,9},{9,8},{10,11... | collective-permute-start | bytes 1990664 | tf_op jit(solution)/shard_map/ppermute | solution.py:73
  516.5 52.9 %all-to-all-start.5 = ((bf16[8,192,256]{2,1,0:T(8,128)(2,1)}), bf16[8,192,256]{2,1,0:T(8,128)(2,1)S(1)}, u32[]{:S(2)}, u32[]{:S(2)}) async-start(bf16[8,192,256]{2,1,0:T(8,128)(2,1)} %bitcast.131), calls=%async_computation.5 | async-start | bytes 1572864 | tf_op jit(solution)/shard_map/all_to_all | solution.py:244
  522.6 59.6 %collective-permute-start.59 = (bf16[1152,288]{0,1:T(8,128)(2,1)}, bf16[1152,288]{0,1:T(8,128)(2,1)}, u32[]{:S(2)}, u32[]{:S(2)}) collective-permute-start(bf16[1152,288]{0,1:T(8,128)(2,1)} %convolution_convert_fusion.16), channel_id=1, source_target_pairs={{0,1},{1,0},{2,3},{3,2},{4,5},{5,4},{6,7},{7,6},{8,9},{9,8},{10,11... | collective-permute-start | bytes 1990664 | tf_op jit(solution)/shard_map/ppermute | solution.py:73
  596.3 33.3 %collective-permute-start.56 = (bf16[256,1152]{1,0:T(8,128)(2,1)}, bf16[256,1152]{1,0:T(8,128)(2,1)}, u32[]{:S(2)}, u32[]{:S(2)}) collective-permute-start(bf16[256,1152]{1,0:T(8,128)(2,1)} %slice.252), channel_id=1, source_target_pairs={{0,1},{1,0},{2,3},{3,2},{4,5},{5,4},{6,7},{7,6},{8,9},{9,8},{10,11... | collective-permute-start | bytes 1769480 | tf_op jit(solution)/shard_map/ppermute | solution.py:73
  615.3 45.5 %collective-permute-start.62 = (bf16[4,144,864]{2,1,0:T(8,128)(2,1)}, bf16[4,144,864]{2,1,0:T(8,128)(2,1)}, u32[]{:S(2)}, u32[]{:S(2)}) collective-permute-start(bf16[4,144,864]{2,1,0:T(8,128)(2,1)} %dynamic-slice_bitcast_fusion.1), channel_id=1, source_target_pairs={{0,4},{4,0},{8,12},{12,8},{16,20},{20,16},{24,28},{28,24},{1,5},{5... | collective-permute-start | bytes 2985992 | tf_op jit(solution)/shard_map/ppermute | solution.py:104
  (171 other events, 1852.4 us)
Sparse Core Ops, SparseCore 0:
  10.2 55.6 all-gather.5
  72.6 87.7 all-gather.7
  162.6 74.4 all-gather.9
  383.4 70.6 reduce-scatter.4
  457.6 98.5 reduce-scatter.2

commit v3 on v2

--- a/solution.py
+++ b/solution.py
@@ -80,9 +80,10 @@
     return jnp.concatenate([own, near], 0), jnp.concatenate([across, far], 0)
 
 
-def scatter_blocks(blocks):
+def scatter_blocks(blocks, *after):
     from_far = swap(blocks[3], 1)
-    across = swap((blocks[2].astype(F32) + from_far.astype(F32)).astype(BF16), 2)
+    pair = (blocks[2].astype(F32) + from_far.astype(F32)).astype(BF16)
+    across = swap(tie(pair, *after) if after else pair, 2)
     from_near = swap(blocks[1], 1)
     return blocks[0].astype(F32) + from_near.astype(F32) + across.astype(F32)
 
@@ -206,15 +207,29 @@
     )(stacked)
 
 
-def reduce_pair(term, *after):
-    count = lax.axis_size("img")
-    rows = term.shape[0] // count
+def pair_send(blocks):
+    count, rows, cols = blocks.shape
     fast = lax.axis_index("img") % 2
-    pairs = term.reshape(count // 2, 2, rows, term.shape[1])
-    send = lax.dynamic_index_in_dim(pairs, 1 - fast, 1, keepdims=False)
-    keep = lax.dynamic_index_in_dim(pairs, fast, 1, keepdims=False)
-    got = tie(img_swap(send), *after) if after else img_swap(send)
-    return (keep.astype(F32) + got.astype(F32)).astype(BF16)
+    pairs = blocks.reshape(count // 2, 2, rows, cols)
+    return img_swap(lax.dynamic_index_in_dim(pairs, 1 - fast, 1, keepdims=False))
+
+
+def pair_sum(terms, gots):
+    count, rows = terms[0].shape[:2]
+    cols = [term.shape[2] for term in terms]
+
+    def body(where, ins, outs):
+        for k in range(count // 2):
+            at = 0
+            for j, size in enumerate(cols):
+                kept = ins[j][2 * k + where[0]].astype(F32)
+                total = kept + ins[len(cols) + j][k].astype(F32)
+                outs[0][k, :, at : at + size] = total.astype(BF16)
+                at += size
+
+    fast = lax.axis_index("img") % 2
+    shape = (count // 2, rows, sum(cols))
+    return arrange(body, [(shape, BF16)], *terms, *gots, place=fast)[0]
 
 
 def slow_exchange(parts):
@@ -624,17 +639,18 @@
 
     grad_second = (product(grad_aligned, third_w) * second_slope).astype(BF16)
     third_blocks = [
-        product_tn(grad_aligned[:, p * zd_part : (p + 1) * zd_part], second_low, BF16)
+        product_tn(second_low, grad_aligned[:, p * zd_part : (p + 1) * zd_part], BF16)
         for p in range(SEQ)
     ]
     grad_seconds = gather_rows(grad_second)
+    third_sum = scatter_blocks(third_blocks, grad_seconds[1]).astype(BF16)
     grad_firsts, sums = [], []
     for side in range(2):
         rows = grad_seconds[side] if side == 0 else tie(grad_seconds[1], sums[0], *third_blocks)
         grad = product_nt(rows, second_w) * first_slopes[side]
         grad_firsts.append(grad.astype(BF16))
         sums.append(product_nt(grad_firsts[side], first_w, BF16))
-    first_acts = tie(jnp.concatenate(first_acts, 0), sums[1])
+    first_acts = tie(jnp.concatenate(first_acts, 0), sums[1], third_sum)
     second_term = product_tn(first_acts, jnp.concatenate(grad_seconds, 0), BF16)
     second_sum = lax.psum_scatter(second_term, "img", scatter_dimension=0, tiled=True)
     grad_first = jnp.concatenate(grad_firsts, 0)
@@ -645,8 +661,17 @@
 
     grad_branch_b = (gate_b * grad_result).astype(BF16)
     grad_branches = gather_rows(grad_branch_b)
-    third_sum = scatter_blocks([tie(block, grad_branches[1]) for block in third_blocks])
-    third_sum = third_sum.astype(BF16)
+
+    def pack_third(where, ins, outs):
+        for i in range(img):
+            for side in range(2):
+                first = (2 * i + side) * third_rows
+                at = side * zd_part
+                outs[0][i, :third_rows, at : at + zd_part] = ins[0][first : first + third_rows]
+
+    third_shape = (img, feat, 2 * zd_part)
+    third_blocks = arrange(pack_third, [(third_shape, BF16)], third_sum)[0]
+    third_half = pair_send(third_blocks)
     grad_pres, sums = [], []
     for side in range(2):
         rows = grad_branches[side] if side == 0 else tie(grad_branches[1], sums[0], first_got)
@@ -658,17 +683,23 @@
     down_sum = lax.psum_scatter(down_term, "img", scatter_dimension=0, tiled=True)
     grad_pre = jnp.concatenate(grad_pres, 0)
     up_term = product_tn(tie(jnp.concatenate(hidden_b, 0), sums[1]), grad_pre, BF16)
-    up_pair = reduce_pair(up_term)
-    grad_hidden_b = tie(scatter_rows(*sums), down_term, up_term, third_sum)
+    up_blocks = up_term.reshape(img, feat, ff_part)
+    up_half = pair_send(up_blocks)
+    grad_hidden_b = tie(scatter_rows(*sums), down_term, up_term)
     grad_after = grad_result + norm_back(normed_b, inverse_b, grad_hidden_b * (1.0 + scale_b))
 
     grad_branch_a = (gate_a * grad_after).astype(BF16)
-    grad_attended = product_nt(tie(grad_branch_a, up_pair), attn_w, BF16)
+    grad_attended = product_nt(grad_branch_a, attn_w, BF16)
     grad_parts = split_columns(grad_attended, place)
     grad_heads = [grad_parts[0]] + [swap(grad_parts[p], p) for p in range(1, SEQ)]
     branch_cols = split_columns(grad_branch_a, place)
     attended = tie(attended, *grad_parts)
-    attn_sum = scatter_blocks([product_tn(attended, cols, BF16) for cols in branch_cols])
+    attn_sum = scatter_blocks(
+        [product_tn(attended, cols, BF16) for cols in branch_cols]
+    ).astype(BF16)
+    attn_sum = attn_sum.reshape(img, feat, part_width)
+    attn_half = pair_send(attn_sum)
+    up_pair = pair_sum([up_blocks, third_blocks], [tie(up_half, *grad_parts), third_half])
     up_got = slow_exchange(tie(up_pair, first_got))
 
     def rows_in_order(where, ins, outs):
@@ -678,9 +709,7 @@
     grad_heads = arrange(rows_in_order, [(chunk, BF16)], *grad_heads, place=distance)[0]
     grad_heads = grad_heads.reshape(SEQ * own_rows, part_width)
     grad_joined = attend_backward(qkv, grad_heads, all_slots)
-    third_send = third_sum.reshape(zd_part, img, ph // img).transpose(1, 0, 2)
-    third_got = img_exchange(tie(third_send, up_got))
-    grad_joined = tie(grad_joined, up_got).reshape(joined)
+    grad_joined = tie(grad_joined, attn_sum).reshape(joined)
 
     def cut_back(where, ins, outs):
         for turn in range(3):
@@ -696,7 +725,7 @@
 
     backs = arrange(cut_back, [(wide, BF16)] * 3, grad_joined, place=place % 3)
     backs = [lax.ppermute(backs[j], "seq", [(b, a) for a, b in turns[j]]) for j in range(3)]
-    backs = [tie(back, third_got) for back in backs]
+    backs = [tie(back, up_got) for back in backs]
 
     def join_back(where, ins, outs):
         for turn in range(SEQ):
@@ -713,12 +742,10 @@
 
     grad_qkv = arrange(join_back, [(qkv_own.shape, BF16)], *backs, place=place)[0]
     far = product_nt(grad_qkv[2 * own_rows :], qkv_w, BF16)
-    near = product_nt(tie(grad_qkv, far)[: 2 * own_rows], qkv_w, BF16)
+    qkv_term = product_tn(tie(hidden_a, far), grad_qkv, BF16)
+    near = product_nt(tie(grad_qkv, qkv_term)[: 2 * own_rows], qkv_w, BF16)
     grad_hidden_a = scatter_rows(near, far)
-    qkv_term = product_tn(tie(hidden_a, near), grad_qkv, BF16)
-    attn_send = attn_sum.astype(BF16).reshape(img, feat, part_width)
-    attn_got = img_exchange(tie(attn_send, third_got))
-    grad_hidden_a = tie(grad_hidden_a, attn_got)
+    qkv_blocks = qkv_term.reshape(img, feat, 3 * part_width)
     normed_a, inverse_a = norm_parts(tokens_f)
     tokens_grad = grad_after + norm_back(normed_a, inverse_a, grad_hidden_a * (1.0 + scale_a))
 
@@ -740,6 +767,32 @@
         column_sums(grad_second).reshape(SEQ, ph_part),
         jnp.stack([pick(aligned_sums, place ^ j) for j in range(SEQ)]),
     ]
+    by_place = jnp.concatenate(by_place, axis=1)
+    seq_got = seq_exchange(by_place)
+    qkv_half = tie(pair_send(qkv_blocks), seq_got)
+    qkv_pair = pair_sum([qkv_blocks, attn_sum], [qkv_half, attn_half])
+    member = (all_slots[None, :] == jnp.arange(slot_count, dtype=jnp.int32)[:, None]).astype(F32)
+    grad_mod = jnp.sum(member[:, :, None] * seq_got[None, :, :mod_cols], axis=1)
+    row_biases = jnp.sum(seq_got[:, mod_cols:], axis=0)
+    bias_sums = jnp.concatenate(
+        [
+            row_biases,
+            column_sums(grad_qkv),
+            column_sums(grad_pre),
+            column_sums(grad_first),
+        ]
+    )
+    mod_size = slot_count * mod_cols
+    leading = lax.reduce_precision(bias_sums, 8, 7)
+    rest = bias_sums - leading
+    packed = [grad_mod.reshape(mod_size), leading, rest]
+    img_got = img_gather(jnp.concatenate([part.astype(BF16) for part in packed]))
+    grad_mods = img_got[:, :mod_size].reshape(img * slot_count, mod_cols)
+    bias_pairs = img_got[:, mod_size:].astype(F32).reshape(img * 2, bias_sums.shape[0])
+    bias_sums = jnp.sum(bias_pairs, axis=0)
+    ada_weight_grad = product_tn(cond_cols, grad_mods)
+    cond_parts = product_nt(grad_mods, ada_weight).reshape(img, slot_count, feat)
+    cond_parts = img_exchange(cond_parts).transpose(1, 0, 2).reshape(slot_count * width)
     def split_sums(where, ins, outs):
         for d in range(SEQ):
             at = d * part_width
@@ -759,33 +812,21 @@
                 outs[0][d, rows, second_at:] = ins[3][:, at : at + half]
 
     hidden_send = arrange(
-        split_sums, [((SEQ, feat, hidden_cols), BF16)], up_got, down_sum, first_got, second_sum
+        split_sums, [((SEQ, feat, hidden_cols), BF16)], tie(up_got, near), down_sum, first_got, second_sum
     )[0]
-    hidden_got = seq_exchange(tie(hidden_send, attn_got))
-
-    by_place = jnp.concatenate(by_place, axis=1)
-    seq_got = seq_exchange(tie(by_place, hidden_got))
-    qkv_pair = reduce_pair(qkv_term, seq_got)
-    member = (all_slots[None, :] == jnp.arange(slot_count, dtype=jnp.int32)[:, None]).astype(F32)
-    grad_mod = jnp.sum(member[:, :, None] * seq_got[None, :, :mod_cols], axis=1)
-    grad_mod = grad_mod.astype(BF16).astype(F32)
-    row_biases = jnp.sum(seq_got[:, mod_cols:], axis=0)
-    bias_sums = jnp.concatenate(
-        [
-            row_biases,
-            column_sums(grad_qkv),
-            column_sums(grad_pre),
-            column_sums(grad_first),
-        ]
-    )
-    mod_size = slot_count * mod_cols
-    img_got = img_gather(jnp.concatenate([grad_mod.reshape(mod_size), bias_sums]))
-    grad_mods = img_got[:, :mod_size].reshape(img * slot_count, mod_cols).astype(BF16)
-    bias_sums = jnp.sum(img_got[:, mod_size:], axis=0)
-    ada_weight_grad = product_tn(cond_cols, grad_mods)
-    cond_parts = product_nt(grad_mods, ada_weight).reshape(img, slot_count, feat)
-    qkv_weight_grad = slow_scatter(qkv_pair, img_got)
-    cond_parts = img_exchange(cond_parts).transpose(1, 0, 2).reshape(slot_count * width)
+    hidden_got = [swap(pick(hidden_send, place ^ p), p) for p in range(1, SEQ)]
+    hidden_got = [pick(hidden_send, place)] + hidden_got
+
+    def in_order(where, ins, outs):
+        for p in range(SEQ):
+            outs[0][where[p]] = ins[p][...]
+
+    hidden_got = [tie(block, img_got) for block in hidden_got]
+    hidden_got = arrange(in_order, [(hidden_send.shape, BF16)], *hidden_got, place=distance)[0]
+
+    qkv_attn_grad = slow_scatter(qkv_pair, cond_parts)
+    qkv_weight_grad = qkv_attn_grad[:, : 3 * part_width]
+    attn_weight_grad = qkv_attn_grad[:, 3 * part_width :]
     last = jnp.concatenate([column_sums(grad_mods), bias_sums, cond_parts])
     last = jnp.pad(last, (0, -last.shape[0] % 1024))
     last = lax.all_gather(last, "seq", axis=0, tiled=False)
@@ -830,8 +871,16 @@
     )
     down_weight_grad = down_weight_grad.reshape(ff // img, part_width)
     second_proj_grad = second_proj_grad.reshape(ph // img, ph_part)
-    third_proj_grad = block_sum(third_got).T
-    attn_weight_grad = block_sum(attn_got)
+
+    def open_third(where, ins, outs):
+        for side in range(2):
+            at = ff_part + side * zd_part
+            total = ins[0][0, :third_rows, at : at + zd_part].astype(F32)
+            for k in range(1, img // 2):
+                total = total + ins[0][k, :third_rows, at : at + zd_part].astype(F32)
+            outs[0][side * third_rows : (side + 1) * third_rows] = total
+
+    third_proj_grad = arrange(open_third, [(third_proj.shape, F32)], tie(up_got, img_got))[0]
     return (
         feed_low,
         tokens_grad,

time: 727 us -> 689 us (0.948)
  waiting for transfers between devices: 241 us -> 193 us
  Pallas kernels: 97.3 us -> 123 us
  starting transfers between devices: 114 us -> 104 us
    all_to_all x1, waiting for transfers between devices: 31.3 us -> 0.01 us  [slow_exchange(): lax.all_to_all(parts, 'img', split_axis=0, concat_axis=0, tiled=True, axi...]
    pallas_call x17 -> x22, Pallas kernels: 49.9 us -> 76.3 us  [arrange(): pl.pallas_call(kernel, grid_spec=pltpu.PrefetchScalarGridSpec(num_scalar_...]
    all_to_all x3 -> x2, waiting for transfers between devices: 27.8 us -> 17.9 us  [seq_exchange(): return lax.all_to_all(parts, 'seq', split_axis=0, concat_axis=0, tiled=True)]
    ppermute x6, waiting for transfers between devices: 21.6 us -> 12.2 us  [slow_swap(): lax.ppermute(values, 'img', [(i, i ^ 2 * distance) for i in range(count)])]
    all_to_all x7 -> x5, starting transfers between devices: 36.1 us -> 28.4 us  [img_exchange(): return lax.all_to_all(parts, 'img', split_axis=0, concat_axis=0, tiled=True)]
    all_to_all x7 -> x5, waiting for transfers between devices: 16.5 us -> 10.9 us  [img_exchange(): return lax.all_to_all(parts, 'img', split_axis=0, concat_axis=0, tiled=True)]
    ppermute x6 -> x8, waiting for transfers between devices: 17.5 us -> 23 us  [img_swap(): return lax.ppermute(values, 'img', [(i, i ^ 1) for i in range(count)])]
    ppermute x48 -> x51, starting transfers between devices: 29.3 us -> 33 us  [swap(): return lax.ppermute(values, 'seq', [(i, i ^ distance) for i in range(SEQ)])]
  transfers between devices with their start and end apart: 82 -> 84, of which waited for: 28 -> 27; matrix products, arithmetic and copies ran while one was open for 29% -> 30% of each run, Pallas kernels for 14% -> 18%
where the time goes in v3:
time: 689 us; the launch traced here: 682 us
  waiting for transfers between devices  193 us (28%)
  Pallas kernels  123 us (18%)
  matrix products  112 us (16%)
  starting transfers between devices  104 us (15%)
  other arithmetic  62.5 us (9%)
  local copies, waits for them, and re-layouts  60 us (9%)
  between operations  15.7 us (2%)
  blocking collectives  10.9 us (2%)
    ppermute x51, waiting for transfers between devices, swap(): return lax.ppermute(values, 'seq', [(i, i ^ distance) for i in range(SEQ)])  117 us
    pallas_call x22, Pallas kernels, arrange(): pl.pallas_call(kernel, grid_spec=pltpu.PrefetchScalarGridSpec(num_scalar_...  76.3 us
    dot_general x12, matrix products, product(): lax.dot_general(left, right, (((1,), (0,)), ((), ())), preferred_element_...  38.9 us
    dot_general x13, matrix products, product_nt(): lax.dot_general(left, right, (((1,), (1,)), ((), ())), preferred_element_...  38.7 us
    dot_general x14, matrix products, product_tn(): lax.dot_general(left, right, (((0,), (0,)), ((), ())), preferred_element_...  34.4 us
    ppermute x51, starting transfers between devices, swap(): return lax.ppermute(values, 'seq', [(i, i ^ distance) for i in range(SEQ)])  33 us
    all_to_all x5, starting transfers between devices, img_exchange(): return lax.all_to_all(parts, 'img', split_axis=0, concat_axis=0, tiled=True)  28.4 us
    pallas_call x1, Pallas kernels, attend_backward(): pl.pallas_call(attend_back_kernel, grid_spec=pltpu.PrefetchScalarGridSpec...  24.6 us
  transfers between devices with their start and end apart: 84, of which 27 were waited for; matrix products, arithmetic and copies ran while one was open for 30% of the time, Pallas kernels for 18%

profile of v3, /device:TPU:0, one launch (start us, length us, event | category | flops | bytes accessed | tf_op | source)
XLA Modules:
  0.0 681.9 jit_solution(13075229369585599155)
XLA Ops:
  9.4 7.3 %all-to-all-start = ((bf16[8,4,144]{2,1,0:T(4,128)(2,1)}), bf16[8,4,144]{2,1,0:T(4,128)(2,1)S(1)}, u32[]{:S(2)}, u32[]{:S(2)}) async-start(bf16[8,4,144]{2,1,0:T(4,128)(2,1)} %copy.176), calls=%async_computation | async-start | bytes 32768 | tf_op jit(solution)/shard_map/all_to_all | solution.py:259
  33.2 5.9 all-to-all-done.1
  55.4 14.2 %all-to-all-done.2.refs_0_ = bf16[4,144,960]{2,1,0:T(8,128)(2,1)} async-done(((bf16[4,144,960]{2,1,0:T(8,128)(2,1)}), bf16[4,144,960]{2,1,0:T(8,128)(2,1)}, u32[]{:S(2)}, u32[]{:S(2)}) %all-to-all-start.2) | async-done | bytes 1105952 | tf_op jit(solution)/shard_map/all_to_all | solution.py:255
  80.8 11.2 %collective-permute-done.7.refs_4_ = bf16[144,288]{1,0:T(8,128)(2,1)} collective-permute-done((bf16[144,288]{1,0:T(8,128)(2,1)}, bf16[144,288]{1,0:T(8,128)(2,1)}, u32[]{:S(2)}, u32[]{:S(2)}) %collective-permute-start.7) | collective-permute-done | bytes 82976 | tf_op jit(solution)/shard_map/ppermute | solution.py:110
  107.2 6.4 add_convert_fusion.refs_0_
  134.3 15.9 %attend.1 = bf16[1024,288]{1,0:T(8,128)(2,1)} custom-call(s32[4]{0:T(128)} %copy-done.94, bf16[1024,864]{1,0:T(8,128)(2,1)} %bitcast.149), custom_call_target="tpu_custom_call" | custom-call | flops 2415919104 | bytes 2359296 | tf_op jit(solution)/shard_map/attend/pallas_call | solution.py:340
  165.1 13.2 %arrange.27 = bf16[256,1152]{1,0:T(8,128)(2,1)} custom-call(s32[1]{0:T(128)} %bitcast.5.where, bf16[256,288]{1,0:T(8,128)(2,1)} %get-tuple-element.96.refs_0_, bf16[256,288]{1,0:T(8,128)(2,1)} %copy-done.64, bf16[256,288]{1,0:T(8,128)(2,1)} %copy-done.65, bf16[256,288]{1,0:T(8,128)(2,1)} %copy-done.66), custom_call_target="tpu_custom_call" | custom-call | tf_op jit(solution)/shard_map/arrange/pallas_call | solution.py:127
  185.2 13.7 %collective-permute-done.21 = bf16[256,1152]{1,0:T(8,128)(2,1)S(1)} collective-permute-done((bf16[256,1152]{1,0:T(8,128)(2,1)S(1)}, bf16[256,1152]{1,0:T(8,128)(2,1)S(1)}, u32[]{:S(2)}, u32[]{:S(2)}) %collective-permute-start.21) | collective-permute-done | bytes 589856 | tf_op jit(solution)/shard_map/ppermute | solution.py:73
  201.1 5.4 multiply_convert_fusion
  217.4 13.7 %collective-permute-done.24 = bf16[256,1152]{1,0:T(8,128)(2,1)S(1)} collective-permute-done((bf16[256,1152]{1,0:T(8,128)(2,1)S(1)}, bf16[256,1152]{1,0:T(8,128)(2,1)S(1)}, u32[]{:S(2)}, u32[]{:S(2)}) %collective-permute-start.24) | collective-permute-done | bytes 589856 | tf_op jit(solution)/shard_map/ppermute | solution.py:73
  233.3 12.9 %collective-permute-done.27 = bf16[256,1152]{1,0:T(8,128)(2,1)S(1)} collective-permute-done((bf16[256,1152]{1,0:T(8,128)(2,1)S(1)}, bf16[256,1152]{1,0:T(8,128)(2,1)S(1)}, u32[]{:S(2)}, u32[]{:S(2)}) %collective-permute-start.27) | collective-permute-done | bytes 589856 | tf_op jit(solution)/shard_map/ppermute | solution.py:73
  246.4 6.6 open_blocks.1
  287.6 18.1 %collective-permute-done.30 = bf16[256,2048]{1,0:T(8,128)(2,1)} collective-permute-done((bf16[256,2048]{1,0:T(8,128)(2,1)}, bf16[256,2048]{1,0:T(8,128)(2,1)}, u32[]{:S(2)}, u32[]{:S(2)}) %collective-permute-start.30) | collective-permute-done | bytes 1048608 | tf_op jit(solution)/shard_map/ppermute | solution.py:73
  322.8 19.5 %collective-permute-done.36 = bf16[256,2048]{1,0:T(8,128)(2,1)S(1)} collective-permute-done((bf16[256,2048]{1,0:T(8,128)(2,1)S(1)}, bf16[256,2048]{1,0:T(8,128)(2,1)S(1)}, u32[]{:S(2)}, u32[]{:S(2)}) %collective-permute-start.36) | collective-permute-done | bytes 1048608 | tf_op jit(solution)/shard_map/ppermute | solution.py:73
  360.8 6.9 %all-to-all-start.3 = ((bf16[8,144,512]{2,1,0:T(8,128)(2,1)}), bf16[8,144,512]{2,1,0:T(8,128)(2,1)}, u32[]{:S(2)}, u32[]{:S(2)}) async-start(bf16[8,144,512]{2,1,0:T(8,128)(2,1)} %bitcast.153), calls=%async_computation.3 | async-start | bytes 2359296 | tf_op jit(solution)/shard_map/all_to_all | solution.py:259
  438.6 6.2 convolution_convert_fusion.1
  444.8 7.8 %collective-permute-done.48 = bf16[256,1152]{1,0:T(8,128)(2,1)} collective-permute-done((bf16[256,1152]{1,0:T(8,128)(2,1)}, bf16[256,1152]{1,0:T(8,128)(2,1)}, u32[]{:S(2)}, u32[]{:S(2)}) %collective-permute-start.48) | collective-permute-done | bytes 589856 | tf_op jit(solution)/shard_map/ppermute | solution.py:73
  497.2 24.6 %attend_back.1 = bf16[1024,864]{1,0:T(8,128)(2,1)} custom-call(s32[4]{0:T(128)} %copy-done.94, bf16[1024,864]{1,0:T(8,128)(2,1)} %bitcast.150, bf16[1024,288]{1,0:T(8,128)(2,1)} %bitcast.162), custom_call_target="tpu_custom_call" | custom-call | flops 4831838208 | bytes 4718592 | tf_op jit(solution)/shard_map/attend_back/pallas_call | solution.py:358
  539.5 7.0 %collective-permute-done.59.refs_2_ = bf16[256,1152]{1,0:T(8,128)(2,1)} collective-permute-done((bf16[256,1152]{1,0:T(8,128)(2,1)}, bf16[256,1152]{1,0:T(8,128)(2,1)}, u32[]{:S(2)}, u32[]{:S(2)}) %collective-permute-start.59) | collective-permute-done | bytes 589856 | tf_op jit(solution)/shard_map/ppermute | solution.py:727
  595.5 5.4 all-to-all-start.6
  600.9 14.1 %collective-permute-done.63.refs_2_ = bf16[4,144,864]{2,1,0:T(8,128)(2,1)} collective-permute-done((bf16[4,144,864]{2,1,0:T(8,128)(2,1)}, bf16[4,144,864]{2,1,0:T(8,128)(2,1)}, u32[]{:S(2)}, u32[]{:S(2)}) %collective-permute-start.63) | collective-permute-done | bytes 995360 | tf_op jit(solution)/shard_map/ppermute | solution.py:105
  632.5 5.4 all-to-all-start.7
  640.5 6.9 %collective-permute-done.70.refs_3_ = bf16[144,960]{1,0:T(8,128)(2,1)} collective-permute-done((bf16[144,960]{1,0:T(8,128)(2,1)}, bf16[144,960]{1,0:T(8,128)(2,1)}, u32[]{:S(2)}, u32[]{:S(2)}) %collective-permute-start.70) | collective-permute-done | bytes 276512 | tf_op jit(solution)/shard_map/ppermute | solution.py:73
  662.9 5.5 all-gather
  (604 shorter events, 412.2 us)
Async XLA Ops:
  7.2 100.0 %all-gather.6.cloned.1.call-start = ((), (), s32[]{:S(2)}) async-start(), calls=%async_computation.10 | async-start | bytes 2322432 | tf_op jit(solution)/shard_map/all_gather | solution.py:427
  53.7 147.3 %all-gather.8.cloned.1.call-start = ((), (), s32[]{:S(2)}) async-start(), calls=%async_computation.11 | async-start | bytes 5971968 | tf_op jit(solution)/shard_map/all_gather | solution.py:489
  72.5 173.9 %all-gather.10.cloned.1.call-start = ((), (), s32[]{:S(2)}) async-start(), calls=%async_computation.12 | async-start | bytes 4976640 | tf_op jit(solution)/shard_map/all_gather | solution.py:491
  122.8 33.5 %collective-permute-start.13 = (bf16[8,144,288]{2,1,0:T(8,128)(2,1)S(1)}, bf16[8,144,288]{2,1,0:T(8,128)(2,1)S(1)}, u32[]{:S(2)}, u32[]{:S(2)}) collective-permute-start(bf16[8,144,288]{2,1,0:T(8,128)(2,1)S(1)} %copy-done.11), channel_id=1, source_target_pairs={{0,1},{1,0},{2,3},{3,2},{4,5},{5,4},{6,7},{7,6},{8,9},{9,8},{10,11... | collective-permute-start | bytes 1990664 | tf_op jit(solution)/shard_map/ppermute | solution.py:73
  125.6 30.7 %collective-permute-start.15 = (bf16[8,144,288]{2,1,0:T(8,128)(2,1)}, bf16[8,144,288]{2,1,0:T(8,128)(2,1)}, u32[]{:S(2)}, u32[]{:S(2)}) collective-permute-start(bf16[8,144,288]{2,1,0:T(8,128)(2,1)} %collective-permute-done.14.refs_2_), channel_id=1, source_target_pairs={{0,1},{1,0},{2,3},{3,2},{4,5},{5,4},{6,7},{7,6},{8,9},{9,8},{10,11... | collective-permute-start | bytes 1990664 | tf_op jit(solution)/shard_map/ppermute | solution.py:73
  274.5 31.2 %collective-permute-start.30 = (bf16[256,2048]{1,0:T(8,128)(2,1)}, bf16[256,2048]{1,0:T(8,128)(2,1)}, u32[]{:S(2)}, u32[]{:S(2)}) collective-permute-start(bf16[256,2048]{1,0:T(8,128)(2,1)} %add_convert_fusion.2), channel_id=1, source_target_pairs={{0,2},{1,3},{2,0},{3,1},{4,6},{5,7},{6,4},{7,5},{8,10},{9,11},{10,... | collective-permute-start | bytes 3145736 | tf_op jit(solution)/shard_map/ppermute | solution.py:73
  279.1 29.0 %collective-permute-start.31 = (bf16[192,2048]{1,0:T(8,128)(2,1)}, bf16[192,2048]{1,0:T(8,128)(2,1)S(1)}, u32[]{:S(2)}, u32[]{:S(2)}) collective-permute-start(bf16[192,2048]{1,0:T(8,128)(2,1)} %bitcast.159), channel_id=1, source_target_pairs={{0,1},{1,0},{2,3},{3,2},{4,5},{5,4},{6,7},{7,6},{8,9},{9,8},{10,11... | collective-permute-start | bytes 2359304 | tf_op jit(solution)/shard_map/ppermute | solution.py:73
  319.7 30.2 %collective-permute-start.41 = (bf16[2048,192]{0,1:T(8,128)(2,1)S(1)}, bf16[2048,192]{0,1:T(8,128)(2,1)S(1)}, u32[]{:S(2)}, u32[]{:S(2)}) collective-permute-start(bf16[2048,192]{0,1:T(8,128)(2,1)S(1)} %convolution_convert_fusion.20), channel_id=1, source_target_pairs={{0,1},{1,0},{2,3},{3,2},{4,5},{5,4},{6,7},{7,6},{8,9},{9,8},{10,11... | collective-permute-start | bytes 2359304 | tf_op jit(solution)/shard_map/ppermute | solution.py:73
  320.8 30.3 %collective-permute-start.40 = (bf16[2048,192]{0,1:T(8,128)(2,1)S(1)}, bf16[2048,192]{0,1:T(8,128)(2,1)}, u32[]{:S(2)}, u32[]{:S(2)}) collective-permute-start(bf16[2048,192]{0,1:T(8,128)(2,1)S(1)} %convolution_convert_fusion.22), channel_id=1, source_target_pairs={{0,1},{1,0},{2,3},{3,2},{4,5},{5,4},{6,7},{7,6},{8,9},{9,8},{10,11... | collective-permute-start | bytes 2359304 | tf_op jit(solution)/shard_map/ppermute | solution.py:73
  354.5 31.5 %collective-permute-start.35 = (bf16[256,1152]{1,0:T(8,128)(2,1)}, bf16[256,1152]{1,0:T(8,128)(2,1)}, u32[]{:S(2)}, u32[]{:S(2)}) collective-permute-start(bf16[256,1152]{1,0:T(8,128)(2,1)} %slice.247), channel_id=1, source_target_pairs={{0,1},{1,0},{2,3},{3,2},{4,5},{5,4},{6,7},{7,6},{8,9},{9,8},{10,11... | collective-permute-start | bytes 1769480 | tf_op jit(solution)/shard_map/ppermute | solution.py:73
  360.8 60.1 %all-to-all-start.3 = ((bf16[8,144,512]{2,1,0:T(8,128)(2,1)}), bf16[8,144,512]{2,1,0:T(8,128)(2,1)}, u32[]{:S(2)}, u32[]{:S(2)}) async-start(bf16[8,144,512]{2,1,0:T(8,128)(2,1)} %bitcast.153), calls=%async_computation.3 | async-start | bytes 2359296 | tf_op jit(solution)/shard_map/all_to_all | solution.py:259
  367.7 256.9 %reduce-scatter.5.cloned.1.call-start = ((), (), s32[]{:S(2)}) async-start(), calls=%async_computation.14 | async-start | bytes 2359296 | tf_op jit(solution)/shard_map/reduce_scatter | solution.py:655
  402.0 70.9 %collective-permute-start.57 = (bf16[4,144,384]{2,1,0:T(8,128)(2,1)}, bf16[4,144,384]{2,1,0:T(8,128)(2,1)}, u32[]{:S(2)}, u32[]{:S(2)}) collective-permute-start(bf16[4,144,384]{2,1,0:T(8,128)(2,1)} %dynamic-slice_bitcast_fusion.3), channel_id=1, source_target_pairs={{0,4},{4,0},{8,12},{12,8},{16,20},{20,16},{24,28},{28,24},{1,5},{5... | collective-permute-start | bytes 1327112 | tf_op jit(solution)/shard_map/ppermute | solution.py:105
  435.2 37.8 %collective-permute-start.56 = (bf16[4,144,1152]{2,1,0:T(8,128)(2,1)}, bf16[4,144,1152]{2,1,0:T(8,128)(2,1)}, u32[]{:S(2)}, u32[]{:S(2)}) collective-permute-start(bf16[4,144,1152]{2,1,0:T(8,128)(2,1)} %dynamic-slice_bitcast_fusion), channel_id=1, source_target_pairs={{0,4},{4,0},{8,12},{12,8},{16,20},{20,16},{24,28},{28,24},{1,5},{5... | collective-permute-start | bytes 3981320 | tf_op jit(solution)/shard_map/ppermute | solution.py:105
  477.2 62.3 %all-to-all-start.4 = ((bf16[4,144,1536]{2,1,0:T(8,128)(2,1)}), bf16[4,144,1536]{2,1,0:T(8,128)(2,1)S(1)}, u32[]{:S(2)}, u32[]{:S(2)}) async-start(bf16[4,144,1536]{2,1,0:T(8,128)(2,1)} %arrange.37), calls=%async_computation.4 | async-start | bytes 3538944 | tf_op jit(solution)/shard_map/all_to_all | solution.py:236
  482.3 142.3 %reduce-scatter.3.cloned.1.call-start = ((), (), s32[]{:S(2)}) async-start(), calls=%async_computation.13 | async-start | bytes 2985984 | tf_op jit(solution)/shard_map/reduce_scatter | solution.py:683
  486.9 34.9 %collective-permute-start.52 = (bf16[1152,288]{0,1:T(8,128)(2,1)}, bf16[1152,288]{0,1:T(8,128)(2,1)}, u32[]{:S(2)}, u32[]{:S(2)}) collective-permute-start(bf16[1152,288]{0,1:T(8,128)(2,1)} %convolution_convert_fusion.16), channel_id=1, source_target_pairs={{0,1},{1,0},{2,3},{3,2},{4,5},{5,4},{6,7},{7,6},{8,9},{9,8},{10,11... | collective-permute-start | bytes 1990664 | tf_op jit(solution)/shard_map/ppermute | solution.py:73
  489.6 32.2 %collective-permute-start.54 = (bf16[1152,288]{0,1:T(8,128)(2,1)}, bf16[1152,288]{0,1:T(8,128)(2,1)}, u32[]{:S(2)}, u32[]{:S(2)}) collective-permute-start(bf16[1152,288]{0,1:T(8,128)(2,1)} %add_convert_fusion.5), channel_id=1, source_target_pairs={{0,2},{1,3},{2,0},{3,1},{4,6},{5,7},{6,4},{7,5},{8,10},{9,11},{10,... | collective-permute-start | bytes 1990664 | tf_op jit(solution)/shard_map/ppermute | solution.py:73
  567.6 47.4 %collective-permute-start.64 = (bf16[4,144,288]{2,1,0:T(8,128)(2,1)}, bf16[4,144,288]{2,1,0:T(8,128)(2,1)}, u32[]{:S(2)}, u32[]{:S(2)}) collective-permute-start(bf16[4,144,288]{2,1,0:T(8,128)(2,1)} %dynamic-slice_bitcast_fusion.2), channel_id=1, source_target_pairs={{0,4},{4,0},{8,12},{12,8},{16,20},{20,16},{24,28},{28,24},{1,5},{5... | collective-permute-start | bytes 995336 | tf_op jit(solution)/shard_map/ppermute | solution.py:105
  572.4 42.5 %collective-permute-start.63 = (bf16[4,144,864]{2,1,0:T(8,128)(2,1)}, bf16[4,144,864]{2,1,0:T(8,128)(2,1)}, u32[]{:S(2)}, u32[]{:S(2)}) collective-permute-start(bf16[4,144,864]{2,1,0:T(8,128)(2,1)} %dynamic-slice_bitcast_fusion.1), channel_id=1, source_target_pairs={{0,4},{4,0},{8,12},{12,8},{16,20},{20,16},{24,28},{28,24},{1,5},{5... | collective-permute-start | bytes 2985992 | tf_op jit(solution)/shard_map/ppermute | solution.py:105
  595.5 35.3 %all-to-all-start.6 = ((bf16[8,2,7264]{2,1,0:T(2,128)(2,1)}), bf16[8,2,7264]{2,1,0:T(2,128)(2,1)S(1)}, u32[]{:S(2)}, u32[]{:S(2)}) async-start(bf16[8,2,7264]{2,1,0:T(2,128)(2,1)} %reshape.462), calls=%async_computation.6 | async-start | bytes 466944 | tf_op jit(solution)/shard_map/all_to_all | solution.py:259
  620.1 39.9 %collective-permute-start.67 = (bf16[144,1152]{1,0:T(8,128)(2,1)S(1)}, bf16[144,1152]{1,0:T(8,128)(2,1)S(1)}, u32[]{:S(2)}, u32[]{:S(2)}) collective-permute-start(bf16[144,1152]{1,0:T(8,128)(2,1)S(1)} %get-tuple-element.347), channel_id=1, source_target_pairs={{0,24},{4,28},{8,16},{12,20},{16,8},{20,12},{24,0},{28,4},{1,25},{... | collective-permute-start | bytes 995336 | tf_op jit(solution)/shard_map/ppermute | solution.py:110
  623.9 36.1 %collective-permute-start.66 = (bf16[144,1152]{1,0:T(8,128)(2,1)S(1)}, bf16[144,1152]{1,0:T(8,128)(2,1)S(1)}, u32[]{:S(2)}, u32[]{:S(2)}) collective-permute-start(bf16[144,1152]{1,0:T(8,128)(2,1)S(1)} %get-tuple-element.348), channel_id=1, source_target_pairs={{0,16},{4,20},{8,24},{12,28},{16,0},{20,4},{24,8},{28,12},{1,17},{... | collective-permute-start | bytes 995336 | tf_op jit(solution)/shard_map/ppermute | solution.py:110
  623.9 36.1 %collective-permute-start.65 = (bf16[144,1152]{1,0:T(8,128)(2,1)S(1)}, bf16[144,1152]{1,0:T(8,128)(2,1)S(1)}, u32[]{:S(2)}, u32[]{:S(2)}) collective-permute-start(bf16[144,1152]{1,0:T(8,128)(2,1)S(1)} %get-tuple-element.346), channel_id=1, source_target_pairs={{0,8},{4,12},{8,0},{12,4},{16,24},{20,28},{24,16},{28,20},{1,9},{5... | collective-permute-start | bytes 995336 | tf_op jit(solution)/shard_map/ppermute | solution.py:110
  (166 other events, 1770.2 us)
Sparse Core Ops, SparseCore 0:
  10.2 55.6 all-gather.5
  72.6 87.7 all-gather.7
  162.6 74.4 all-gather.9
  400.3 76.5 reduce-scatter.4
  538.9 84.5 reduce-scatter.2

commit v4 on v3

--- a/solution.py
+++ b/solution.py
@@ -652,7 +652,8 @@
         sums.append(product_nt(grad_firsts[side], first_w, BF16))
     first_acts = tie(jnp.concatenate(first_acts, 0), sums[1], third_sum)
     second_term = product_tn(first_acts, jnp.concatenate(grad_seconds, 0), BF16)
-    second_sum = lax.psum_scatter(second_term, "img", scatter_dimension=0, tiled=True)
+    second_blocks = second_term.reshape(img, ph_cell, ph)
+    second_half = pair_send(second_blocks)
     grad_first = jnp.concatenate(grad_firsts, 0)
     first_term = product_tn(tie(jnp.concatenate(feed, 0), sums[1]), grad_first, BF16)
     first_got = img_exchange(first_term.reshape(img, feat, ph_part))
@@ -685,7 +686,9 @@
     up_term = product_tn(tie(jnp.concatenate(hidden_b, 0), sums[1]), grad_pre, BF16)
     up_blocks = up_term.reshape(img, feat, ff_part)
     up_half = pair_send(up_blocks)
-    grad_hidden_b = tie(scatter_rows(*sums), down_term, up_term)
+    second_pair = pair_sum([second_blocks], [tie(second_half, grad_branches[1])])
+    second_got = slow_exchange(tie(second_pair, first_got))
+    grad_hidden_b = tie(scatter_rows(*sums), down_term, up_term, second_pair)
     grad_after = grad_result + norm_back(normed_b, inverse_b, grad_hidden_b * (1.0 + scale_b))
 
     grad_branch_a = (gate_a * grad_after).astype(BF16)
@@ -700,7 +703,7 @@
     attn_sum = attn_sum.reshape(img, feat, part_width)
     attn_half = pair_send(attn_sum)
     up_pair = pair_sum([up_blocks, third_blocks], [tie(up_half, *grad_parts), third_half])
-    up_got = slow_exchange(tie(up_pair, first_got))
+    up_got = slow_exchange(tie(up_pair, second_got))
 
     def rows_in_order(where, ins, outs):
         for p in range(SEQ):
@@ -809,10 +812,13 @@
             for side in range(2):
                 rows = slice(side * ph_cell, (side + 1) * ph_cell)
                 at = (2 * d + side) * half
-                outs[0][d, rows, second_at:] = ins[3][:, at : at + half]
+                total = ins[3][0, :, at : at + half].astype(F32)
+                for k in range(1, img // 2):
+                    total = total + ins[3][k, :, at : at + half].astype(F32)
+                outs[0][d, rows, second_at:] = total.astype(BF16)
 
     hidden_send = arrange(
-        split_sums, [((SEQ, feat, hidden_cols), BF16)], tie(up_got, near), down_sum, first_got, second_sum
+        split_sums, [((SEQ, feat, hidden_cols), BF16)], tie(up_got, near), down_sum, first_got, second_got
     )[0]
     hidden_got = [swap(pick(hidden_send, place ^ p), p) for p in range(1, SEQ)]
     hidden_got = [pick(hidden_send, place)] + hidden_got

time: 689 us -> 682 us (0.990)
  waiting for transfers between devices: 193 us -> 166 us
  starting transfers between devices: 104 us -> 120 us
  local copies, waits for them, and re-layouts: 60 us -> 67.2 us
    ppermute x8 -> x9, waiting for transfers between devices: 23 us -> 3.72 us  [img_swap(): return lax.ppermute(values, 'img', [(i, i ^ 1) for i in range(count)])]
    ppermute x51, waiting for transfers between devices: 117 us -> 106 us  [swap(): return lax.ppermute(values, 'seq', [(i, i ^ distance) for i in range(SEQ)])]
    all_to_all x5, waiting for transfers between devices: 10.9 us -> 18.3 us  [img_exchange(): return lax.all_to_all(parts, 'img', split_axis=0, concat_axis=0, tiled=True)]
    pallas_call x22 -> x23, Pallas kernels: 76.3 us -> 69.3 us  [arrange(): pl.pallas_call(kernel, grid_spec=pltpu.PrefetchScalarGridSpec(num_scalar_...]
    unnamed x231 -> x234, local copies, waits for them, and re-layouts: 20.5 us -> 24.7 us
  transfers between devices with their start and end apart: 84 -> 85, of which waited for: 27 -> 25; matrix products, arithmetic and copies ran while one was open for 30% -> 31% of each run, Pallas kernels for 18% -> 17%
where the time goes in v4:
time: 682 us; the launch traced here: 670 us
  waiting for transfers between devices  166 us (24%)
  starting transfers between devices  120 us (18%)
  Pallas kernels  117 us (17%)
  matrix products  112 us (16%)
  local copies, waits for them, and re-layouts  67.2 us (10%)
  other arithmetic  60.1 us (9%)
  between operations  16 us (2%)
  blocking collectives  11 us (2%)
    ppermute x51, waiting for transfers between devices, swap(): return lax.ppermute(values, 'seq', [(i, i ^ distance) for i in range(SEQ)])  106 us
    pallas_call x23, Pallas kernels, arrange(): pl.pallas_call(kernel, grid_spec=pltpu.PrefetchScalarGridSpec(num_scalar_...  69.3 us
    dot_general x12, matrix products, product(): lax.dot_general(left, right, (((1,), (0,)), ((), ())), preferred_element_...  39.3 us
    dot_general x13, matrix products, product_nt(): lax.dot_general(left, right, (((1,), (1,)), ((), ())), preferred_element_...  38.4 us
    dot_general x14, matrix products, product_tn(): lax.dot_general(left, right, (((0,), (0,)), ((), ())), preferred_element_...  34.7 us
    ppermute x51, starting transfers between devices, swap(): return lax.ppermute(values, 'seq', [(i, i ^ distance) for i in range(SEQ)])  33 us
    all_to_all x5, starting transfers between devices, img_exchange(): return lax.all_to_all(parts, 'img', split_axis=0, concat_axis=0, tiled=True)  28.7 us
    unnamed x234, local copies, waits for them, and re-layouts  24.7 us
  transfers between devices with their start and end apart: 85, of which 25 were waited for; matrix products, arithmetic and copies ran while one was open for 31% of the time, Pallas kernels for 17%

profile of v4, /device:TPU:0, one launch (start us, length us, event | category | flops | bytes accessed | tf_op | source)
XLA Modules:
  0.0 669.7 jit_solution(12752592224350265199)
XLA Ops:
  9.4 7.3 %all-to-all-start = ((bf16[8,4,144]{2,1,0:T(4,128)(2,1)}), bf16[8,4,144]{2,1,0:T(4,128)(2,1)S(1)}, u32[]{:S(2)}, u32[]{:S(2)}) async-start(bf16[8,4,144]{2,1,0:T(4,128)(2,1)} %copy.183), calls=%async_computation | async-start | bytes 32768 | tf_op jit(solution)/shard_map/all_to_all | solution.py:259
  33.2 5.9 all-to-all-done.1
  41.6 5.4 all-gather.1
  55.4 14.2 %all-to-all-done.2.refs_0_ = bf16[4,144,960]{2,1,0:T(8,128)(2,1)} async-done(((bf16[4,144,960]{2,1,0:T(8,128)(2,1)}), bf16[4,144,960]{2,1,0:T(8,128)(2,1)}, u32[]{:S(2)}, u32[]{:S(2)}) %all-to-all-start.2) | async-done | bytes 1105952 | tf_op jit(solution)/shard_map/all_to_all | solution.py:255
  80.8 11.2 %collective-permute-done.7.refs_4_ = bf16[144,288]{1,0:T(8,128)(2,1)} collective-permute-done((bf16[144,288]{1,0:T(8,128)(2,1)}, bf16[144,288]{1,0:T(8,128)(2,1)}, u32[]{:S(2)}, u32[]{:S(2)}) %collective-permute-start.7) | collective-permute-done | bytes 82976 | tf_op jit(solution)/shard_map/ppermute | solution.py:110
  107.2 6.4 add_convert_fusion.refs_0_
  117.0 6.0 collective-permute-start.3
  138.4 15.8 %attend.1 = bf16[1024,288]{1,0:T(8,128)(2,1)} custom-call(s32[4]{0:T(128)} %copy-done.94, bf16[1024,864]{1,0:T(8,128)(2,1)} %bitcast.157), custom_call_target="tpu_custom_call" | custom-call | flops 2415919104 | bytes 2359296 | tf_op jit(solution)/shard_map/attend/pallas_call | solution.py:340
  178.1 13.7 %collective-permute-done.21 = bf16[256,1152]{1,0:T(8,128)(2,1)S(1)} collective-permute-done((bf16[256,1152]{1,0:T(8,128)(2,1)S(1)}, bf16[256,1152]{1,0:T(8,128)(2,1)S(1)}, u32[]{:S(2)}, u32[]{:S(2)}) %collective-permute-start.21) | collective-permute-done | bytes 589856 | tf_op jit(solution)/shard_map/ppermute | solution.py:73
  193.9 5.6 multiply_convert_fusion
  210.3 13.7 %collective-permute-done.24 = bf16[256,1152]{1,0:T(8,128)(2,1)S(1)} collective-permute-done((bf16[256,1152]{1,0:T(8,128)(2,1)S(1)}, bf16[256,1152]{1,0:T(8,128)(2,1)S(1)}, u32[]{:S(2)}, u32[]{:S(2)}) %collective-permute-start.24) | collective-permute-done | bytes 589856 | tf_op jit(solution)/shard_map/ppermute | solution.py:73
  226.0 12.9 %collective-permute-done.27 = bf16[256,1152]{1,0:T(8,128)(2,1)} collective-permute-done((bf16[256,1152]{1,0:T(8,128)(2,1)S(1)}, bf16[256,1152]{1,0:T(8,128)(2,1)}, u32[]{:S(2)}, u32[]{:S(2)}) %collective-permute-start.27) | collective-permute-done | bytes 589856 | tf_op jit(solution)/shard_map/ppermute | solution.py:73
  239.1 7.1 %open_blocks.1 = (bf16[8,144,512]{2,1,0:T(8,128)(2,1)}, bf16[8,64,2048]{2,1,0:T(8,128)(2,1)}, bf16[8,256,192]{2,1,0:T(8,128)(2,1)}) custom-call(bf16[8,144,1920]{2,1,0:T(8,128)(2,1)} %bitcast.156), custom_call_target="tpu_custom_call" | custom-call | tf_op jit(solution)/shard_map/open_blocks/pallas_call | solution.py:200
  281.0 18.0 %collective-permute-done.30 = bf16[256,2048]{1,0:T(8,128)(2,1)} collective-permute-done((bf16[256,2048]{1,0:T(8,128)(2,1)}, bf16[256,2048]{1,0:T(8,128)(2,1)}, u32[]{:S(2)}, u32[]{:S(2)}) %collective-permute-start.30) | collective-permute-done | bytes 1048608 | tf_op jit(solution)/shard_map/ppermute | solution.py:73
  315.9 19.5 %collective-permute-done.36 = bf16[256,2048]{1,0:T(8,128)(2,1)S(1)} collective-permute-done((bf16[256,2048]{1,0:T(8,128)(2,1)S(1)}, bf16[256,2048]{1,0:T(8,128)(2,1)S(1)}, u32[]{:S(2)}, u32[]{:S(2)}) %collective-permute-start.36) | collective-permute-done | bytes 1048608 | tf_op jit(solution)/shard_map/ppermute | solution.py:73
  354.8 7.1 %all-to-all-start.3 = ((bf16[8,144,512]{2,1,0:T(8,128)(2,1)}), bf16[8,144,512]{2,1,0:T(8,128)(2,1)}, u32[]{:S(2)}, u32[]{:S(2)}) async-start(bf16[8,144,512]{2,1,0:T(8,128)(2,1)} %bitcast.161), calls=%async_computation.3 | async-start | bytes 2359296 | tf_op jit(solution)/shard_map/all_to_all | solution.py:259
  434.9 6.7 all-to-all-start.4
  445.4 7.1 %convolution_convert_fusion.1 = bf16[1152,1152]{1,0:T(8,128)(2,1)} fusion(bf16[1024,1152]{1,0:T(8,128)(2,1)} %pad_maximum_fusion.3, bf16[256,1152]{1,0:T(8,128)(2,1)} %copy-done.54, bf16[256,1152]{1,0:T(8,128)(2,1)} %collective-permute-done.45, bf16[256,1152]{1,0:T(8,128)(2,1)} %collective-permute-done.43, bf16[256,1152]{1,0:T(8,128)(2,1)} %get-tuple-element.343), kind=kOutput, calls=%fused_computation.1 | convolution fusion | flops 2728673280 | bytes 7372800 | tf_op jit(solution)/shard_map/dot_general | solution.py:27
  452.6 6.7 collective-permute-done.48
  498.5 24.5 %attend_back.1 = bf16[1024,864]{1,0:T(8,128)(2,1)} custom-call(s32[4]{0:T(128)} %copy-done.94, bf16[1024,864]{1,0:T(8,128)(2,1)} %bitcast.158, bf16[1024,288]{1,0:T(8,128)(2,1)} %bitcast.170), custom_call_target="tpu_custom_call" | custom-call | flops 4831838208 | bytes 4718592 | tf_op jit(solution)/shard_map/attend_back/pallas_call | solution.py:358
  530.9 6.0 collective-permute-start.56
  599.1 5.8 all-to-all-start.7
  640.0 7.4 %all-to-all-done.8 = f32[8,4,144]{2,1,0:T(4,128)S(1)} async-done(((f32[8,4,144]{2,1,0:T(4,128)}), f32[8,4,144]{2,1,0:T(4,128)S(1)}, u32[]{:S(2)}, u32[]{:S(2)}) %all-to-all-start.8) | async-done | bytes 18464 | tf_op jit(solution)/shard_map/all_to_all | solution.py:259
  650.4 5.6 all-gather
  (610 shorter events, 414.2 us)
Async XLA Ops:
  7.2 100.0 %all-gather.6.cloned.1.call-start = ((), (), s32[]{:S(2)}) async-start(), calls=%async_computation.10 | async-start | bytes 2322432 | tf_op jit(solution)/shard_map/all_gather | solution.py:427
  53.7 140.1 %all-gather.8.cloned.1.call-start = ((), (), s32[]{:S(2)}) async-start(), calls=%async_computation.11 | async-start | bytes 5971968 | tf_op jit(solution)/shard_map/all_gather | solution.py:489
  72.5 166.6 %all-gather.10.cloned.1.call-start = ((), (), s32[]{:S(2)}) async-start(), calls=%async_computation.12 | async-start | bytes 4976640 | tf_op jit(solution)/shard_map/all_gather | solution.py:491
  101.2 28.5 %collective-permute-start.14 = (bf16[8,144,288]{2,1,0:T(8,128)(2,1)}, bf16[8,144,288]{2,1,0:T(8,128)(2,1)}, u32[]{:S(2)}, u32[]{:S(2)}) collective-permute-start(bf16[8,144,288]{2,1,0:T(8,128)(2,1)} %arrange.26.refs_0_), channel_id=1, source_target_pairs={{0,2},{1,3},{2,0},{3,1},{4,6},{5,7},{6,4},{7,5},{8,10},{9,11},{10,... | collective-permute-start | bytes 1990664 | tf_op jit(solution)/shard_map/ppermute | solution.py:73
  126.9 33.5 %collective-permute-start.13 = (bf16[8,144,288]{2,1,0:T(8,128)(2,1)S(1)}, bf16[8,144,288]{2,1,0:T(8,128)(2,1)S(1)}, u32[]{:S(2)}, u32[]{:S(2)}) collective-permute-start(bf16[8,144,288]{2,1,0:T(8,128)(2,1)S(1)} %copy-done.14), channel_id=1, source_target_pairs={{0,1},{1,0},{2,3},{3,2},{4,5},{5,4},{6,7},{7,6},{8,9},{9,8},{10,11... | collective-permute-start | bytes 1990664 | tf_op jit(solution)/shard_map/ppermute | solution.py:73
  129.7 30.7 %collective-permute-start.15 = (bf16[8,144,288]{2,1,0:T(8,128)(2,1)}, bf16[8,144,288]{2,1,0:T(8,128)(2,1)}, u32[]{:S(2)}, u32[]{:S(2)}) collective-permute-start(bf16[8,144,288]{2,1,0:T(8,128)(2,1)} %collective-permute-done.14.refs_2_), channel_id=1, source_target_pairs={{0,1},{1,0},{2,3},{3,2},{4,5},{5,4},{6,7},{7,6},{8,9},{9,8},{10,11... | collective-permute-start | bytes 1990664 | tf_op jit(solution)/shard_map/ppermute | solution.py:73
  267.9 31.1 %collective-permute-start.30 = (bf16[256,2048]{1,0:T(8,128)(2,1)}, bf16[256,2048]{1,0:T(8,128)(2,1)}, u32[]{:S(2)}, u32[]{:S(2)}) collective-permute-start(bf16[256,2048]{1,0:T(8,128)(2,1)} %add_convert_fusion.2), channel_id=1, source_target_pairs={{0,2},{1,3},{2,0},{3,1},{4,6},{5,7},{6,4},{7,5},{8,10},{9,11},{10,... | collective-permute-start | bytes 3145736 | tf_op jit(solution)/shard_map/ppermute | solution.py:73
  312.8 31.1 %collective-permute-start.41 = (bf16[2048,192]{0,1:T(8,128)(2,1)S(1)}, bf16[2048,192]{0,1:T(8,128)(2,1)S(1)}, u32[]{:S(2)}, u32[]{:S(2)}) collective-permute-start(bf16[2048,192]{0,1:T(8,128)(2,1)S(1)} %convolution_convert_fusion.20), channel_id=1, source_target_pairs={{0,1},{1,0},{2,3},{3,2},{4,5},{5,4},{6,7},{7,6},{8,9},{9,8},{10,11... | collective-permute-start | bytes 2359304 | tf_op jit(solution)/shard_map/ppermute | solution.py:73
  313.8 31.3 %collective-permute-start.40 = (bf16[2048,192]{0,1:T(8,128)(2,1)S(1)}, bf16[2048,192]{0,1:T(8,128)(2,1)}, u32[]{:S(2)}, u32[]{:S(2)}) collective-permute-start(bf16[2048,192]{0,1:T(8,128)(2,1)S(1)} %convolution_convert_fusion.22), channel_id=1, source_target_pairs={{0,1},{1,0},{2,3},{3,2},{4,5},{5,4},{6,7},{7,6},{8,9},{9,8},{10,11... | collective-permute-start | bytes 2359304 | tf_op jit(solution)/shard_map/ppermute | solution.py:73
  348.5 31.5 %collective-permute-start.35 = (bf16[256,1152]{1,0:T(8,128)(2,1)}, bf16[256,1152]{1,0:T(8,128)(2,1)}, u32[]{:S(2)}, u32[]{:S(2)}) collective-permute-start(bf16[256,1152]{1,0:T(8,128)(2,1)} %slice.247), channel_id=1, source_target_pairs={{0,1},{1,0},{2,3},{3,2},{4,5},{5,4},{6,7},{7,6},{8,9},{9,8},{10,11... | collective-permute-start | bytes 1769480 | tf_op jit(solution)/shard_map/ppermute | solution.py:73
  354.8 58.8 %all-to-all-start.3 = ((bf16[8,144,512]{2,1,0:T(8,128)(2,1)}), bf16[8,144,512]{2,1,0:T(8,128)(2,1)}, u32[]{:S(2)}, u32[]{:S(2)}) async-start(bf16[8,144,512]{2,1,0:T(8,128)(2,1)} %bitcast.161), calls=%async_computation.3 | async-start | bytes 2359296 | tf_op jit(solution)/shard_map/all_to_all | solution.py:259
  391.9 36.0 %collective-permute-start.49 = (bf16[4,64,2048]{2,1,0:T(8,128)(2,1)}, bf16[4,64,2048]{2,1,0:T(8,128)(2,1)}, u32[]{:S(2)}, u32[]{:S(2)}) collective-permute-start(bf16[4,64,2048]{2,1,0:T(8,128)(2,1)} %dynamic-slice_bitcast_fusion.1), channel_id=1, source_target_pairs={{0,4},{4,0},{8,12},{12,8},{16,20},{20,16},{24,28},{28,24},{1,5},{5... | collective-permute-start | bytes 3145736 | tf_op jit(solution)/shard_map/ppermute | solution.py:105
  393.7 80.7 %collective-permute-start.58 = (bf16[4,144,384]{2,1,0:T(8,128)(2,1)}, bf16[4,144,384]{2,1,0:T(8,128)(2,1)}, u32[]{:S(2)}, u32[]{:S(2)}) collective-permute-start(bf16[4,144,384]{2,1,0:T(8,128)(2,1)} %dynamic-slice_bitcast_fusion.4), channel_id=1, source_target_pairs={{0,4},{4,0},{8,12},{12,8},{16,20},{20,16},{24,28},{28,24},{1,5},{5... | collective-permute-start | bytes 1327112 | tf_op jit(solution)/shard_map/ppermute | solution.py:105
  409.4 43.2 %collective-permute-start.44 = (bf16[256,1152]{1,0:T(8,128)(2,1)}, bf16[256,1152]{1,0:T(8,128)(2,1)}, u32[]{:S(2)}, u32[]{:S(2)}) collective-permute-start(bf16[256,1152]{1,0:T(8,128)(2,1)} %slice.255), channel_id=1, source_target_pairs={{0,1},{1,0},{2,3},{3,2},{4,5},{5,4},{6,7},{7,6},{8,9},{9,8},{10,11... | collective-permute-start | bytes 1769480 | tf_op jit(solution)/shard_map/ppermute | solution.py:73
  430.7 43.7 %collective-permute-start.57 = (bf16[4,144,1152]{2,1,0:T(8,128)(2,1)}, bf16[4,144,1152]{2,1,0:T(8,128)(2,1)}, u32[]{:S(2)}, u32[]{:S(2)}) collective-permute-start(bf16[4,144,1152]{2,1,0:T(8,128)(2,1)} %dynamic-slice_bitcast_fusion), channel_id=1, source_target_pairs={{0,4},{4,0},{8,12},{12,8},{16,20},{20,16},{24,28},{28,24},{1,5},{5... | collective-permute-start | bytes 3981320 | tf_op jit(solution)/shard_map/ppermute | solution.py:105
  434.9 43.6 %all-to-all-start.4 = ((bf16[4,64,2048]{2,1,0:T(8,128)(2,1)}), bf16[4,64,2048]{2,1,0:T(8,128)(2,1)}, u32[]{:S(2)}, u32[]{:S(2)}) async-start(bf16[4,64,2048]{2,1,0:T(8,128)(2,1)} %arrange.33), calls=%async_computation.4 | async-start | bytes 2097152 | tf_op jit(solution)/shard_map/all_to_all | solution.py:236
  478.5 66.7 %all-to-all-start.5 = ((bf16[4,144,1536]{2,1,0:T(8,128)(2,1)}), bf16[4,144,1536]{2,1,0:T(8,128)(2,1)S(1)}, u32[]{:S(2)}, u32[]{:S(2)}) async-start(bf16[4,144,1536]{2,1,0:T(8,128)(2,1)} %arrange.39), calls=%async_computation.5 | async-start | bytes 3538944 | tf_op jit(solution)/shard_map/all_to_all | solution.py:236
  483.3 107.5 %reduce-scatter.2.cloned.1.call-start = ((), (), s32[]{:S(2)}) async-start(), calls=%async_computation.13 | async-start | bytes 2985984 | tf_op jit(solution)/shard_map/reduce_scatter | solution.py:684
  487.1 35.9 %collective-permute-start.53 = (bf16[1152,288]{0,1:T(8,128)(2,1)}, bf16[1152,288]{0,1:T(8,128)(2,1)S(1)}, u32[]{:S(2)}, u32[]{:S(2)}) collective-permute-start(bf16[1152,288]{0,1:T(8,128)(2,1)} %convolution_convert_fusion.16), channel_id=1, source_target_pairs={{0,1},{1,0},{2,3},{3,2},{4,5},{5,4},{6,7},{7,6},{8,9},{9,8},{10,11... | collective-permute-start | bytes 1990664 | tf_op jit(solution)/shard_map/ppermute | solution.py:73
  490.0 33.0 %collective-permute-start.55 = (bf16[1152,288]{0,1:T(8,128)(2,1)}, bf16[1152,288]{0,1:T(8,128)(2,1)}, u32[]{:S(2)}, u32[]{:S(2)}) collective-permute-start(bf16[1152,288]{0,1:T(8,128)(2,1)} %add_convert_fusion.5), channel_id=1, source_target_pairs={{0,2},{1,3},{2,0},{3,1},{4,6},{5,7},{6,4},{7,5},{8,10},{9,11},{10,... | collective-permute-start | bytes 1990664 | tf_op jit(solution)/shard_map/ppermute | solution.py:73
  571.2 36.9 %collective-permute-start.65 = (bf16[4,144,288]{2,1,0:T(8,128)(2,1)}, bf16[4,144,288]{2,1,0:T(8,128)(2,1)}, u32[]{:S(2)}, u32[]{:S(2)}) collective-permute-start(bf16[4,144,288]{2,1,0:T(8,128)(2,1)} %dynamic-slice_bitcast_fusion.3), channel_id=1, source_target_pairs={{0,4},{4,0},{8,12},{12,8},{16,20},{20,16},{24,28},{28,24},{1,5},{5... | collective-permute-start | bytes 995336 | tf_op jit(solution)/shard_map/ppermute | solution.py:105
  576.4 31.6 %collective-permute-start.64 = (bf16[4,144,864]{2,1,0:T(8,128)(2,1)}, bf16[4,144,864]{2,1,0:T(8,128)(2,1)}, u32[]{:S(2)}, u32[]{:S(2)}) collective-permute-start(bf16[4,144,864]{2,1,0:T(8,128)(2,1)} %dynamic-slice_bitcast_fusion.2), channel_id=1, source_target_pairs={{0,4},{4,0},{8,12},{12,8},{16,20},{20,16},{24,28},{28,24},{1,5},{5... | collective-permute-start | bytes 2985992 | tf_op jit(solution)/shard_map/ppermute | solution.py:105
  613.2 34.2 %collective-permute-start.68 = (bf16[144,1152]{1,0:T(8,128)(2,1)S(1)}, bf16[144,1152]{1,0:T(8,128)(2,1)S(1)}, u32[]{:S(2)}, u32[]{:S(2)}) collective-permute-start(bf16[144,1152]{1,0:T(8,128)(2,1)S(1)} %get-tuple-element.351), channel_id=1, source_target_pairs={{0,24},{4,28},{8,16},{12,20},{16,8},{20,12},{24,0},{28,4},{1,25},{... | collective-permute-start | bytes 995336 | tf_op jit(solution)/shard_map/ppermute | solution.py:110
  617.1 30.3 %collective-permute-start.67 = (bf16[144,1152]{1,0:T(8,128)(2,1)S(1)}, bf16[144,1152]{1,0:T(8,128)(2,1)S(1)}, u32[]{:S(2)}, u32[]{:S(2)}) collective-permute-start(bf16[144,1152]{1,0:T(8,128)(2,1)S(1)} %get-tuple-element.352), channel_id=1, source_target_pairs={{0,16},{4,20},{8,24},{12,28},{16,0},{20,4},{24,8},{28,12},{1,17},{... | collective-permute-start | bytes 995336 | tf_op jit(solution)/shard_map/ppermute | solution.py:110
  (168 other events, 1823.7 us)
Sparse Core Ops, SparseCore 0:
  10.2 55.6 all-gather.5
  72.6 87.7 all-gather.7
  162.6 74.4 all-gather.9
  487.5 96.3 reduce-scatter.1
